TPU v7x, 32 devices: a whole 2x2x4 slice. The times are simulated.
32 devices in a mesh: grp: 4 (over z), dev: 8 (over y, x, core).
Axes of the slice: x: 2, y: 2, z: 4, core: 2. Of those that a mesh axis runs over, the one named last changes fastest.
Arguments:
- layer_inputs: bfloat16 [4, 4096, 4096], P(None, 'grp', 'dev')
- output_grads: bfloat16 [4, 4096, 2048], P(None, ('grp', 'dev'))
- layer_owner: int32 [4], replicated, may hold values from 0 to 3, each once
- master_weights: float32 [4, 4096, 2048], P('grp', 'dev')
- momentum: float32 [4, 4096, 2048], P('grp', 'dev'), may hold values from -6 to 6
- table_blocks: float32 [4, 64, 128, 128], P('grp', 'dev'), may hold values from -6 to 6
- block_grads: bfloat16 [4, 8, 16, 128, 128], P('grp', 'dev'), may hold values from -6 to 6
- block_ids: int32 [4, 8, 16], P('grp', 'dev'), may hold values from 0 to 7
- block_counts: int32 [4, 8, 8], P('grp', 'dev'), may hold values from 0 to 2, as said below
Outputs:
- new_master: float32 [4, 4096, 2048], P('grp', 'dev')
- new_momentum: float32 [4, 4096, 2048], P('grp', 'dev')
- new_weights: bfloat16 [4, 4096, 2048], P(None, 'dev')
- new_table: float32 [4, 64, 128, 128], P('grp', 'dev')
Inputs may be any that keep to these rules, and one draw needn't show every extreme that they name: `layer_owner`: each group owns exactly one layer. `block_ids`: several live slots may name the same block; their gradients add. `block_counts`: in every group some owners receive 2 live slots from every device; slots at or past the count hold stale data.
All inputs are finite; a program needn't handle non-finite values.
Results may differ from a plain program's by a relative error of at most 0.001.
Values may be sent and summed in bfloat16 or wider, within the bound.
No kernel may reach another device: no remote copies, remote signals or barrier semaphores. Data moves between devices by JAX's collectives and lax.ppermute only.
A program may use at most 128 MiB of HBM per device.

v0:
```python
import jax
import jax.numpy as jnp
from jax import lax
from jax.experimental import pallas as pl
from jax.experimental.pallas import tpu as pltpu
from jax.sharding import PartitionSpec as P


tower_rate = 0.5
momentum_keep = 0.9
tower_decay = 0.1
table_rate = 0.5
table_decay = 0.2
eps_norm = 1e-06
weight_chunks = 2
lanes = 128
mib = 1 << 20


anywhere = pl.BlockSpec(memory_space=pl.ANY)


def accumulate(acc, inputs, near, far, last):
    devices = lax.axis_size("dev")
    half = devices // 2
    count = len(inputs)
    rows, tokens = inputs[0].shape
    per_dev = tokens // devices
    columns = near.shape[1]
    tile = min(columns, 512)
    tiles = columns // tile

    def kernel(*refs):
        refs = list(refs)
        acc_ref = refs.pop(0) if acc is not None else None
        x_refs = [refs.pop(0) for _ in range(count)]
        near_ref, far_ref, out_ref = refs.pop(0), refs.pop(0), refs.pop(0)
        square_ref = refs.pop(0) if last else None
        x_all, g_all, x_sem, g_sem = refs
        column = pl.program_id(0)
        device = lax.axis_index("dev")

        @pl.when(column == 0)
        def _():
            for i in range(count):
                pltpu.make_async_copy(x_refs[i], x_all.at[i], x_sem).start()
            for t in range(tiles):
                for side, ref in enumerate((near_ref, far_ref)):
                    for place in range(half):
                        owner = device ^ (2 * place + side)
                        for i in range(count):
                            pltpu.make_async_copy(
                                ref.at[
                                    pl.ds((place * count + i) * per_dev, per_dev),
                                    pl.ds(t * tile, tile),
                                ],
                                g_all.at[t, i, pl.ds(pl.multiple_of(owner * per_dev, per_dev), per_dev)],
                                g_sem.at[t],
                            ).start()
            pltpu.make_async_copy(x_all, x_all, x_sem).wait()

        pltpu.make_async_copy(g_all.at[column], g_all.at[column], g_sem.at[column]).wait()
        total = acc_ref[...] if acc is not None else None
        for i in range(count):
            part = jnp.dot(x_all[i], g_all[column, i], preferred_element_type=jnp.float32)
            total = part if total is None else total + part
        out_ref[...] = total
        if last:
            squares = jnp.sum(total * total, axis=0, keepdims=True)
            folded = sum(squares[:, k * lanes : (k + 1) * lanes] for k in range(tile // lanes))

            @pl.when(column == 0)
            def _():
                square_ref[...] = folded

            @pl.when(column > 0)
            def _():
                square_ref[...] += folded

    block = pl.BlockSpec((rows, tile), lambda j: (0, j))
    operands = ([acc] if acc is not None else []) + list(inputs) + [near, far]
    out_shape = [jax.ShapeDtypeStruct((rows, columns), jnp.float32)]
    out_specs = [block]
    if last:
        out_shape.append(jax.ShapeDtypeStruct((1, lanes), jnp.float32))
        out_specs.append(pl.BlockSpec((1, lanes), lambda j: (0, 0)))
    result = pl.pallas_call(
        kernel,
        grid=(tiles,),
        in_specs=([block] if acc is not None else []) + [anywhere] * (count + 2),
        out_specs=out_specs,
        out_shape=out_shape,
        scratch_shapes=[
            pltpu.VMEM((count, rows, tokens), jnp.bfloat16),
            pltpu.VMEM((tiles, count, tokens, tile), jnp.bfloat16),
            pltpu.SemaphoreType.DMA,
            pltpu.SemaphoreType.DMA((tiles,)),
        ],
        compiler_params=pltpu.CompilerParams(
            vmem_limit_bytes=2 * count * tokens * (rows + columns) + 16 * rows * tile + 2 * mib
        ),
        cost_estimate=pl.CostEstimate(
            flops=2 * count * rows * tokens * columns,
            bytes_accessed=2 * count * tokens * (rows + columns) + 8 * rows * columns,
            transcendentals=0,
        ),
        name="accumulate",
    )(*operands)
    return result if last else result[0]


def update(slot_layer, weight_squares, grad_squares, grad, master, moment, chunk, buffers):
    groups = lax.axis_size("grp")
    rows, columns = grad.shape
    height = rows // weight_chunks
    step = min(height, 32)
    steps = height // step
    count = len(weight_squares)

    def kernel(slot_ref, *refs):
        refs = list(refs)
        weight_refs = [refs.pop(0) for _ in range(count)]
        grad_refs = [refs.pop(0) for _ in range(count)]
        grad_ref, master_ref, moment_ref = refs[:3]
        piece_ref, weights_out, master_out, moment_out = refs[-4:]

        def norm(parts):
            total = sum(ref[...] for ref in parts)
            return jnp.sqrt(jnp.sum(total, axis=1, keepdims=True) + eps_norm)

        weight_norm = norm(weight_refs)
        trust = weight_norm / (norm(grad_refs) + tower_decay * weight_norm)
        value = master_ref[...]
        new_moment = momentum_keep * moment_ref[...] + tower_rate * trust * (
            grad_ref[...] + tower_decay * value
        )
        new_master = value - new_moment
        moment_out[...] = new_moment
        master_out[...] = new_master
        piece = new_master.astype(jnp.bfloat16)
        piece_ref[...] = piece
        weights_out[0] = piece

    vector = pl.BlockSpec((1, lanes), lambda i, slot: (0, 0))
    block = pl.BlockSpec((step, columns), lambda i, slot: (chunk * steps + i, 0))
    operands = [slot_layer, *weight_squares, *grad_squares, grad, master, moment]
    first = len(operands)
    return pl.pallas_call(
        kernel,
        grid_spec=pltpu.PrefetchScalarGridSpec(
            num_scalar_prefetch=1,
            grid=(steps,),
            in_specs=[vector] * (2 * count) + [block] * 3 + [anywhere] * len(buffers),
            out_specs=[
                pl.BlockSpec((step, columns), lambda i, slot: (i, 0)),
                pl.BlockSpec(
                    (1, step, columns),
                    lambda i, slot: (slot[lax.axis_index("grp")], chunk * steps + i, 0),
                ),
                block,
                block,
            ],
        ),
        out_shape=[
            jax.ShapeDtypeStruct((height, columns), jnp.bfloat16),
            jax.ShapeDtypeStruct((groups, rows, columns), jnp.bfloat16),
            jax.ShapeDtypeStruct((rows, columns), jnp.float32),
            jax.ShapeDtypeStruct((rows, columns), jnp.float32),
        ],
        input_output_aliases={first + i: 1 + i for i in range(len(buffers))},
        compiler_params=pltpu.CompilerParams(vmem_limit_bytes=48 * step * columns + 2 * mib),
        cost_estimate=pl.CostEstimate(
            flops=8 * height * columns, bytes_accessed=24 * height * columns, transcendentals=0
        ),
        name="update",
    )(*operands, *buffers)


def place(slot_layer, weights, above, below, step, chunk):
    groups = lax.axis_size("grp")
    height, columns = above.shape

    def kernel(slot_ref, weights_ref, above_ref, below_ref, out_ref, held, in_sem, out_sem):
        group = lax.axis_index("grp")
        sides = (
            (above_ref, group - step, group >= step),
            (below_ref, group + step, group + step < groups),
        )
        for side, (ref, source, valid) in enumerate(sides):

            @pl.when(valid)
            def _():
                pltpu.make_async_copy(ref, held.at[side], in_sem.at[side]).start()

        for side, (ref, source, valid) in enumerate(sides):

            @pl.when(valid)
            def _():
                pltpu.make_async_copy(ref, held.at[side], in_sem.at[side]).wait()
                layer = slot_ref[source]
                copy = pltpu.make_async_copy(
                    held.at[side], out_ref.at[layer, pl.ds(chunk * height, height)], out_sem.at[side]
                )
                copy.start()

        for side, (ref, source, valid) in enumerate(sides):

            @pl.when(valid)
            def _():
                pltpu.make_async_copy(
                    held.at[side], out_ref.at[0, pl.ds(chunk * height, height)], out_sem.at[side]
                ).wait()

    return pl.pallas_call(
        kernel,
        grid_spec=pltpu.PrefetchScalarGridSpec(
            num_scalar_prefetch=1,
            grid=(1,),
            in_specs=[anywhere] * 3,
            out_specs=anywhere,
            scratch_shapes=[
                pltpu.VMEM((2, height, columns), jnp.bfloat16),
                pltpu.SemaphoreType.DMA((2,)),
                pltpu.SemaphoreType.DMA((2,)),
            ],
        ),
        out_shape=jax.ShapeDtypeStruct(weights.shape, weights.dtype),
        input_output_aliases={1: 0},
        compiler_params=pltpu.CompilerParams(vmem_limit_bytes=4 * height * columns + 2 * mib),
        cost_estimate=pl.CostEstimate(
            flops=0, bytes_accessed=8 * height * columns, transcendentals=0
        ),
        name="place",
    )(slot_layer, weights, above, below)


def rounds_of(groups):
    rounds = [[0]]
    for step in range(1, groups // 2 + 1):
        rounds.append([step] if 2 * step == groups else [step, groups - step])
    return rounds


def local(
    layer_inputs,
    output_grads,
    layer_owner,
    master_weights,
    momentum,
    table_blocks,
    block_grads,
    block_ids,
    block_counts,
):
    groups = lax.axis_size("grp")
    devices = lax.axis_size("dev")
    group = lax.axis_index("grp")
    masks = range(2, devices, 2)

    def swap(value, mask):
        return lax.ppermute(value, "dev", [(i, i ^ mask) for i in range(devices)])

    def shift(value, step):
        if step == 0:
            return value
        return lax.ppermute(value, "grp", [(i, (i + step) % groups) for i in range(groups)])

    def dev_parts(value):
        pair = value + swap(value, 1)
        return [pair] + [swap(pair, mask) for mask in masks]

    layers = jnp.arange(groups, dtype=jnp.int32)
    slot_layer = jnp.sum(
        jnp.where(layer_owner[None, :] == layers[:, None], layers[None, :], 0), axis=1
    )
    master = master_weights[0]
    moment = momentum[0]
    _, columns = master.shape

    rounds = rounds_of(groups)
    steps = [step for some in rounds for step in some]

    def owned(value, step):
        return lax.dynamic_index_in_dim(
            value, slot_layer[(group + step) % groups], 0, keepdims=False
        )

    g_own = {step: shift(owned(output_grads, step), step) for step in steps}
    x_own = {step: shift(owned(layer_inputs, step).T, step) for step in steps}

    squares = jnp.sum(master * master, axis=0, keepdims=True)
    squares = jnp.sum(squares.reshape(columns // lanes, lanes), axis=0, keepdims=True)
    weight_squares = dev_parts(squares)

    new_table = update_table(table_blocks[0], block_grads, block_ids, block_counts, g_own[steps[1]])

    grad = None
    for some in rounds:
        pieces = [g_own[step] for step in some]
        piece = jnp.concatenate(pieces, axis=0) if len(some) > 1 else pieces[0]
        near = jnp.concatenate([piece] + [swap(piece, mask) for mask in masks], axis=0)
        far = swap(near, 1)
        inputs = [x_own[step] for step in some]
        last = some is rounds[-1]
        if last:
            inputs[0], new_table = lax.optimization_barrier((inputs[0], new_table))
        grad = accumulate(grad, inputs, near, far, last)
    grad, squares = grad
    grad_squares = dev_parts(squares)

    up = [(i, i + 1) for i in range(groups - 1)]
    down = [(i + 1, i) for i in range(groups - 1)]
    buffers, above, below = [], [], []
    for chunk in range(weight_chunks):
        piece, *buffers = update(
            slot_layer, weight_squares, grad_squares, grad, master, moment, chunk, buffers
        )
        above.append(piece)
        below.append(piece)
    new_weights, new_master, new_moment = buffers
    for step in range(1, groups):
        for chunk in range(weight_chunks):
            above[chunk] = lax.ppermute(above[chunk], "grp", up)
            below[chunk] = lax.ppermute(below[chunk], "grp", down)
            new_weights = place(slot_layer, new_weights, above[chunk], below[chunk], step, chunk)
    return (new_master[None], new_moment[None], new_weights, new_table[None])


def update_table(table, block_grads, block_ids, block_counts, behind):
    devices = lax.axis_size("dev")
    grads, ids, _ = lax.optimization_barrier((block_grads[0, 0], block_ids[0, 0], behind))
    counts = block_counts[0, 0]
    capacity = ids.shape[0] // devices
    slot_rank = jnp.arange(devices * capacity, dtype=jnp.int32) % capacity
    live = slot_rank < jnp.repeat(counts, capacity)
    tagged = jnp.where(live, ids, -1)
    got_grads, got_ids = (
        lax.all_to_all(grads, "dev", split_axis=0, concat_axis=0, tiled=True),
        lax.all_to_all(tagged, "dev", split_axis=0, concat_axis=0, tiled=True),
    )
    nblocks = table.shape[0]
    width = table.shape[1] * table.shape[2]
    matches = got_ids[None, :] == jnp.arange(nblocks, dtype=jnp.int32)[:, None]
    block_sum = jnp.dot(
        matches.astype(jnp.bfloat16),
        got_grads.reshape(got_ids.shape[0], width),
        preferred_element_type=jnp.float32,
    )
    hits = jnp.sum(matches.astype(jnp.int32), axis=1)
    flat = table.reshape(nblocks, width)
    w_norm = jnp.sqrt(jnp.sum(flat * flat, axis=1) + eps_norm)
    g_norm = jnp.sqrt(jnp.sum(block_sum * block_sum, axis=1) + eps_norm)
    block_trust = w_norm / (g_norm + table_decay * w_norm)
    moved = flat - table_rate * block_trust[:, None] * (block_sum + table_decay * flat)
    return jnp.where((hits > 0)[:, None], moved, flat).reshape(table.shape)


def solution(mesh):
    return jax.shard_map(
        local,
        mesh=mesh,
        in_specs=(
            P(None, "grp", "dev"),
            P(None, ("grp", "dev"), None),
            P(),
            P("grp", "dev", None),
            P("grp", "dev", None),
            P("grp", "dev", None, None),
            P("grp", "dev", None, None, None),
            P("grp", "dev", None),
            P("grp", "dev", None),
        ),
        out_specs=(
            P("grp", "dev", None),
            P("grp", "dev", None),
            P(None, "dev", None),
            P("grp", "dev", None, None),
        ),
        check_vma=False,
    )
```

profile of v0, /device:TPU:0, one launch (start us, length us, event | category | flops | bytes accessed | tf_op | source)
XLA Modules:
  0.0 396.8 jit_solution(6955590005750420230)
XLA Ops:
  9.8 2.5 dynamic-slice_bitcast_fusion
  12.4 3.1 collective-permute-start.10
  15.4 2.0 collective-permute-start.11
  17.4 12.8 %collective-permute-done.10 = bf16[128,2048]{1,0:T(8,128)(2,1)S(1)} collective-permute-done((bf16[128,2048]{1,0:T(8,128)(2,1)S(1)}, bf16[128,2048]{1,0:T(8,128)(2,1)S(1)}, u32[]{:S(2)}, u32[]{:S(2)}) %collective-permute-start.10) | collective-permute-done | bytes 524320 | tf_op jit(solution)/shard_map/ppermute | solution.py:266
  31.2 8.9 %collective-permute-done.11 = bf16[128,2048]{1,0:T(8,128)(2,1)S(1)} collective-permute-done((bf16[128,2048]{1,0:T(8,128)(2,1)S(1)}, bf16[128,2048]{1,0:T(8,128)(2,1)S(1)}, u32[]{:S(2)}, u32[]{:S(2)}) %collective-permute-start.11) | collective-permute-done | bytes 524320 | tf_op jit(solution)/shard_map/ppermute | solution.py:266
  40.9 1.5 collective-permute-start.12
  42.4 1.5 collective-permute-start.13
  44.4 22.5 %collective-permute-done.12 = bf16[256,2048]{1,0:T(8,128)(2,1)S(1)} collective-permute-done((bf16[256,2048]{1,0:T(8,128)(2,1)S(1)}, bf16[256,2048]{1,0:T(8,128)(2,1)S(1)}, u32[]{:S(2)}, u32[]{:S(2)}) %collective-permute-start.12) | collective-permute-done | bytes 1048608 | tf_op jit(solution)/shard_map/ppermute | solution.py:261
  68.0 21.1 %collective-permute-done.13 = bf16[256,2048]{1,0:T(8,128)(2,1)S(1)} collective-permute-done((bf16[256,2048]{1,0:T(8,128)(2,1)S(1)}, bf16[256,2048]{1,0:T(8,128)(2,1)S(1)}, u32[]{:S(2)}, u32[]{:S(2)}) %collective-permute-start.13) | collective-permute-done | bytes 1048608 | tf_op jit(solution)/shard_map/ppermute | solution.py:261
  92.0 1.5 collective-permute-start.6
  93.6 1.8 collective-permute-start.4
  95.9 21.9 %collective-permute-done.17 = bf16[128,2048]{1,0:T(8,128)(2,1)} collective-permute-done((bf16[128,2048]{1,0:T(8,128)(2,1)S(1)}, bf16[128,2048]{1,0:T(8,128)(2,1)}, u32[]{:S(2)}, u32[]{:S(2)}) %collective-permute-start.17) | collective-permute-done | bytes 524320 | tf_op jit(solution)/shard_map/ppermute | solution.py:266
  118.0 1.4 constant_dynamic-slice_fusion
  119.5 1.3 copy.41
  120.8 1.3 copy.39
  122.2 1.3 copy.40
  123.5 1.7 collective-permute-start.9
  125.1 2.8 collective-permute-start.20
  128.4 1.7 pad_maximum_fusion.refs_1_
  130.1 1.9 constant_dynamic-update-slice_fusion.10
  132.9 1.9 constant_dynamic-update-slice_fusion.9
  134.8 17.6 %collective-permute-done.19 = bf16[128,2048]{1,0:T(8,128)(2,1)S(1)} collective-permute-done((bf16[128,2048]{1,0:T(8,128)(2,1)}, bf16[128,2048]{1,0:T(8,128)(2,1)S(1)}, u32[]{:S(2)}, u32[]{:S(2)}) %collective-permute-start.19) | collective-permute-done | bytes 524320 | tf_op jit(solution)/shard_map/ppermute | solution.py:261
  154.8 3.3 all-to-all-start
  158.1 1.5 copy.38
  159.6 3.0 all-to-all-done
  162.6 4.2 %all-to-all-start.1 = ((bf16[16,128,128]{2,1,0:T(8,128)(2,1)}), bf16[16,128,128]{2,1,0:T(8,128)(2,1)}, u32[]{:S(2)}, u32[]{:S(2)}) async-start(bf16[16,128,128]{2,1,0:T(8,128)(2,1)} %bitcast.68), calls=%async_computation.1 | async-start | bytes 1048576 | tf_op jit(solution)/shard_map/all_to_all | solution.py:338
  169.4 29.9 %collective-permute-done.16.refs_1_ = bf16[512,1024]{1,0:T(8,128)(2,1)} collective-permute-done((bf16[512,1024]{1,0:T(8,128)(2,1)}, bf16[512,1024]{1,0:T(8,128)(2,1)}, u32[]{:S(2)}, u32[]{:S(2)}) %collective-permute-start.16) | collective-permute-done | bytes 1048608 | tf_op jit(solution)/shard_map/ppermute | solution.py:266
  199.3 1.6 multiply_reduce_fusion.1
  200.8 1.4 fusion
  202.3 4.4 %accumulate.3.refs_0_ = f32[512,2048]{1,0:T(8,128)S(1)} custom-call(bf16[512,1024]{1,0:T(8,128)(2,1)S(1)} %bitcast.64, bf16[512,2048]{1,0:T(8,128)(2,1)S(1)} %pad_maximum_fusion.refs_1_, bf16[512,2048]{1,0:T(8,128)(2,1)} %collective-permute-done.7.refs_2_), custom_call_target="tpu_custom_call" | custom-call | flops 2147483648 | bytes 13631488 | tf_op jit(solution)/shard_map/accumulate/pallas_call | solution.py:87
  206.8 19.6 %collective-permute-done.8.refs_1_ = bf16[512,1024]{1,0:T(8,128)(2,1)} collective-permute-done((bf16[512,1024]{1,0:T(8,128)(2,1)}, bf16[512,1024]{1,0:T(8,128)(2,1)}, u32[]{:S(2)}, u32[]{:S(2)}) %collective-permute-start.8) | collective-permute-done | bytes 1048608 | tf_op jit(solution)/shard_map/ppermute | solution.py:266
  226.4 9.9 %accumulate.4.refs_0_ = f32[512,2048]{1,0:T(8,128)S(1)} custom-call(f32[512,2048]{1,0:T(8,128)S(1)} %accumulate.3.refs_0_, bf16[512,1024]{1,0:T(8,128)(2,1)} %collective-permute-done.8.refs_1_, bf16[512,1024]{1,0:T(8,128)(2,1)} %collective-permute-done.9.refs_2_, bf16[1024,2048]{1,0:T(8,128)(2,1)} %constant_dynamic-update-slice_fusion.2.refs_3_, ...), custom_call_target="tpu_custom_call" | custom-call | flops 4294967296 | bytes 18874368 | tf_op jit(solution)/shard_map/accumulate/pallas_call | solution.py:87
  236.4 6.4 %accumulate.5 = (f32[512,2048]{1,0:T(8,128)S(1)}, f32[1,128]{1,0:T(1,128)S(1)}) custom-call(f32[512,2048]{1,0:T(8,128)S(1)} %accumulate.4.refs_0_, bf16[512,1024]{1,0:T(8,128)(2,1)} %collective-permute-done.16.refs_1_, bf16[512,2048]{1,0:T(8,128)(2,1)} %constant_dynamic-update-slice_fusion.7.refs_2_, bf16[512,2048]{1,0:T(8,128)(2,1)} %collective-permute-done.21.refs_3_), custom_call_target="tpu_custom_call" | custom-call | flops 2147483648 | bytes 13631488 | tf_op jit(solution)/shard_map/accumulate/pallas_call | solution.py:87
  243.0 2.0 collective-permute-start.2
  245.0 1.5 collective-permute-start.1
  246.5 1.9 collective-permute-start.24
  248.5 1.5 collective-permute-start.23
  252.0 4.8 %update.2 = (bf16[256,2048]{1,0:T(8,128)(2,1)S(1)}, bf16[4,512,2048]{2,1,0:T(8,128)(2,1)}, f32[512,2048]{1,0:T(8,128)}, f32[512,2048]{1,0:T(8,128)}) custom-call(s32[4]{0:T(128)S(1)} %select_reduce_fusion.slot_ref, f32[1,128]{1,0:T(1,128)S(1)} %bitcast_add_fusion.refs_0_, f32[1,128]{1,0:T(1,128)S(1)} %collective-permute-done.1.refs_1_, ...), custom_call_target="tpu_custom_call" | custom-call | flops 4194304 | bytes 12582912 | tf_op jit(solution)/shard_map/update/pallas_call | solution.py:148
  256.8 1.3 collective-permute-start.27
  258.1 4.6 %collective-permute-start.26 = (bf16[256,2048]{1,0:T(8,128)(2,1)S(1)}, bf16[256,2048]{1,0:T(8,128)(2,1)S(1)}, u32[]{:S(2)}, u32[]{:S(2)}) collective-permute-start(bf16[256,2048]{1,0:T(8,128)(2,1)S(1)} %get-tuple-element.29), channel_id=1, source_target_pairs={{0,8},{8,16},{16,24},{1,9},{9,17},{17,25},{2,10},{10,18},{18,26},{... | collective-permute-start | bytes 3145736 | tf_op jit(solution)/shard_map/ppermute | solution.py:323
  262.7 4.8 %update.3 = (bf16[256,2048]{1,0:T(8,128)(2,1)S(1)}, bf16[4,512,2048]{2,1,0:T(8,128)(2,1)}, f32[512,2048]{1,0:T(8,128)}, f32[512,2048]{1,0:T(8,128)}) custom-call(s32[4]{0:T(128)S(1)} %select_reduce_fusion.slot_ref, f32[1,128]{1,0:T(1,128)S(1)} %bitcast_add_fusion.refs_0_, ...), custom_call_target="tpu_custom_call", output_to_operand_aliasing={{1}: (12, {}), {2}: (13, {}), {3}: (14, {})} | custom-call | flops 4194304 | bytes 12582912 | tf_op jit(solution)/shard_map/update/pallas_call | solution.py:148
  267.5 1.3 collective-permute-start.29
  268.8 4.6 %collective-permute-start.28 = (bf16[256,2048]{1,0:T(8,128)(2,1)S(1)}, bf16[256,2048]{1,0:T(8,128)(2,1)S(1)}, u32[]{:S(2)}, u32[]{:S(2)}) collective-permute-start(bf16[256,2048]{1,0:T(8,128)(2,1)S(1)} %get-tuple-element.30), channel_id=1, source_target_pairs={{0,8},{8,16},{16,24},{1,9},{9,17},{17,25},{2,10},{10,18},{18,26},{... | collective-permute-start | bytes 3145736 | tf_op jit(solution)/shard_map/ppermute | solution.py:323
  273.4 11.3 %collective-permute-done.27.below_ref = bf16[256,2048]{1,0:T(8,128)(2,1)S(1)} collective-permute-done((bf16[256,2048]{1,0:T(8,128)(2,1)S(1)}, bf16[256,2048]{1,0:T(8,128)(2,1)S(1)}, u32[]{:S(2)}, u32[]{:S(2)}) %collective-permute-start.27) | collective-permute-done | bytes 1048608 | tf_op jit(solution)/shard_map/ppermute | solution.py:324
  284.7 1.3 collective-permute-start.31
  286.2 4.5 %collective-permute-start.30 = (bf16[256,2048]{1,0:T(8,128)(2,1)S(1)}, bf16[256,2048]{1,0:T(8,128)(2,1)S(1)}, u32[]{:S(2)}, u32[]{:S(2)}) collective-permute-start(bf16[256,2048]{1,0:T(8,128)(2,1)S(1)} %collective-permute-done.26.above_ref), channel_id=1, source_target_pairs={{0,8},{8,16},{16,24},{1,9},{9,17},{17,25},{2,10},{10,18},{18,26},{... | collective-permute-start | bytes 3145736 | tf_op jit(solution)/shard_map/ppermute | solution.py:323
  290.7 16.6 %collective-permute-done.29.below_ref = bf16[256,2048]{1,0:T(8,128)(2,1)S(1)} collective-permute-done((bf16[256,2048]{1,0:T(8,128)(2,1)S(1)}, bf16[256,2048]{1,0:T(8,128)(2,1)S(1)}, u32[]{:S(2)}, u32[]{:S(2)}) %collective-permute-start.29) | collective-permute-done | bytes 1048608 | tf_op jit(solution)/shard_map/ppermute | solution.py:324
  307.2 1.3 collective-permute-start.33
  308.7 4.5 %collective-permute-start.32 = (bf16[256,2048]{1,0:T(8,128)(2,1)S(1)}, bf16[256,2048]{1,0:T(8,128)(2,1)S(1)}, u32[]{:S(2)}, u32[]{:S(2)}) collective-permute-start(bf16[256,2048]{1,0:T(8,128)(2,1)S(1)} %collective-permute-done.28.above_ref), channel_id=1, source_target_pairs={{0,8},{8,16},{16,24},{1,9},{9,17},{17,25},{2,10},{10,18},{18,26},{... | collective-permute-start | bytes 3145736 | tf_op jit(solution)/shard_map/ppermute | solution.py:323
  313.1 16.6 %collective-permute-done.31.below_ref = bf16[256,2048]{1,0:T(8,128)(2,1)S(1)} collective-permute-done((bf16[256,2048]{1,0:T(8,128)(2,1)S(1)}, bf16[256,2048]{1,0:T(8,128)(2,1)S(1)}, u32[]{:S(2)}, u32[]{:S(2)}) %collective-permute-start.31) | collective-permute-done | bytes 1048608 | tf_op jit(solution)/shard_map/ppermute | solution.py:324
  329.7 1.3 collective-permute-start.35
  331.1 4.5 %collective-permute-start.34 = (bf16[256,2048]{1,0:T(8,128)(2,1)S(1)}, bf16[256,2048]{1,0:T(8,128)(2,1)S(1)}, u32[]{:S(2)}, u32[]{:S(2)}) collective-permute-start(bf16[256,2048]{1,0:T(8,128)(2,1)S(1)} %collective-permute-done.30.above_ref), channel_id=1, source_target_pairs={{0,8},{8,16},{16,24},{1,9},{9,17},{17,25},{2,10},{10,18},{18,26},{... | collective-permute-start | bytes 3145736 | tf_op jit(solution)/shard_map/ppermute | solution.py:323
  335.6 16.6 %collective-permute-done.33.below_ref = bf16[256,2048]{1,0:T(8,128)(2,1)S(1)} collective-permute-done((bf16[256,2048]{1,0:T(8,128)(2,1)S(1)}, bf16[256,2048]{1,0:T(8,128)(2,1)S(1)}, u32[]{:S(2)}, u32[]{:S(2)}) %collective-permute-start.33) | collective-permute-done | bytes 1048608 | tf_op jit(solution)/shard_map/ppermute | solution.py:324
  352.1 1.3 collective-permute-start.37
  353.6 4.5 %collective-permute-start.36 = (bf16[256,2048]{1,0:T(8,128)(2,1)S(1)}, bf16[256,2048]{1,0:T(8,128)(2,1)S(1)}, u32[]{:S(2)}, u32[]{:S(2)}) collective-permute-start(bf16[256,2048]{1,0:T(8,128)(2,1)S(1)} %collective-permute-done.32.above_ref), channel_id=1, source_target_pairs={{0,8},{8,16},{16,24},{1,9},{9,17},{17,25},{2,10},{10,18},{18,26},{... | collective-permute-start | bytes 3145736 | tf_op jit(solution)/shard_map/ppermute | solution.py:323
  359.0 1.6 place.6.weights_ref
  360.6 1.7 place.7.weights_ref
  362.3 1.6 place.8.weights_ref
  363.9 1.7 place.9.weights_ref
  365.6 9.0 %collective-permute-done.35.below_ref = bf16[256,2048]{1,0:T(8,128)(2,1)S(1)} collective-permute-done((bf16[256,2048]{1,0:T(8,128)(2,1)S(1)}, bf16[256,2048]{1,0:T(8,128)(2,1)S(1)}, u32[]{:S(2)}, u32[]{:S(2)}) %collective-permute-start.35) | collective-permute-done | bytes 1048608 | tf_op jit(solution)/shard_map/ppermute | solution.py:324
  374.6 1.5 collective-permute-done.34.above_ref
  376.1 1.6 place.10.weights_ref
  377.7 16.3 %collective-permute-done.37.below_ref = bf16[256,2048]{1,0:T(8,128)(2,1)S(1)} collective-permute-done((bf16[256,2048]{1,0:T(8,128)(2,1)S(1)}, bf16[256,2048]{1,0:T(8,128)(2,1)S(1)}, u32[]{:S(2)}, u32[]{:S(2)}) %collective-permute-start.37) | collective-permute-done | bytes 1048608 | tf_op jit(solution)/shard_map/ppermute | solution.py:324
  395.2 1.6 place.11
  (75 shorter events, 20.1 us)
Async XLA Ops:
  12.4 17.9 %collective-permute-start.10 = (bf16[128,2048]{1,0:T(8,128)(2,1)S(1)}, bf16[128,2048]{1,0:T(8,128)(2,1)S(1)}, u32[]{:S(2)}, u32[]{:S(2)}) collective-permute-start(bf16[128,2048]{1,0:T(8,128)(2,1)S(1)} %get-tuple-element.37), channel_id=1, source_target_pairs={{0,8},{8,16},{16,24},{24,0},{1,9},{9,17},{17,25},{25,1},{2,10},{10... | collective-permute-start | bytes 1572872 | tf_op jit(solution)/shard_map/ppermute | solution.py:266
  15.4 24.6 %collective-permute-start.11 = (bf16[128,2048]{1,0:T(8,128)(2,1)S(1)}, bf16[128,2048]{1,0:T(8,128)(2,1)S(1)}, u32[]{:S(2)}, u32[]{:S(2)}) collective-permute-start(bf16[128,2048]{1,0:T(8,128)(2,1)S(1)} %get-tuple-element.39), channel_id=1, source_target_pairs={{0,24},{8,0},{16,8},{24,16},{1,25},{9,1},{17,9},{25,17},{2,26},{10... | collective-permute-start | bytes 1572872 | tf_op jit(solution)/shard_map/ppermute | solution.py:266
  31.2 64.3 %copy-start = (f32[1,512,2048]{2,1,0:T(8,128)S(1)}, f32[1,512,2048]{2,1,0:T(8,128)}, u32[]{:S(2)}) copy-start(f32[1,512,2048]{2,1,0:T(8,128)} %param.12) | copy-start | bytes 12582916
  40.9 26.0 %collective-permute-start.12 = (bf16[256,2048]{1,0:T(8,128)(2,1)S(1)}, bf16[256,2048]{1,0:T(8,128)(2,1)S(1)}, u32[]{:S(2)}, u32[]{:S(2)}) collective-permute-start(bf16[256,2048]{1,0:T(8,128)(2,1)S(1)} %get-tuple-element.40), channel_id=1, source_target_pairs={{0,2},{1,3},{2,0},{3,1},{4,6},{5,7},{6,4},{7,5},{8,10},{9,11},{10,... | collective-permute-start | bytes 3145736 | tf_op jit(solution)/shard_map/ppermute | solution.py:261
  42.4 46.7 %collective-permute-start.13 = (bf16[256,2048]{1,0:T(8,128)(2,1)S(1)}, bf16[256,2048]{1,0:T(8,128)(2,1)S(1)}, u32[]{:S(2)}, u32[]{:S(2)}) collective-permute-start(bf16[256,2048]{1,0:T(8,128)(2,1)S(1)} %get-tuple-element.40), channel_id=1, source_target_pairs={{0,4},{1,5},{2,6},{3,7},{4,0},{5,1},{6,2},{7,3},{8,12},{9,13},{10,... | collective-permute-start | bytes 3145736 | tf_op jit(solution)/shard_map/ppermute | solution.py:261
  44.0 46.2 %collective-permute-start.14 = (bf16[256,2048]{1,0:T(8,128)(2,1)S(1)}, bf16[256,2048]{1,0:T(8,128)(2,1)S(1)}, u32[]{:S(2)}, u32[]{:S(2)}) collective-permute-start(bf16[256,2048]{1,0:T(8,128)(2,1)S(1)} %get-tuple-element.40), channel_id=1, source_target_pairs={{0,6},{1,7},{2,4},{3,5},{4,2},{5,3},{6,0},{7,1},{8,14},{9,15},{10,... | collective-permute-start | bytes 3145736 | tf_op jit(solution)/shard_map/ppermute | solution.py:261
  68.0 50.0 %copy-start.3 = (bf16[4,1024,512]{2,1,0:T(8,128)(2,1)S(1)}, bf16[4,1024,512]{2,1,0:T(8,128)(2,1)}, u32[]{:S(2)}) copy-start(bf16[4,1024,512]{2,1,0:T(8,128)(2,1)} %param.9) | copy-start | bytes 12582916
  91.2 135.2 %collective-permute-start.15 = (bf16[1024,2048]{1,0:T(8,128)(2,1)}, bf16[1024,2048]{1,0:T(8,128)(2,1)}, u32[]{:S(2)}, u32[]{:S(2)}) collective-permute-start(bf16[1024,2048]{1,0:T(8,128)(2,1)} %constant_dynamic-update-slice_fusion.2.refs_3_), channel_id=1, source_target_pairs={{0,1},{1,0},{2,3},{3,2},{4,5},{5,4},{6,7},{7,6},{8,9},{9,8},{10,11... | collective-permute-start | bytes 12582920 | tf_op jit(solution)/shard_map/ppermute | solution.py:261
  91.2 26.6 %collective-permute-start.17 = (bf16[128,2048]{1,0:T(8,128)(2,1)S(1)}, bf16[128,2048]{1,0:T(8,128)(2,1)}, u32[]{:S(2)}, u32[]{:S(2)}) collective-permute-start(bf16[128,2048]{1,0:T(8,128)(2,1)S(1)} %get-tuple-element.36), channel_id=1, source_target_pairs={{0,16},{8,24},{16,0},{24,8},{1,17},{9,25},{17,1},{25,9},{2,18},{10... | collective-permute-start | bytes 1572872 | tf_op jit(solution)/shard_map/ppermute | solution.py:266
  92.0 31.5 %collective-permute-start.6 = (bf16[128,2048]{1,0:T(8,128)(2,1)}, bf16[128,2048]{1,0:T(8,128)(2,1)}, u32[]{:S(2)}, u32[]{:S(2)}) collective-permute-start(bf16[128,2048]{1,0:T(8,128)(2,1)} %get-tuple-element.38), channel_id=1, source_target_pairs={{0,6},{1,7},{2,4},{3,5},{4,2},{5,3},{6,0},{7,1},{8,14},{9,15},{10,... | collective-permute-start | bytes 1572872 | tf_op jit(solution)/shard_map/ppermute | solution.py:261
  93.5 31.6 %collective-permute-start.5 = (bf16[128,2048]{1,0:T(8,128)(2,1)}, bf16[128,2048]{1,0:T(8,128)(2,1)}, u32[]{:S(2)}, u32[]{:S(2)}) collective-permute-start(bf16[128,2048]{1,0:T(8,128)(2,1)} %get-tuple-element.38), channel_id=1, source_target_pairs={{0,4},{1,5},{2,6},{3,7},{4,0},{5,1},{6,2},{7,3},{8,12},{9,13},{10,... | collective-permute-start | bytes 1572872 | tf_op jit(solution)/shard_map/ppermute | solution.py:261
  93.6 34.3 %collective-permute-start.4 = (bf16[128,2048]{1,0:T(8,128)(2,1)}, bf16[128,2048]{1,0:T(8,128)(2,1)}, u32[]{:S(2)}, u32[]{:S(2)}) collective-permute-start(bf16[128,2048]{1,0:T(8,128)(2,1)} %get-tuple-element.38), channel_id=1, source_target_pairs={{0,2},{1,3},{2,0},{3,1},{4,6},{5,7},{6,4},{7,5},{8,10},{9,11},{10,... | collective-permute-start | bytes 1572872 | tf_op jit(solution)/shard_map/ppermute | solution.py:261
  95.9 23.5 %copy-start.4 = (s32[1,1,8]{2,1,0:T(1,128)S(1)}, s32[1,1,8]{2,1,0:T(1,128)}, u32[]{:S(2)}) copy-start(s32[1,1,8]{2,1,0:T(1,128)} %param.17) | copy-start | bytes 100
  117.8 15.1 %collective-permute-start.18 = (bf16[128,2048]{1,0:T(8,128)(2,1)}, bf16[128,2048]{1,0:T(8,128)(2,1)}, u32[]{:S(2)}, u32[]{:S(2)}) collective-permute-start(bf16[128,2048]{1,0:T(8,128)(2,1)} %collective-permute-done.17), channel_id=1, source_target_pairs={{0,2},{1,3},{2,0},{3,1},{4,6},{5,7},{6,4},{7,5},{8,10},{9,11},{10,... | collective-permute-start | bytes 1572872 | tf_op jit(solution)/shard_map/ppermute | solution.py:261
  123.5 30.6 %copy-start.5 = (s32[1,1,16]{2,1,0:T(1,128)S(1)}, s32[1,1,16]{2,1,0:T(1,128)}, u32[]{:S(2)}) copy-start(s32[1,1,16]{2,1,0:T(1,128)} %param.16) | copy-start | bytes 196
  123.5 83.3 %collective-permute-start.9 = (bf16[512,1024]{1,0:T(8,128)(2,1)}, bf16[512,1024]{1,0:T(8,128)(2,1)}, u32[]{:S(2)}, u32[]{:S(2)}) collective-permute-start(bf16[512,1024]{1,0:T(8,128)(2,1)} %bitcast.12), channel_id=1, source_target_pairs={{0,24},{8,0},{16,8},{24,16},{1,25},{9,1},{17,9},{25,17},{2,26},{10... | collective-permute-start | bytes 3145736 | tf_op jit(solution)/shard_map/ppermute | solution.py:266
  125.1 28.1 %collective-permute-start.20 = (bf16[128,2048]{1,0:T(8,128)(2,1)}, bf16[128,2048]{1,0:T(8,128)(2,1)S(1)}, u32[]{:S(2)}, u32[]{:S(2)}) collective-permute-start(bf16[128,2048]{1,0:T(8,128)(2,1)} %collective-permute-done.17), channel_id=1, source_target_pairs={{0,6},{1,7},{2,4},{3,5},{4,2},{5,3},{6,0},{7,1},{8,14},{9,15},{10,... | collective-permute-start | bytes 1572872 | tf_op jit(solution)/shard_map/ppermute | solution.py:261
  127.9 24.4 %collective-permute-start.19 = (bf16[128,2048]{1,0:T(8,128)(2,1)}, bf16[128,2048]{1,0:T(8,128)(2,1)S(1)}, u32[]{:S(2)}, u32[]{:S(2)}) collective-permute-start(bf16[128,2048]{1,0:T(8,128)(2,1)} %collective-permute-done.17), channel_id=1, source_target_pairs={{0,4},{1,5},{2,6},{3,7},{4,0},{5,1},{6,2},{7,3},{8,12},{9,13},{10,... | collective-permute-start | bytes 1572872 | tf_op jit(solution)/shard_map/ppermute | solution.py:261
  132.9 69.3 %collective-permute-start.7 = (bf16[512,2048]{1,0:T(8,128)(2,1)S(1)}, bf16[512,2048]{1,0:T(8,128)(2,1)}, u32[]{:S(2)}, u32[]{:S(2)}) collective-permute-start(bf16[512,2048]{1,0:T(8,128)(2,1)S(1)} %pad_maximum_fusion.refs_1_), channel_id=1, source_target_pairs={{0,1},{1,0},{2,3},{3,2},{4,5},{5,4},{6,7},{7,6},{8,9},{9,8},{10,11... | collective-permute-start | bytes 6291464 | tf_op jit(solution)/shard_map/ppermute | solution.py:261
  152.3 46.9 %collective-permute-start.16 = (bf16[512,1024]{1,0:T(8,128)(2,1)}, bf16[512,1024]{1,0:T(8,128)(2,1)}, u32[]{:S(2)}, u32[]{:S(2)}) collective-permute-start(bf16[512,1024]{1,0:T(8,128)(2,1)} %bitcast.17), channel_id=1, source_target_pairs={{0,16},{8,24},{16,0},{24,8},{1,17},{9,25},{17,1},{25,9},{2,18},{10... | collective-permute-start | bytes 3145736 | tf_op jit(solution)/shard_map/ppermute | solution.py:266
  154.0 82.3 %collective-permute-start.21 = (bf16[512,2048]{1,0:T(8,128)(2,1)}, bf16[512,2048]{1,0:T(8,128)(2,1)}, u32[]{:S(2)}, u32[]{:S(2)}) collective-permute-start(bf16[512,2048]{1,0:T(8,128)(2,1)} %constant_dynamic-update-slice_fusion.7.refs_2_), channel_id=1, source_target_pairs={{0,1},{1,0},{2,3},{3,2},{4,5},{5,4},{6,7},{7,6},{8,9},{9,8},{10,11... | collective-permute-start | bytes 6291464 | tf_op jit(solution)/shard_map/ppermute | solution.py:261
  154.8 7.9 %all-to-all-start = ((s32[8,2,1]{1,2,0:T(1,128)}), s32[8,2,1]{1,2,0:T(1,128)S(1)}, u32[]{:S(2)}, u32[]{:S(2)}) async-start(s32[8,2,1]{1,2,0:T(1,128)} %bitcast.21), calls=%async_computation | async-start | bytes 8192 | tf_op jit(solution)/shard_map/all_to_all | solution.py:339
  162.6 36.6 %all-to-all-start.1 = ((bf16[16,128,128]{2,1,0:T(8,128)(2,1)}), bf16[16,128,128]{2,1,0:T(8,128)(2,1)}, u32[]{:S(2)}, u32[]{:S(2)}) async-start(bf16[16,128,128]{2,1,0:T(8,128)(2,1)} %bitcast.68), calls=%async_computation.1 | async-start | bytes 1048576 | tf_op jit(solution)/shard_map/all_to_all | solution.py:338
  199.2 27.2 %collective-permute-start.8 = (bf16[512,1024]{1,0:T(8,128)(2,1)}, bf16[512,1024]{1,0:T(8,128)(2,1)}, u32[]{:S(2)}, u32[]{:S(2)}) collective-permute-start(bf16[512,1024]{1,0:T(8,128)(2,1)} %bitcast.67), channel_id=1, source_target_pairs={{0,8},{8,16},{16,24},{24,0},{1,9},{9,17},{17,25},{25,1},{2,10},{10... | collective-permute-start | bytes 3145736 | tf_op jit(solution)/shard_map/ppermute | solution.py:266
  202.2 40.6 %collective-permute-start = (f32[1,128]{1,0:T(1,128)S(1)}, f32[1,128]{1,0:T(1,128)S(1)}, u32[]{:S(2)}, u32[]{:S(2)}) collective-permute-start(f32[1,128]{1,0:T(1,128)S(1)} %bitcast.71), channel_id=1, source_target_pairs={{0,1},{1,0},{2,3},{3,2},{4,5},{5,4},{6,7},{7,6},{8,9},{9,8},{10,11... | collective-permute-start | bytes 1544 | tf_op jit(solution)/shard_map/ppermute | solution.py:261
  236.4 15.7 %copy-start.1 = (f32[1,512,2048]{2,1,0:T(8,128)S(1)}, f32[1,512,2048]{2,1,0:T(8,128)}, u32[]{:S(2)}) copy-start(f32[1,512,2048]{2,1,0:T(8,128)} %param.12) | copy-start | bytes 12582916
  236.4 15.7 %copy-start.2 = (f32[1,512,2048]{2,1,0:T(8,128)S(1)}, f32[1,512,2048]{2,1,0:T(8,128)}, u32[]{:S(2)}) copy-start(f32[1,512,2048]{2,1,0:T(8,128)} %param.13) | copy-start | bytes 12582916
  242.8 3.7 collective-permute-start.22
  242.9 5.6 %collective-permute-start.3 = (f32[1,128]{1,0:T(1,128)S(1)}, f32[1,128]{1,0:T(1,128)S(1)}, u32[]{:S(2)}, u32[]{:S(2)}) collective-permute-start(f32[1,128]{1,0:T(1,128)S(1)} %bitcast_add_fusion.refs_0_), channel_id=1, source_target_pairs={{0,6},{1,7},{2,4},{3,5},{4,2},{5,3},{6,0},{7,1},{8,14},{9,15},{10,... | collective-permute-start | bytes 1544 | tf_op jit(solution)/shard_map/ppermute | solution.py:261
  243.0 7.0 %collective-permute-start.2 = (f32[1,128]{1,0:T(1,128)S(1)}, f32[1,128]{1,0:T(1,128)S(1)}, u32[]{:S(2)}, u32[]{:S(2)}) collective-permute-start(f32[1,128]{1,0:T(1,128)S(1)} %bitcast_add_fusion.refs_0_), channel_id=1, source_target_pairs={{0,4},{1,5},{2,6},{3,7},{4,0},{5,1},{6,2},{7,3},{8,12},{9,13},{10,... | collective-permute-start | bytes 1544 | tf_op jit(solution)/shard_map/ppermute | solution.py:261
  245.0 5.0 %collective-permute-start.1 = (f32[1,128]{1,0:T(1,128)S(1)}, f32[1,128]{1,0:T(1,128)S(1)}, u32[]{:S(2)}, u32[]{:S(2)}) collective-permute-start(f32[1,128]{1,0:T(1,128)S(1)} %bitcast_add_fusion.refs_0_), channel_id=1, source_target_pairs={{0,2},{1,3},{2,0},{3,1},{4,6},{5,7},{6,4},{7,5},{8,10},{9,11},{10,... | collective-permute-start | bytes 1544 | tf_op jit(solution)/shard_map/ppermute | solution.py:261
  246.5 4.5 %collective-permute-start.25 = (f32[1,128]{1,0:T(1,128)S(1)}, f32[1,128]{1,0:T(1,128)S(1)}, u32[]{:S(2)}, u32[]{:S(2)}) collective-permute-start(f32[1,128]{1,0:T(1,128)S(1)} %add.120.refs_4_), channel_id=1, source_target_pairs={{0,6},{1,7},{2,4},{3,5},{4,2},{5,3},{6,0},{7,1},{8,14},{9,15},{10,... | collective-permute-start | bytes 1544 | tf_op jit(solution)/shard_map/ppermute | solution.py:261
  246.5 4.4 %collective-permute-start.24 = (f32[1,128]{1,0:T(1,128)S(1)}, f32[1,128]{1,0:T(1,128)S(1)}, u32[]{:S(2)}, u32[]{:S(2)}) collective-permute-start(f32[1,128]{1,0:T(1,128)S(1)} %add.120.refs_4_), channel_id=1, source_target_pairs={{0,4},{1,5},{2,6},{3,7},{4,0},{5,1},{6,2},{7,3},{8,12},{9,13},{10,... | collective-permute-start | bytes 1544 | tf_op jit(solution)/shard_map/ppermute | solution.py:261
  248.5 3.6 collective-permute-start.23
  256.8 27.9 %collective-permute-start.27 = (bf16[256,2048]{1,0:T(8,128)(2,1)S(1)}, bf16[256,2048]{1,0:T(8,128)(2,1)S(1)}, u32[]{:S(2)}, u32[]{:S(2)}) collective-permute-start(bf16[256,2048]{1,0:T(8,128)(2,1)S(1)} %get-tuple-element.29), channel_id=1, source_target_pairs={{8,0},{16,8},{24,16},{9,1},{17,9},{25,17},{10,2},{18,10},{26,18},{... | collective-permute-start | bytes 3145736 | tf_op jit(solution)/shard_map/ppermute | solution.py:324
  258.1 28.1 %collective-permute-start.26 = (bf16[256,2048]{1,0:T(8,128)(2,1)S(1)}, bf16[256,2048]{1,0:T(8,128)(2,1)S(1)}, u32[]{:S(2)}, u32[]{:S(2)}) collective-permute-start(bf16[256,2048]{1,0:T(8,128)(2,1)S(1)} %get-tuple-element.29), channel_id=1, source_target_pairs={{0,8},{8,16},{16,24},{1,9},{9,17},{17,25},{2,10},{10,18},{18,26},{... | collective-permute-start | bytes 3145736 | tf_op jit(solution)/shard_map/ppermute | solution.py:323
  267.5 39.7 %collective-permute-start.29 = (bf16[256,2048]{1,0:T(8,128)(2,1)S(1)}, bf16[256,2048]{1,0:T(8,128)(2,1)S(1)}, u32[]{:S(2)}, u32[]{:S(2)}) collective-permute-start(bf16[256,2048]{1,0:T(8,128)(2,1)S(1)} %get-tuple-element.30), channel_id=1, source_target_pairs={{8,0},{16,8},{24,16},{9,1},{17,9},{25,17},{10,2},{18,10},{26,18},{... | collective-permute-start | bytes 3145736 | tf_op jit(solution)/shard_map/ppermute | solution.py:324
  268.8 39.9 %collective-permute-start.28 = (bf16[256,2048]{1,0:T(8,128)(2,1)S(1)}, bf16[256,2048]{1,0:T(8,128)(2,1)S(1)}, u32[]{:S(2)}, u32[]{:S(2)}) collective-permute-start(bf16[256,2048]{1,0:T(8,128)(2,1)S(1)} %get-tuple-element.30), channel_id=1, source_target_pairs={{0,8},{8,16},{16,24},{1,9},{9,17},{17,25},{2,10},{10,18},{18,26},{... | collective-permute-start | bytes 3145736 | tf_op jit(solution)/shard_map/ppermute | solution.py:323
  284.7 44.9 %collective-permute-start.31 = (bf16[256,2048]{1,0:T(8,128)(2,1)S(1)}, bf16[256,2048]{1,0:T(8,128)(2,1)S(1)}, u32[]{:S(2)}, u32[]{:S(2)}) collective-permute-start(bf16[256,2048]{1,0:T(8,128)(2,1)S(1)} %collective-permute-done.27.below_ref), channel_id=1, source_target_pairs={{8,0},{16,8},{24,16},{9,1},{17,9},{25,17},{10,2},{18,10},{26,18},{... | collective-permute-start | bytes 3145736 | tf_op jit(solution)/shard_map/ppermute | solution.py:324
  286.2 44.9 %collective-permute-start.30 = (bf16[256,2048]{1,0:T(8,128)(2,1)S(1)}, bf16[256,2048]{1,0:T(8,128)(2,1)S(1)}, u32[]{:S(2)}, u32[]{:S(2)}) collective-permute-start(bf16[256,2048]{1,0:T(8,128)(2,1)S(1)} %collective-permute-done.26.above_ref), channel_id=1, source_target_pairs={{0,8},{8,16},{16,24},{1,9},{9,17},{17,25},{2,10},{10,18},{18,26},{... | collective-permute-start | bytes 3145736 | tf_op jit(solution)/shard_map/ppermute | solution.py:323
  307.2 44.9 %collective-permute-start.33 = (bf16[256,2048]{1,0:T(8,128)(2,1)S(1)}, bf16[256,2048]{1,0:T(8,128)(2,1)S(1)}, u32[]{:S(2)}, u32[]{:S(2)}) collective-permute-start(bf16[256,2048]{1,0:T(8,128)(2,1)S(1)} %collective-permute-done.29.below_ref), channel_id=1, source_target_pairs={{8,0},{16,8},{24,16},{9,1},{17,9},{25,17},{10,2},{18,10},{26,18},{... | collective-permute-start | bytes 3145736 | tf_op jit(solution)/shard_map/ppermute | solution.py:324
  308.7 44.9 %collective-permute-start.32 = (bf16[256,2048]{1,0:T(8,128)(2,1)S(1)}, bf16[256,2048]{1,0:T(8,128)(2,1)S(1)}, u32[]{:S(2)}, u32[]{:S(2)}) collective-permute-start(bf16[256,2048]{1,0:T(8,128)(2,1)S(1)} %collective-permute-done.28.above_ref), channel_id=1, source_target_pairs={{0,8},{8,16},{16,24},{1,9},{9,17},{17,25},{2,10},{10,18},{18,26},{... | collective-permute-start | bytes 3145736 | tf_op jit(solution)/shard_map/ppermute | solution.py:323
  329.7 44.9 %collective-permute-start.35 = (bf16[256,2048]{1,0:T(8,128)(2,1)S(1)}, bf16[256,2048]{1,0:T(8,128)(2,1)S(1)}, u32[]{:S(2)}, u32[]{:S(2)}) collective-permute-start(bf16[256,2048]{1,0:T(8,128)(2,1)S(1)} %collective-permute-done.31.below_ref), channel_id=1, source_target_pairs={{8,0},{16,8},{24,16},{9,1},{17,9},{25,17},{10,2},{18,10},{26,18},{... | collective-permute-start | bytes 3145736 | tf_op jit(solution)/shard_map/ppermute | solution.py:324
  331.1 44.9 %collective-permute-start.34 = (bf16[256,2048]{1,0:T(8,128)(2,1)S(1)}, bf16[256,2048]{1,0:T(8,128)(2,1)S(1)}, u32[]{:S(2)}, u32[]{:S(2)}) collective-permute-start(bf16[256,2048]{1,0:T(8,128)(2,1)S(1)} %collective-permute-done.30.above_ref), channel_id=1, source_target_pairs={{0,8},{8,16},{16,24},{1,9},{9,17},{17,25},{2,10},{10,18},{18,26},{... | collective-permute-start | bytes 3145736 | tf_op jit(solution)/shard_map/ppermute | solution.py:323
  352.1 41.8 %collective-permute-start.37 = (bf16[256,2048]{1,0:T(8,128)(2,1)S(1)}, bf16[256,2048]{1,0:T(8,128)(2,1)S(1)}, u32[]{:S(2)}, u32[]{:S(2)}) collective-permute-start(bf16[256,2048]{1,0:T(8,128)(2,1)S(1)} %collective-permute-done.33.below_ref), channel_id=1, source_target_pairs={{8,0},{16,8},{24,16},{9,1},{17,9},{25,17},{10,2},{18,10},{26,18},{... | collective-permute-start | bytes 3145736 | tf_op jit(solution)/shard_map/ppermute | solution.py:324
  353.6 41.6 %collective-permute-start.36 = (bf16[256,2048]{1,0:T(8,128)(2,1)S(1)}, bf16[256,2048]{1,0:T(8,128)(2,1)S(1)}, u32[]{:S(2)}, u32[]{:S(2)}) collective-permute-start(bf16[256,2048]{1,0:T(8,128)(2,1)S(1)} %collective-permute-done.32.above_ref), channel_id=1, source_target_pairs={{0,8},{8,16},{16,24},{1,9},{9,17},{17,25},{2,10},{10,18},{18,26},{... | collective-permute-start | bytes 3145736 | tf_op jit(solution)/shard_map/ppermute | solution.py:323
where the time goes:
time: 398 us; the launch traced here: 397 us
  waiting for transfers between devices  250 us (63%)
  starting transfers between devices  67.3 us (17%)
  Pallas kernels  40.2 us (10%)
  local copies, waits for them, and re-layouts  22.6 us (6%)
  between operations  8.8 us (2%)
  other arithmetic  6.24 us (2%)
    ppermute x6, waiting for transfers between devices, shift(): lax.ppermute(value, 'grp', [(i, (i + step) % groups) for i in range(group...  93.1 us
    ppermute x6, waiting for transfers between devices, local(): below[chunk] = lax.ppermute(below[chunk], 'grp', down)  86.3 us
    ppermute x20, waiting for transfers between devices, swap(): return lax.ppermute(value, 'dev', [(i, i ^ mask) for i in range(devices)])  64.3 us
    ppermute x6, starting transfers between devices, local(): above[chunk] = lax.ppermute(above[chunk], 'grp', up)  27 us
    pallas_call x3, Pallas kernels, accumulate(): pl.pallas_call(kernel, grid=(tiles,), in_specs=([block] if acc is not Non...  20.8 us
    ppermute x20, starting transfers between devices, swap(): return lax.ppermute(value, 'dev', [(i, i ^ mask) for i in range(devices)])  17.7 us
    pallas_call x6, Pallas kernels, place(): pl.pallas_call(kernel, grid_spec=pltpu.PrefetchScalarGridSpec(num_scalar_...  9.88 us
    pallas_call x2, Pallas kernels, update(): pl.pallas_call(kernel, grid_spec=pltpu.PrefetchScalarGridSpec(num_scalar_...  9.56 us
  transfers between devices with their start and end apart: 40, of which 24 were waited for; matrix products, arithmetic and copies ran while one was open for 6% of the time, Pallas kernels for 9%

commit v1 on v0

--- a/solution.py
+++ b/solution.py
@@ -12,12 +12,63 @@
 table_rate = 0.5
 table_decay = 0.2
 eps_norm = 1e-06
-weight_chunks = 2
+weight_parts = (1, 6, 1)
 lanes = 128
 mib = 1 << 20
 
 
 anywhere = pl.BlockSpec(memory_space=pl.ANY)
+
+
+def layer_of(owner_ref, target):
+    return sum(jnp.where(owner_ref[layer] == target, layer, 0) for layer in range(owner_ref.shape[0]))
+
+
+def chunks_of(rows):
+    unit = rows // sum(weight_parts)
+    starts = [unit * sum(weight_parts[:i]) for i in range(len(weight_parts))]
+    return [(start, unit * part) for start, part in zip(starts, weight_parts)]
+
+
+def pick(layer_owner, value, steps):
+    groups = lax.axis_size("grp")
+    count = len(steps)
+
+    def kernel(owner_ref, value_ref, *refs):
+        sems = refs[count]
+        group = lax.axis_index("grp")
+        copies = [
+            pltpu.make_async_copy(
+                value_ref.at[layer_of(owner_ref, lax.rem(group + step, groups))],
+                refs[i],
+                sems.at[i],
+            )
+            for i, step in enumerate(steps)
+        ]
+        for copy in copies:
+            copy.start()
+        for copy in copies:
+            copy.wait()
+
+    shape = value.shape[1:]
+    return pl.pallas_call(
+        kernel,
+        grid_spec=pltpu.PrefetchScalarGridSpec(
+            num_scalar_prefetch=1,
+            grid=(1,),
+            in_specs=[anywhere],
+            out_specs=[pl.BlockSpec(shape, lambda i, owner: (0, 0))] * count,
+            scratch_shapes=[pltpu.SemaphoreType.DMA((count,))],
+        ),
+        out_shape=[jax.ShapeDtypeStruct(shape, value.dtype)] * count,
+        compiler_params=pltpu.CompilerParams(
+            vmem_limit_bytes=4 * count * shape[0] * shape[1] + 2 * mib
+        ),
+        cost_estimate=pl.CostEstimate(
+            flops=0, bytes_accessed=4 * count * shape[0] * shape[1], transcendentals=0
+        ),
+        name="pick",
+    )(layer_owner, value)
 
 
 def accumulate(acc, inputs, near, far, last):
@@ -109,15 +160,15 @@
     return result if last else result[0]
 
 
-def update(slot_layer, weight_squares, grad_squares, grad, master, moment, chunk, buffers):
+def update(layer_owner, weight_squares, grad_squares, grad, master, moment, chunk, buffers):
     groups = lax.axis_size("grp")
     rows, columns = grad.shape
-    height = rows // weight_chunks
-    step = min(height, 32)
-    steps = height // step
+    start, height = chunk
+    step = min(32, rows // sum(weight_parts))
+    first, steps = start // step, height // step
     count = len(weight_squares)
 
-    def kernel(slot_ref, *refs):
+    def kernel(owner_ref, *refs):
         refs = list(refs)
         weight_refs = [refs.pop(0) for _ in range(count)]
         grad_refs = [refs.pop(0) for _ in range(count)]
@@ -141,10 +192,10 @@
         piece_ref[...] = piece
         weights_out[0] = piece
 
-    vector = pl.BlockSpec((1, lanes), lambda i, slot: (0, 0))
-    block = pl.BlockSpec((step, columns), lambda i, slot: (chunk * steps + i, 0))
-    operands = [slot_layer, *weight_squares, *grad_squares, grad, master, moment]
-    first = len(operands)
+    vector = pl.BlockSpec((1, lanes), lambda i, owner: (0, 0))
+    block = pl.BlockSpec((step, columns), lambda i, owner: (first + i, 0))
+    operands = [layer_owner, *weight_squares, *grad_squares, grad, master, moment]
+    taken = len(operands)
     return pl.pallas_call(
         kernel,
         grid_spec=pltpu.PrefetchScalarGridSpec(
@@ -152,10 +203,10 @@
             grid=(steps,),
             in_specs=[vector] * (2 * count) + [block] * 3 + [anywhere] * len(buffers),
             out_specs=[
-                pl.BlockSpec((step, columns), lambda i, slot: (i, 0)),
+                pl.BlockSpec((step, columns), lambda i, owner: (i, 0)),
                 pl.BlockSpec(
                     (1, step, columns),
-                    lambda i, slot: (slot[lax.axis_index("grp")], chunk * steps + i, 0),
+                    lambda i, owner: (layer_of(owner, lax.axis_index("grp")), first + i, 0),
                 ),
                 block,
                 block,
@@ -167,7 +218,7 @@
             jax.ShapeDtypeStruct((rows, columns), jnp.float32),
             jax.ShapeDtypeStruct((rows, columns), jnp.float32),
         ],
-        input_output_aliases={first + i: 1 + i for i in range(len(buffers))},
+        input_output_aliases={taken + i: 1 + i for i in range(len(buffers))},
         compiler_params=pltpu.CompilerParams(vmem_limit_bytes=48 * step * columns + 2 * mib),
         cost_estimate=pl.CostEstimate(
             flops=8 * height * columns, bytes_accessed=24 * height * columns, transcendentals=0
@@ -176,11 +227,12 @@
     )(*operands, *buffers)
 
 
-def place(slot_layer, weights, above, below, step, chunk):
+def place(layer_owner, weights, above, below, step, chunk):
     groups = lax.axis_size("grp")
-    height, columns = above.shape
-
-    def kernel(slot_ref, weights_ref, above_ref, below_ref, out_ref, held, in_sem, out_sem):
+    columns = above.shape[1]
+    start, height = chunk
+
+    def kernel(owner_ref, weights_ref, above_ref, below_ref, out_ref, held, in_sem, out_sem):
         group = lax.axis_index("grp")
         sides = (
             (above_ref, group - step, group >= step),
@@ -197,9 +249,9 @@
             @pl.when(valid)
             def _():
                 pltpu.make_async_copy(ref, held.at[side], in_sem.at[side]).wait()
-                layer = slot_ref[source]
+                layer = layer_of(owner_ref, source)
                 copy = pltpu.make_async_copy(
-                    held.at[side], out_ref.at[layer, pl.ds(chunk * height, height)], out_sem.at[side]
+                    held.at[side], out_ref.at[layer, pl.ds(start, height)], out_sem.at[side]
                 )
                 copy.start()
 
@@ -208,7 +260,7 @@
             @pl.when(valid)
             def _():
                 pltpu.make_async_copy(
-                    held.at[side], out_ref.at[0, pl.ds(chunk * height, height)], out_sem.at[side]
+                    held.at[side], out_ref.at[0, pl.ds(start, height)], out_sem.at[side]
                 ).wait()
 
     return pl.pallas_call(
@@ -231,7 +283,7 @@
             flops=0, bytes_accessed=8 * height * columns, transcendentals=0
         ),
         name="place",
-    )(slot_layer, weights, above, below)
+    )(layer_owner, weights, above, below)
 
 
 def rounds_of(groups):
@@ -269,30 +321,28 @@
         pair = value + swap(value, 1)
         return [pair] + [swap(pair, mask) for mask in masks]
 
-    layers = jnp.arange(groups, dtype=jnp.int32)
-    slot_layer = jnp.sum(
-        jnp.where(layer_owner[None, :] == layers[:, None], layers[None, :], 0), axis=1
-    )
     master = master_weights[0]
     moment = momentum[0]
-    _, columns = master.shape
+    rows, columns = master.shape
 
     rounds = rounds_of(groups)
     steps = [step for some in rounds for step in some]
 
+    layers = jnp.arange(groups, dtype=jnp.int32)
+
     def owned(value, step):
-        return lax.dynamic_index_in_dim(
-            value, slot_layer[(group + step) % groups], 0, keepdims=False
-        )
-
-    g_own = {step: shift(owned(output_grads, step), step) for step in steps}
+        target = (group + step) % groups
+        layer = jnp.sum(jnp.where(layer_owner == target, layers, 0)).astype(jnp.uint32)
+        return lax.dynamic_index_in_dim(value, layer, 0, keepdims=False)
+
+    g_own = dict(zip(steps, pick(layer_owner, output_grads, steps)))
+    new_table = update_table(table_blocks[0], block_grads[0, 0], block_ids[0, 0], block_counts[0, 0])
+    g_own = {step: shift(g_own[step], step) for step in steps}
     x_own = {step: shift(owned(layer_inputs, step).T, step) for step in steps}
 
     squares = jnp.sum(master * master, axis=0, keepdims=True)
     squares = jnp.sum(squares.reshape(columns // lanes, lanes), axis=0, keepdims=True)
     weight_squares = dev_parts(squares)
-
-    new_table = update_table(table_blocks[0], block_grads, block_ids, block_counts, g_own[steps[1]])
 
     grad = None
     for some in rounds:
@@ -302,42 +352,41 @@
         far = swap(near, 1)
         inputs = [x_own[step] for step in some]
         last = some is rounds[-1]
-        if last:
-            inputs[0], new_table = lax.optimization_barrier((inputs[0], new_table))
         grad = accumulate(grad, inputs, near, far, last)
     grad, squares = grad
     grad_squares = dev_parts(squares)
 
     up = [(i, i + 1) for i in range(groups - 1)]
     down = [(i + 1, i) for i in range(groups - 1)]
+    chunks = chunks_of(rows)
     buffers, above, below = [], [], []
-    for chunk in range(weight_chunks):
+    for chunk in chunks:
         piece, *buffers = update(
-            slot_layer, weight_squares, grad_squares, grad, master, moment, chunk, buffers
+            layer_owner, weight_squares, grad_squares, grad, master, moment, chunk, buffers
         )
         above.append(piece)
         below.append(piece)
     new_weights, new_master, new_moment = buffers
     for step in range(1, groups):
-        for chunk in range(weight_chunks):
-            above[chunk] = lax.ppermute(above[chunk], "grp", up)
-            below[chunk] = lax.ppermute(below[chunk], "grp", down)
-            new_weights = place(slot_layer, new_weights, above[chunk], below[chunk], step, chunk)
+        for number, chunk in enumerate(chunks):
+            above[number] = lax.ppermute(above[number], "grp", up)
+            below[number] = lax.ppermute(below[number], "grp", down)
+            new_weights = place(layer_owner, new_weights, above[number], below[number], step, chunk)
     return (new_master[None], new_moment[None], new_weights, new_table[None])
 
 
-def update_table(table, block_grads, block_ids, block_counts, behind):
+def update_table(table, grads, ids, counts):
     devices = lax.axis_size("dev")
-    grads, ids, _ = lax.optimization_barrier((block_grads[0, 0], block_ids[0, 0], behind))
-    counts = block_counts[0, 0]
     capacity = ids.shape[0] // devices
     slot_rank = jnp.arange(devices * capacity, dtype=jnp.int32) % capacity
     live = slot_rank < jnp.repeat(counts, capacity)
     tagged = jnp.where(live, ids, -1)
-    got_grads, got_ids = (
-        lax.all_to_all(grads, "dev", split_axis=0, concat_axis=0, tiled=True),
-        lax.all_to_all(tagged, "dev", split_axis=0, concat_axis=0, tiled=True),
-    )
+    got_ids = lax.all_to_all(tagged, "dev", split_axis=0, concat_axis=0, tiled=True)
+    got_grads = lax.all_to_all(grads, "dev", split_axis=0, concat_axis=0, tiled=True)
+    return move_table(table, got_ids, got_grads)
+
+
+def move_table(table, got_ids, got_grads):
     nblocks = table.shape[0]
     width = table.shape[1] * table.shape[2]
     matches = got_ids[None, :] == jnp.arange(nblocks, dtype=jnp.int32)[:, None]

time: 398 us -> 432 us (1.085)
  starting transfers between devices: 67.3 us -> 84.6 us
  Pallas kernels: 40.2 us -> 50.5 us
  local copies, waits for them, and re-layouts: 22.6 us -> 32.5 us
  blocking collectives: 0 us -> 7.04 us
  waiting for transfers between devices: 250 us -> 243 us
  between operations: 8.8 us -> 3.66 us
    ppermute x12 -> x18, waiting for transfers between devices: 89.6 us -> 61.9 us  [the longest x9 60.1 us: local(): above[number] = lax.ppermute(above[number], 'grp', up)]
    ppermute x6, waiting for transfers between devices: 93.1 us -> 113 us  [shift(): lax.ppermute(value, 'grp', [(i, (i + step) % groups) for i in range(group...]
    ppermute x12 -> x18, starting transfers between devices: 34.7 us -> 52.8 us  [the longest x9 41.2 us: local(): above[number] = lax.ppermute(above[number], 'grp', up)]
    unnamed x18 -> x43, local copies, waits for them, and re-layouts: 7.62 us -> 18.3 us
    pallas_call x6 -> x9, Pallas kernels: 9.88 us -> 18.8 us  [place(): pl.pallas_call(kernel, grid_spec=pltpu.PrefetchScalarGridSpec(num_scalar_...]
    all_to_all x0 -> x1, blocking collectives: none -> 7.04 us  [update_table(): lax.all_to_all(tagged, 'dev', split_axis=0, concat_axis=0, tiled=True)]
    ppermute x20, waiting for transfers between devices: 64.3 us -> 68.8 us  [swap(): return lax.ppermute(value, 'dev', [(i, i ^ mask) for i in range(devices)])]
    dynamic_slice x6 -> x5, local copies, waits for them, and re-layouts: 7.39 us -> 11.2 us  [owned(): return lax.dynamic_index_in_dim(value, layer, 0, keepdims=False)]
  transfers between devices with their start and end apart: 40 -> 45, of which waited for: 24 -> 19; matrix products, arithmetic and copies ran while one was open for 6% -> 7% of each run, Pallas kernels for 9% -> 9%
where the time goes in v1:
time: 432 us; the launch traced here: 431 us
  waiting for transfers between devices  243 us (56%)
  starting transfers between devices  84.6 us (20%)
  Pallas kernels  50.5 us (12%)
  local copies, waits for them, and re-layouts  32.5 us (8%)
  other arithmetic  7.42 us (2%)
  blocking collectives  7.04 us (2%)
    ppermute x6, waiting for transfers between devices, shift(): lax.ppermute(value, 'grp', [(i, (i + step) % groups) for i in range(group...  113 us
    ppermute x20, waiting for transfers between devices, swap(): return lax.ppermute(value, 'dev', [(i, i ^ mask) for i in range(devices)])  68.8 us
    ppermute x9, waiting for transfers between devices, local(): above[number] = lax.ppermute(above[number], 'grp', up)  60.1 us
    ppermute x9, starting transfers between devices, local(): above[number] = lax.ppermute(above[number], 'grp', up)  41.2 us
    pallas_call x3, Pallas kernels, accumulate(): pl.pallas_call(kernel, grid=(tiles,), in_specs=([block] if acc is not Non...  20.6 us
    pallas_call x9, Pallas kernels, place(): pl.pallas_call(kernel, grid_spec=pltpu.PrefetchScalarGridSpec(num_scalar_...  18.8 us
    unnamed x43, local copies, waits for them, and re-layouts  18.3 us
    ppermute x20, starting transfers between devices, swap(): return lax.ppermute(value, 'dev', [(i, i ^ mask) for i in range(devices)])  17.5 us
  transfers between devices with their start and end apart: 45, of which 19 were waited for; matrix products, arithmetic and copies ran while one was open for 7% of the time, Pallas kernels for 9%

profile of v1, /device:TPU:0, one launch (start us, length us, event | category | flops | bytes accessed | tf_op | source)
XLA Modules:
  0.0 430.7 jit_solution(1670100126146148480)
XLA Ops:
  0.6 1.6 copy-done.6
  3.6 3.1 collective-permute-start.10
  6.7 2.1 collective-permute-start.11
  8.8 12.8 %collective-permute-done.10 = bf16[128,2048]{1,0:T(8,128)(2,1)S(1)} collective-permute-done((bf16[128,2048]{1,0:T(8,128)(2,1)S(1)}, bf16[128,2048]{1,0:T(8,128)(2,1)S(1)}, u32[]{:S(2)}, u32[]{:S(2)}) %collective-permute-start.10) | collective-permute-done | bytes 524320 | tf_op jit(solution)/shard_map/ppermute | solution.py:318
  22.5 8.9 %collective-permute-done.11 = bf16[128,2048]{1,0:T(8,128)(2,1)S(1)} collective-permute-done((bf16[128,2048]{1,0:T(8,128)(2,1)S(1)}, bf16[128,2048]{1,0:T(8,128)(2,1)S(1)}, u32[]{:S(2)}, u32[]{:S(2)}) %collective-permute-start.11) | collective-permute-done | bytes 524320 | tf_op jit(solution)/shard_map/ppermute | solution.py:318
  32.3 1.5 collective-permute-start.12
  33.8 1.5 collective-permute-start.13
  35.8 22.5 %collective-permute-done.12 = bf16[256,2048]{1,0:T(8,128)(2,1)S(1)} collective-permute-done((bf16[256,2048]{1,0:T(8,128)(2,1)S(1)}, bf16[256,2048]{1,0:T(8,128)(2,1)S(1)}, u32[]{:S(2)}, u32[]{:S(2)}) %collective-permute-start.12) | collective-permute-done | bytes 1048608 | tf_op jit(solution)/shard_map/ppermute | solution.py:313
  59.4 21.1 %collective-permute-done.13 = bf16[256,2048]{1,0:T(8,128)(2,1)S(1)} collective-permute-done((bf16[256,2048]{1,0:T(8,128)(2,1)S(1)}, bf16[256,2048]{1,0:T(8,128)(2,1)S(1)}, u32[]{:S(2)}, u32[]{:S(2)}) %collective-permute-start.13) | collective-permute-done | bytes 1048608 | tf_op jit(solution)/shard_map/ppermute | solution.py:313
  83.5 1.9 collective-permute-start.5
  85.4 1.4 collective-permute-start.6
  86.9 22.2 %collective-permute-done.17 = bf16[128,2048]{1,0:T(8,128)(2,1)S(1)} collective-permute-done((bf16[128,2048]{1,0:T(8,128)(2,1)S(1)}, bf16[128,2048]{1,0:T(8,128)(2,1)S(1)}, u32[]{:S(2)}, u32[]{:S(2)}) %collective-permute-start.17) | collective-permute-done | bytes 524320 | tf_op jit(solution)/shard_map/ppermute | solution.py:318
  109.7 1.7 collective-permute-start.19
  111.4 1.4 collective-permute-start.20
  113.7 10.2 %collective-permute-done.18 = bf16[128,2048]{1,0:T(8,128)(2,1)S(1)} collective-permute-done((bf16[128,2048]{1,0:T(8,128)(2,1)S(1)}, bf16[128,2048]{1,0:T(8,128)(2,1)S(1)}, u32[]{:S(2)}, u32[]{:S(2)}) %collective-permute-start.18) | collective-permute-done | bytes 524320 | tf_op jit(solution)/shard_map/ppermute | solution.py:313
  124.7 10.6 %collective-permute-done.19 = bf16[128,2048]{1,0:T(8,128)(2,1)S(1)} collective-permute-done((bf16[128,2048]{1,0:T(8,128)(2,1)S(1)}, bf16[128,2048]{1,0:T(8,128)(2,1)S(1)}, u32[]{:S(2)}, u32[]{:S(2)}) %collective-permute-start.19) | collective-permute-done | bytes 524320 | tf_op jit(solution)/shard_map/ppermute | solution.py:313
  140.2 3.9 constant_dynamic-slice_fusion
  144.1 2.3 copy.45
  146.4 1.5 collective-permute-start.8
  147.9 2.3 copy.46
  150.1 2.4 collective-permute-start.9
  154.2 1.5 copy.44
  155.7 2.6 multiply_reduce_fusion
  158.2 4.4 %accumulate.3.refs_0_ = f32[512,2048]{1,0:T(8,128)S(1)} custom-call(bf16[512,1024]{1,0:T(8,128)(2,1)S(1)} %bitcast.50, bf16[512,2048]{1,0:T(8,128)(2,1)S(1)} %constant_dynamic-update-slice_fusion.refs_1_, bf16[512,2048]{1,0:T(8,128)(2,1)} %collective-permute-done.7.refs_2_), custom_call_target="tpu_custom_call" | custom-call | flops 2147483648 | bytes 13631488 | tf_op jit(solution)/shard_map/accumulate/pallas_call | solution.py:138
  162.7 11.9 %collective-permute-done.8.refs_1_ = bf16[512,1024]{1,0:T(8,128)(2,1)} collective-permute-done((bf16[512,1024]{1,0:T(8,128)(2,1)}, bf16[512,1024]{1,0:T(8,128)(2,1)}, u32[]{:S(2)}, u32[]{:S(2)}) %collective-permute-start.8) | collective-permute-done | bytes 1048608 | tf_op jit(solution)/shard_map/ppermute | solution.py:318
  174.6 22.0 %collective-permute-done.9.refs_2_ = bf16[512,1024]{1,0:T(8,128)(2,1)} collective-permute-done((bf16[512,1024]{1,0:T(8,128)(2,1)}, bf16[512,1024]{1,0:T(8,128)(2,1)}, u32[]{:S(2)}, u32[]{:S(2)}) %collective-permute-start.9) | collective-permute-done | bytes 1048608 | tf_op jit(solution)/shard_map/ppermute | solution.py:318
  196.6 9.9 %accumulate.4.refs_0_ = f32[512,2048]{1,0:T(8,128)S(1)} custom-call(f32[512,2048]{1,0:T(8,128)S(1)} %accumulate.3.refs_0_, bf16[512,1024]{1,0:T(8,128)(2,1)} %collective-permute-done.8.refs_1_, bf16[512,1024]{1,0:T(8,128)(2,1)} %collective-permute-done.9.refs_2_, bf16[1024,2048]{1,0:T(8,128)(2,1)} %constant_dynamic-update-slice_fusion.6.refs_3_, ...), custom_call_target="tpu_custom_call" | custom-call | flops 4294967296 | bytes 18874368 | tf_op jit(solution)/shard_map/accumulate/pallas_call | solution.py:138
  206.5 35.0 %collective-permute-done.16.refs_1_ = bf16[512,1024]{1,0:T(8,128)(2,1)} collective-permute-done((bf16[512,1024]{1,0:T(8,128)(2,1)}, bf16[512,1024]{1,0:T(8,128)(2,1)}, u32[]{:S(2)}, u32[]{:S(2)}) %collective-permute-start.16) | collective-permute-done | bytes 1048608 | tf_op jit(solution)/shard_map/ppermute | solution.py:318
  241.5 6.3 %accumulate.5 = (f32[512,2048]{1,0:T(8,128)S(1)}, f32[1,128]{1,0:T(1,128)S(1)}) custom-call(f32[512,2048]{1,0:T(8,128)S(1)} %accumulate.4.refs_0_, bf16[512,1024]{1,0:T(8,128)(2,1)} %collective-permute-done.16.refs_1_, bf16[512,2048]{1,0:T(8,128)(2,1)} %constant_dynamic-update-slice_fusion.11.refs_2_, bf16[512,2048]{1,0:T(8,128)(2,1)} %collective-permute-done.21.refs_3_), custom_call_target="tpu_custom_call" | custom-call | flops 2147483648 | bytes 13631488 | tf_op jit(solution)/shard_map/accumulate/pallas_call | solution.py:138
  247.9 1.7 collective-permute-start.1
  249.6 1.5 collective-permute-start.2
  251.5 1.6 collective-permute-start.23
  253.1 1.5 collective-permute-start.24
  256.6 2.4 collective-permute-done.25.refs_7_
  259.1 1.8 update.3
  260.9 6.7 %update.4 = (bf16[384,2048]{1,0:T(8,128)(2,1)S(1)}, bf16[4,512,2048]{2,1,0:T(8,128)(2,1)}, f32[512,2048]{1,0:T(8,128)}, f32[512,2048]{1,0:T(8,128)}) custom-call(s32[4]{0:T(128)S(1)} %copy-done.12, f32[1,128]{1,0:T(1,128)S(1)} %bitcast_add_fusion.refs_0_, ...), custom_call_target="tpu_custom_call", output_to_operand_aliasing={{1}: (12, {}), {2}: (13, {}), {3}: (14, {})} | custom-call | flops 6291456 | bytes 18874368 | tf_op jit(solution)/shard_map/update/pallas_call | solution.py:199
  267.6 1.4 collective-permute-start.28
  270.3 30.5 %collective-permute-done.28.above_ref = bf16[384,2048]{1,0:T(8,128)(2,1)S(1)} collective-permute-done((bf16[384,2048]{1,0:T(8,128)(2,1)S(1)}, bf16[384,2048]{1,0:T(8,128)(2,1)S(1)}, u32[]{:S(2)}, u32[]{:S(2)}) %collective-permute-start.28) | collective-permute-done | bytes 1572896 | tf_op jit(solution)/shard_map/ppermute | solution.py:372
  300.8 4.5 %collective-permute-start.34 = (bf16[384,2048]{1,0:T(8,128)(2,1)S(1)}, bf16[384,2048]{1,0:T(8,128)(2,1)S(1)}, u32[]{:S(2)}, u32[]{:S(2)}) collective-permute-start(bf16[384,2048]{1,0:T(8,128)(2,1)S(1)} %collective-permute-done.28.above_ref), channel_id=1, source_target_pairs={{0,8},{8,16},{16,24},{1,9},{9,17},{17,25},{2,10},{10,18},{18,26},{... | collective-permute-start | bytes 4718600 | tf_op jit(solution)/shard_map/ppermute | solution.py:372
  309.0 27.3 %collective-permute-done.34.above_ref = bf16[384,2048]{1,0:T(8,128)(2,1)S(1)} collective-permute-done((bf16[384,2048]{1,0:T(8,128)(2,1)S(1)}, bf16[384,2048]{1,0:T(8,128)(2,1)S(1)}, u32[]{:S(2)}, u32[]{:S(2)}) %collective-permute-start.34) | collective-permute-done | bytes 1572896 | tf_op jit(solution)/shard_map/ppermute | solution.py:372
  336.3 5.6 %collective-permute-start.40 = (bf16[384,2048]{1,0:T(8,128)(2,1)S(1)}, bf16[384,2048]{1,0:T(8,128)(2,1)}, u32[]{:S(2)}, u32[]{:S(2)}) collective-permute-start(bf16[384,2048]{1,0:T(8,128)(2,1)S(1)} %collective-permute-done.34.above_ref), channel_id=1, source_target_pairs={{0,8},{8,16},{16,24},{1,9},{9,17},{17,25},{2,10},{10,18},{18,26},{... | collective-permute-start | bytes 4718600 | tf_op jit(solution)/shard_map/ppermute | solution.py:372
  344.4 4.6 %collective-permute-start.26 = (bf16[64,2048]{1,0:T(8,128)(2,1)}, bf16[64,2048]{1,0:T(8,128)(2,1)S(1)}, u32[]{:S(2)}, u32[]{:S(2)}) collective-permute-start(bf16[64,2048]{1,0:T(8,128)(2,1)} %copy-done.13), channel_id=1, source_target_pairs={{0,8},{8,16},{16,24},{1,9},{9,17},{17,25},{2,10},{10,18},{18,26},{... | collective-permute-start | bytes 786440 | tf_op jit(solution)/shard_map/ppermute | solution.py:372
  350.3 2.2 copy-done.1
  352.5 2.2 copy-done.3
  354.7 2.2 copy-done.5
  356.9 1.9 update.5
  358.7 5.2 %collective-permute-start.30 = (bf16[64,2048]{1,0:T(8,128)(2,1)}, bf16[64,2048]{1,0:T(8,128)(2,1)}, u32[]{:S(2)}, u32[]{:S(2)}) collective-permute-start(bf16[64,2048]{1,0:T(8,128)(2,1)} %get-tuple-element.39), channel_id=1, source_target_pairs={{0,8},{8,16},{16,24},{1,9},{9,17},{17,25},{2,10},{10,18},{18,26},{... | collective-permute-start | bytes 786440 | tf_op jit(solution)/shard_map/ppermute | solution.py:372
  364.1 7.0 %all_to_all.11 = s32[8,2,1]{1,2,0:T(1,128)S(1)} all-to-all(s32[8,2,1]{1,2,0:T(1,128)S(1)} %bitcast.57), channel_id=1, replica_groups=mesh['grp'=4,'dev'=8] {'dev'}, dimensions={0} | all-to-all | bytes 128 | tf_op jit(solution)/shard_map/all_to_all | solution.py:384
  371.1 4.1 all-to-all-start.1
  377.2 2.3 collective-permute-done.26.above_ref
  381.9 4.4 %collective-permute-start.32 = (bf16[64,2048]{1,0:T(8,128)(2,1)S(1)}, bf16[64,2048]{1,0:T(8,128)(2,1)}, u32[]{:S(2)}, u32[]{:S(2)}) collective-permute-start(bf16[64,2048]{1,0:T(8,128)(2,1)S(1)} %collective-permute-done.26.above_ref), channel_id=1, source_target_pairs={{0,8},{8,16},{16,24},{1,9},{9,17},{17,25},{2,10},{10,18},{18,26},{... | collective-permute-start | bytes 786440 | tf_op jit(solution)/shard_map/ppermute | solution.py:372
  388.4 5.7 %collective-permute-start.36 = (bf16[64,2048]{1,0:T(8,128)(2,1)}, bf16[64,2048]{1,0:T(8,128)(2,1)}, u32[]{:S(2)}, u32[]{:S(2)}) collective-permute-start(bf16[64,2048]{1,0:T(8,128)(2,1)} %collective-permute-done.30.above_ref), channel_id=1, source_target_pairs={{0,8},{8,16},{16,24},{1,9},{9,17},{17,25},{2,10},{10,18},{18,26},{... | collective-permute-start | bytes 786440 | tf_op jit(solution)/shard_map/ppermute | solution.py:372
  395.4 5.3 %collective-permute-start.38 = (bf16[64,2048]{1,0:T(8,128)(2,1)}, bf16[64,2048]{1,0:T(8,128)(2,1)}, u32[]{:S(2)}, u32[]{:S(2)}) collective-permute-start(bf16[64,2048]{1,0:T(8,128)(2,1)} %collective-permute-done.32.above_ref), channel_id=1, source_target_pairs={{0,8},{8,16},{16,24},{1,9},{9,17},{17,25},{2,10},{10,18},{18,26},{... | collective-permute-start | bytes 786440 | tf_op jit(solution)/shard_map/ppermute | solution.py:372
  400.7 1.6 multiply_reduce_fusion.1
  403.6 4.6 %collective-permute-start.42 = (bf16[64,2048]{1,0:T(8,128)(2,1)}, bf16[64,2048]{1,0:T(8,128)(2,1)S(1)}, u32[]{:S(2)}, u32[]{:S(2)}) collective-permute-start(bf16[64,2048]{1,0:T(8,128)(2,1)} %collective-permute-done.36.above_ref), channel_id=1, source_target_pairs={{0,8},{8,16},{16,24},{1,9},{9,17},{17,25},{2,10},{10,18},{18,26},{... | collective-permute-start | bytes 786440 | tf_op jit(solution)/shard_map/ppermute | solution.py:372
  409.4 1.4 fusion
  411.7 2.5 place.9.weights_ref
  414.3 1.9 place.10.weights_ref
  416.2 2.2 place.11.weights_ref
  418.4 2.2 place.12.weights_ref
  420.7 1.9 place.13.weights_ref
  422.5 2.2 place.14.weights_ref
  426.1 3.1 place.16.weights_ref
  429.3 1.3 place.17
  (111 shorter events, 38.2 us)
Async XLA Ops:
  0.6 1.6 copy-start.6
  2.2 0.7 copy-start.11
  3.6 17.9 %collective-permute-start.10 = (bf16[128,2048]{1,0:T(8,128)(2,1)S(1)}, bf16[128,2048]{1,0:T(8,128)(2,1)S(1)}, u32[]{:S(2)}, u32[]{:S(2)}) collective-permute-start(bf16[128,2048]{1,0:T(8,128)(2,1)S(1)} %get-tuple-element.23), channel_id=1, source_target_pairs={{0,8},{8,16},{16,24},{24,0},{1,9},{9,17},{17,25},{25,1},{2,10},{10... | collective-permute-start | bytes 1572872 | tf_op jit(solution)/shard_map/ppermute | solution.py:318
  6.7 24.6 %collective-permute-start.11 = (bf16[128,2048]{1,0:T(8,128)(2,1)S(1)}, bf16[128,2048]{1,0:T(8,128)(2,1)S(1)}, u32[]{:S(2)}, u32[]{:S(2)}) collective-permute-start(bf16[128,2048]{1,0:T(8,128)(2,1)S(1)} %get-tuple-element.24), channel_id=1, source_target_pairs={{0,24},{8,0},{16,8},{24,16},{1,25},{9,1},{17,9},{25,17},{2,26},{10... | collective-permute-start | bytes 1572872 | tf_op jit(solution)/shard_map/ppermute | solution.py:318
  32.3 26.0 %collective-permute-start.12 = (bf16[256,2048]{1,0:T(8,128)(2,1)S(1)}, bf16[256,2048]{1,0:T(8,128)(2,1)S(1)}, u32[]{:S(2)}, u32[]{:S(2)}) collective-permute-start(bf16[256,2048]{1,0:T(8,128)(2,1)S(1)} %get-tuple-element.64), channel_id=1, source_target_pairs={{0,2},{1,3},{2,0},{3,1},{4,6},{5,7},{6,4},{7,5},{8,10},{9,11},{10,... | collective-permute-start | bytes 3145736 | tf_op jit(solution)/shard_map/ppermute | solution.py:313
  33.8 46.7 %collective-permute-start.13 = (bf16[256,2048]{1,0:T(8,128)(2,1)S(1)}, bf16[256,2048]{1,0:T(8,128)(2,1)S(1)}, u32[]{:S(2)}, u32[]{:S(2)}) collective-permute-start(bf16[256,2048]{1,0:T(8,128)(2,1)S(1)} %get-tuple-element.64), channel_id=1, source_target_pairs={{0,4},{1,5},{2,6},{3,7},{4,0},{5,1},{6,2},{7,3},{8,12},{9,13},{10,... | collective-permute-start | bytes 3145736 | tf_op jit(solution)/shard_map/ppermute | solution.py:313
  35.3 46.2 %collective-permute-start.14 = (bf16[256,2048]{1,0:T(8,128)(2,1)S(1)}, bf16[256,2048]{1,0:T(8,128)(2,1)S(1)}, u32[]{:S(2)}, u32[]{:S(2)}) collective-permute-start(bf16[256,2048]{1,0:T(8,128)(2,1)S(1)} %get-tuple-element.64), channel_id=1, source_target_pairs={{0,6},{1,7},{2,4},{3,5},{4,2},{5,3},{6,0},{7,1},{8,14},{9,15},{10,... | collective-permute-start | bytes 3145736 | tf_op jit(solution)/shard_map/ppermute | solution.py:313
  82.6 114.0 %collective-permute-start.15 = (bf16[1024,2048]{1,0:T(8,128)(2,1)}, bf16[1024,2048]{1,0:T(8,128)(2,1)}, u32[]{:S(2)}, u32[]{:S(2)}) collective-permute-start(bf16[1024,2048]{1,0:T(8,128)(2,1)} %constant_dynamic-update-slice_fusion.6.refs_3_), channel_id=1, source_target_pairs={{0,1},{1,0},{2,3},{3,2},{4,5},{5,4},{6,7},{7,6},{8,9},{9,8},{10,11... | collective-permute-start | bytes 12582920 | tf_op jit(solution)/shard_map/ppermute | solution.py:313
  82.6 26.5 %collective-permute-start.17 = (bf16[128,2048]{1,0:T(8,128)(2,1)S(1)}, bf16[128,2048]{1,0:T(8,128)(2,1)S(1)}, u32[]{:S(2)}, u32[]{:S(2)}) collective-permute-start(bf16[128,2048]{1,0:T(8,128)(2,1)S(1)} %get-tuple-element.25), channel_id=1, source_target_pairs={{0,16},{8,24},{16,0},{24,8},{1,17},{9,25},{17,1},{25,9},{2,18},{10... | collective-permute-start | bytes 1572872 | tf_op jit(solution)/shard_map/ppermute | solution.py:318
  83.3 53.6 %copy-start.12 = (s32[4]{0:T(128)S(1)}, s32[4]{0:T(128)}, u32[]{:S(2)}) copy-start(s32[4]{0:T(128)} %owner_ref.25) | copy-start | bytes 52
  83.3 25.9 %collective-permute-start.4 = (bf16[128,2048]{1,0:T(8,128)(2,1)S(1)}, bf16[128,2048]{1,0:T(8,128)(2,1)S(1)}, u32[]{:S(2)}, u32[]{:S(2)}) collective-permute-start(bf16[128,2048]{1,0:T(8,128)(2,1)S(1)} %get-tuple-element.22), channel_id=1, source_target_pairs={{0,2},{1,3},{2,0},{3,1},{4,6},{5,7},{6,4},{7,5},{8,10},{9,11},{10,... | collective-permute-start | bytes 1572872 | tf_op jit(solution)/shard_map/ppermute | solution.py:313
  83.5 25.8 %collective-permute-start.5 = (bf16[128,2048]{1,0:T(8,128)(2,1)S(1)}, bf16[128,2048]{1,0:T(8,128)(2,1)S(1)}, u32[]{:S(2)}, u32[]{:S(2)}) collective-permute-start(bf16[128,2048]{1,0:T(8,128)(2,1)S(1)} %get-tuple-element.22), channel_id=1, source_target_pairs={{0,4},{1,5},{2,6},{3,7},{4,0},{5,1},{6,2},{7,3},{8,12},{9,13},{10,... | collective-permute-start | bytes 1572872 | tf_op jit(solution)/shard_map/ppermute | solution.py:313
  85.4 24.2 %collective-permute-start.6 = (bf16[128,2048]{1,0:T(8,128)(2,1)S(1)}, bf16[128,2048]{1,0:T(8,128)(2,1)S(1)}, u32[]{:S(2)}, u32[]{:S(2)}) collective-permute-start(bf16[128,2048]{1,0:T(8,128)(2,1)S(1)} %get-tuple-element.22), channel_id=1, source_target_pairs={{0,6},{1,7},{2,4},{3,5},{4,2},{5,3},{6,0},{7,1},{8,14},{9,15},{10,... | collective-permute-start | bytes 1572872 | tf_op jit(solution)/shard_map/ppermute | solution.py:313
  109.0 14.8 %collective-permute-start.18 = (bf16[128,2048]{1,0:T(8,128)(2,1)S(1)}, bf16[128,2048]{1,0:T(8,128)(2,1)S(1)}, u32[]{:S(2)}, u32[]{:S(2)}) collective-permute-start(bf16[128,2048]{1,0:T(8,128)(2,1)S(1)} %collective-permute-done.17), channel_id=1, source_target_pairs={{0,2},{1,3},{2,0},{3,1},{4,6},{5,7},{6,4},{7,5},{8,10},{9,11},{10,... | collective-permute-start | bytes 1572872 | tf_op jit(solution)/shard_map/ppermute | solution.py:313
  109.6 44.2 %collective-permute-start.7 = (bf16[512,2048]{1,0:T(8,128)(2,1)S(1)}, bf16[512,2048]{1,0:T(8,128)(2,1)}, u32[]{:S(2)}, u32[]{:S(2)}) collective-permute-start(bf16[512,2048]{1,0:T(8,128)(2,1)S(1)} %constant_dynamic-update-slice_fusion.refs_1_), channel_id=1, source_target_pairs={{0,1},{1,0},{2,3},{3,2},{4,5},{5,4},{6,7},{7,6},{8,9},{9,8},{10,11... | collective-permute-start | bytes 6291464 | tf_op jit(solution)/shard_map/ppermute | solution.py:313
  109.7 25.6 %collective-permute-start.19 = (bf16[128,2048]{1,0:T(8,128)(2,1)S(1)}, bf16[128,2048]{1,0:T(8,128)(2,1)S(1)}, u32[]{:S(2)}, u32[]{:S(2)}) collective-permute-start(bf16[128,2048]{1,0:T(8,128)(2,1)S(1)} %collective-permute-done.17), channel_id=1, source_target_pairs={{0,4},{1,5},{2,6},{3,7},{4,0},{5,1},{6,2},{7,3},{8,12},{9,13},{10,... | collective-permute-start | bytes 1572872 | tf_op jit(solution)/shard_map/ppermute | solution.py:313
  111.4 24.7 %collective-permute-start.20 = (bf16[128,2048]{1,0:T(8,128)(2,1)S(1)}, bf16[128,2048]{1,0:T(8,128)(2,1)S(1)}, u32[]{:S(2)}, u32[]{:S(2)}) collective-permute-start(bf16[128,2048]{1,0:T(8,128)(2,1)S(1)} %collective-permute-done.17), channel_id=1, source_target_pairs={{0,6},{1,7},{2,4},{3,5},{4,2},{5,3},{6,0},{7,1},{8,14},{9,15},{10,... | collective-permute-start | bytes 1572872 | tf_op jit(solution)/shard_map/ppermute | solution.py:313
  136.9 104.6 %collective-permute-start.21 = (bf16[512,2048]{1,0:T(8,128)(2,1)}, bf16[512,2048]{1,0:T(8,128)(2,1)}, u32[]{:S(2)}, u32[]{:S(2)}) collective-permute-start(bf16[512,2048]{1,0:T(8,128)(2,1)} %constant_dynamic-update-slice_fusion.11.refs_2_), channel_id=1, source_target_pairs={{0,1},{1,0},{2,3},{3,2},{4,5},{5,4},{6,7},{7,6},{8,9},{9,8},{10,11... | collective-permute-start | bytes 6291464 | tf_op jit(solution)/shard_map/ppermute | solution.py:313
  146.4 28.2 %collective-permute-start.8 = (bf16[512,1024]{1,0:T(8,128)(2,1)}, bf16[512,1024]{1,0:T(8,128)(2,1)}, u32[]{:S(2)}, u32[]{:S(2)}) collective-permute-start(bf16[512,1024]{1,0:T(8,128)(2,1)} %bitcast.55), channel_id=1, source_target_pairs={{0,8},{8,16},{16,24},{24,0},{1,9},{9,17},{17,25},{25,1},{2,10},{10... | collective-permute-start | bytes 3145736 | tf_op jit(solution)/shard_map/ppermute | solution.py:318
  150.1 46.4 %collective-permute-start.9 = (bf16[512,1024]{1,0:T(8,128)(2,1)}, bf16[512,1024]{1,0:T(8,128)(2,1)}, u32[]{:S(2)}, u32[]{:S(2)}) collective-permute-start(bf16[512,1024]{1,0:T(8,128)(2,1)} %bitcast.54), channel_id=1, source_target_pairs={{0,24},{8,0},{16,8},{24,16},{1,25},{9,1},{17,9},{25,17},{2,26},{10... | collective-permute-start | bytes 3145736 | tf_op jit(solution)/shard_map/ppermute | solution.py:318
  153.8 87.7 %collective-permute-start.16 = (bf16[512,1024]{1,0:T(8,128)(2,1)}, bf16[512,1024]{1,0:T(8,128)(2,1)}, u32[]{:S(2)}, u32[]{:S(2)}) collective-permute-start(bf16[512,1024]{1,0:T(8,128)(2,1)} %bitcast.53), channel_id=1, source_target_pairs={{0,16},{8,24},{16,0},{24,8},{1,17},{9,25},{17,1},{25,9},{2,18},{10... | collective-permute-start | bytes 3145736 | tf_op jit(solution)/shard_map/ppermute | solution.py:318
  174.6 73.3 %collective-permute-start = (f32[1,128]{1,0:T(1,128)S(1)}, f32[1,128]{1,0:T(1,128)S(1)}, u32[]{:S(2)}, u32[]{:S(2)}) collective-permute-start(f32[1,128]{1,0:T(1,128)S(1)} %bitcast.59), channel_id=1, source_target_pairs={{0,1},{1,0},{2,3},{3,2},{4,5},{5,4},{6,7},{7,6},{8,9},{9,8},{10,11... | collective-permute-start | bytes 1544 | tf_op jit(solution)/shard_map/ppermute | solution.py:313
  206.5 52.6 %copy-start = (f32[1,512,2048]{2,1,0:T(8,128)S(1)}, f32[1,512,2048]{2,1,0:T(8,128)}, u32[]{:S(2)}) copy-start(f32[1,512,2048]{2,1,0:T(8,128)} %param.12) | copy-start | bytes 12582916
  206.5 52.5 %copy-start.2 = (f32[1,512,2048]{2,1,0:T(8,128)S(1)}, f32[1,512,2048]{2,1,0:T(8,128)}, u32[]{:S(2)}) copy-start(f32[1,512,2048]{2,1,0:T(8,128)} %param.13) | copy-start | bytes 12582916
  247.8 13.1 %copy-start.4 = (f32[512,2048]{1,0:T(8,128)}, f32[512,2048]{1,0:T(8,128)S(1)}, u32[]{:S(2)}) copy-start(f32[512,2048]{1,0:T(8,128)S(1)} %get-tuple-element.27.refs_8_) | copy-start | bytes 12582916
  247.8 3.7 collective-permute-start.22
  247.9 6.7 %collective-permute-start.1 = (f32[1,128]{1,0:T(1,128)S(1)}, f32[1,128]{1,0:T(1,128)S(1)}, u32[]{:S(2)}, u32[]{:S(2)}) collective-permute-start(f32[1,128]{1,0:T(1,128)S(1)} %bitcast_add_fusion.refs_0_), channel_id=1, source_target_pairs={{0,2},{1,3},{2,0},{3,1},{4,6},{5,7},{6,4},{7,5},{8,10},{9,11},{10,... | collective-permute-start | bytes 1544 | tf_op jit(solution)/shard_map/ppermute | solution.py:313
  249.6 5.4 %collective-permute-start.2 = (f32[1,128]{1,0:T(1,128)S(1)}, f32[1,128]{1,0:T(1,128)S(1)}, u32[]{:S(2)}, u32[]{:S(2)}) collective-permute-start(f32[1,128]{1,0:T(1,128)S(1)} %bitcast_add_fusion.refs_0_), channel_id=1, source_target_pairs={{0,4},{1,5},{2,6},{3,7},{4,0},{5,1},{6,2},{7,3},{8,12},{9,13},{10,... | collective-permute-start | bytes 1544 | tf_op jit(solution)/shard_map/ppermute | solution.py:313
  251.1 4.5 %collective-permute-start.3 = (f32[1,128]{1,0:T(1,128)S(1)}, f32[1,128]{1,0:T(1,128)S(1)}, u32[]{:S(2)}, u32[]{:S(2)}) collective-permute-start(f32[1,128]{1,0:T(1,128)S(1)} %bitcast_add_fusion.refs_0_), channel_id=1, source_target_pairs={{0,6},{1,7},{2,4},{3,5},{4,2},{5,3},{6,0},{7,1},{8,14},{9,15},{10,... | collective-permute-start | bytes 1544 | tf_op jit(solution)/shard_map/ppermute | solution.py:313
  251.5 4.1 collective-permute-start.23
  253.1 3.6 collective-permute-start.24
  254.6 4.5 %collective-permute-start.25 = (f32[1,128]{1,0:T(1,128)S(1)}, f32[1,128]{1,0:T(1,128)S(1)}, u32[]{:S(2)}, u32[]{:S(2)}) collective-permute-start(f32[1,128]{1,0:T(1,128)S(1)} %add.80.refs_4_), channel_id=1, source_target_pairs={{0,6},{1,7},{2,4},{3,5},{4,2},{5,3},{6,0},{7,1},{8,14},{9,15},{10,... | collective-permute-start | bytes 1544 | tf_op jit(solution)/shard_map/ppermute | solution.py:313
  260.8 6.7 %copy-start.13 = (bf16[64,2048]{1,0:T(8,128)(2,1)}, bf16[64,2048]{1,0:T(8,128)(2,1)S(1)}, u32[]{:S(2)}) copy-start(bf16[64,2048]{1,0:T(8,128)(2,1)S(1)} %get-tuple-element.37) | copy-start | bytes 786436
  260.9 82.9 %copy-start.15 = (s32[1,1,16]{2,1,0:T(1,128)S(1)}, s32[1,1,16]{2,1,0:T(1,128)}, u32[]{:S(2)}) copy-start(s32[1,1,16]{2,1,0:T(1,128)} %param.16) | copy-start | bytes 196
  267.6 33.2 %collective-permute-start.28 = (bf16[384,2048]{1,0:T(8,128)(2,1)S(1)}, bf16[384,2048]{1,0:T(8,128)(2,1)S(1)}, u32[]{:S(2)}, u32[]{:S(2)}) collective-permute-start(bf16[384,2048]{1,0:T(8,128)(2,1)S(1)} %get-tuple-element.38), channel_id=1, source_target_pairs={{0,8},{8,16},{16,24},{1,9},{9,17},{17,25},{2,10},{10,18},{18,26},{... | collective-permute-start | bytes 4718600 | tf_op jit(solution)/shard_map/ppermute | solution.py:372
  269.0 37.6 %collective-permute-start.29 = (bf16[384,2048]{1,0:T(8,128)(2,1)S(1)}, bf16[384,2048]{1,0:T(8,128)(2,1)S(1)}, u32[]{:S(2)}, u32[]{:S(2)}) collective-permute-start(bf16[384,2048]{1,0:T(8,128)(2,1)S(1)} %get-tuple-element.38), channel_id=1, source_target_pairs={{8,0},{16,8},{24,16},{9,1},{17,9},{25,17},{10,2},{18,10},{26,18},{... | collective-permute-start | bytes 4718600 | tf_op jit(solution)/shard_map/ppermute | solution.py:373
  300.8 35.5 %collective-permute-start.34 = (bf16[384,2048]{1,0:T(8,128)(2,1)S(1)}, bf16[384,2048]{1,0:T(8,128)(2,1)S(1)}, u32[]{:S(2)}, u32[]{:S(2)}) collective-permute-start(bf16[384,2048]{1,0:T(8,128)(2,1)S(1)} %collective-permute-done.28.above_ref), channel_id=1, source_target_pairs={{0,8},{8,16},{16,24},{1,9},{9,17},{17,25},{2,10},{10,18},{18,26},{... | collective-permute-start | bytes 4718600 | tf_op jit(solution)/shard_map/ppermute | solution.py:372
  305.3 1.2 copy-start.7
  306.5 35.3 %collective-permute-start.35 = (bf16[384,2048]{1,0:T(8,128)(2,1)S(1)}, bf16[384,2048]{1,0:T(8,128)(2,1)S(1)}, u32[]{:S(2)}, u32[]{:S(2)}) collective-permute-start(bf16[384,2048]{1,0:T(8,128)(2,1)S(1)} %collective-permute-done.29.below_ref), channel_id=1, source_target_pairs={{8,0},{16,8},{24,16},{9,1},{17,9},{25,17},{10,2},{18,10},{26,18},{... | collective-permute-start | bytes 4718600 | tf_op jit(solution)/shard_map/ppermute | solution.py:373
  307.8 1.2 copy-start.9
  336.3 89.8 %collective-permute-start.40 = (bf16[384,2048]{1,0:T(8,128)(2,1)S(1)}, bf16[384,2048]{1,0:T(8,128)(2,1)}, u32[]{:S(2)}, u32[]{:S(2)}) collective-permute-start(bf16[384,2048]{1,0:T(8,128)(2,1)S(1)} %collective-permute-done.34.above_ref), channel_id=1, source_target_pairs={{0,8},{8,16},{16,24},{1,9},{9,17},{17,25},{2,10},{10,18},{18,26},{... | collective-permute-start | bytes 4718600 | tf_op jit(solution)/shard_map/ppermute | solution.py:372
  341.9 84.3 %collective-permute-start.41 = (bf16[384,2048]{1,0:T(8,128)(2,1)S(1)}, bf16[384,2048]{1,0:T(8,128)(2,1)}, u32[]{:S(2)}, u32[]{:S(2)}) collective-permute-start(bf16[384,2048]{1,0:T(8,128)(2,1)S(1)} %collective-permute-done.35.below_ref), channel_id=1, source_target_pairs={{8,0},{16,8},{24,16},{9,1},{17,9},{25,17},{10,2},{18,10},{26,18},{... | collective-permute-start | bytes 4718600 | tf_op jit(solution)/shard_map/ppermute | solution.py:373
  344.4 35.0 %collective-permute-start.26 = (bf16[64,2048]{1,0:T(8,128)(2,1)}, bf16[64,2048]{1,0:T(8,128)(2,1)S(1)}, u32[]{:S(2)}, u32[]{:S(2)}) collective-permute-start(bf16[64,2048]{1,0:T(8,128)(2,1)} %copy-done.13), channel_id=1, source_target_pairs={{0,8},{8,16},{16,24},{1,9},{9,17},{17,25},{2,10},{10,18},{18,26},{... | collective-permute-start | bytes 786440 | tf_op jit(solution)/shard_map/ppermute | solution.py:372
  349.0 32.9 %collective-permute-start.27 = (bf16[64,2048]{1,0:T(8,128)(2,1)}, bf16[64,2048]{1,0:T(8,128)(2,1)}, u32[]{:S(2)}, u32[]{:S(2)}) collective-permute-start(bf16[64,2048]{1,0:T(8,128)(2,1)} %copy-done.13), channel_id=1, source_target_pairs={{8,0},{16,8},{24,16},{9,1},{17,9},{25,17},{10,2},{18,10},{26,18},{... | collective-permute-start | bytes 786440 | tf_op jit(solution)/shard_map/ppermute | solution.py:373
  350.3 2.2 copy-start.1
  352.5 2.2 copy-start.3
  354.7 2.2 copy-start.5
  356.9 7.1 %copy-start.14 = (s32[1,1,8]{2,1,0:T(1,128)S(1)}, s32[1,1,8]{2,1,0:T(1,128)}, u32[]{:S(2)}) copy-start(s32[1,1,8]{2,1,0:T(1,128)} %param.17) | copy-start | bytes 100
  358.7 27.6 %collective-permute-start.30 = (bf16[64,2048]{1,0:T(8,128)(2,1)}, bf16[64,2048]{1,0:T(8,128)(2,1)}, u32[]{:S(2)}, u32[]{:S(2)}) collective-permute-start(bf16[64,2048]{1,0:T(8,128)(2,1)} %get-tuple-element.39), channel_id=1, source_target_pairs={{0,8},{8,16},{16,24},{1,9},{9,17},{17,25},{2,10},{10,18},{18,26},{... | collective-permute-start | bytes 786440 | tf_op jit(solution)/shard_map/ppermute | solution.py:372
  371.1 29.6 %all-to-all-start.1 = ((bf16[16,128,128]{2,1,0:T(8,128)(2,1)}), bf16[16,128,128]{2,1,0:T(8,128)(2,1)}, u32[]{:S(2)}, u32[]{:S(2)}) async-start(bf16[16,128,128]{2,1,0:T(8,128)(2,1)} %bitcast.56), calls=%async_computation.1 | async-start | bytes 1048576 | tf_op jit(solution)/shard_map/all_to_all | solution.py:385
  379.4 8.9 %collective-permute-start.31 = (bf16[64,2048]{1,0:T(8,128)(2,1)}, bf16[64,2048]{1,0:T(8,128)(2,1)}, u32[]{:S(2)}, u32[]{:S(2)}) collective-permute-start(bf16[64,2048]{1,0:T(8,128)(2,1)} %get-tuple-element.39), channel_id=1, source_target_pairs={{8,0},{16,8},{24,16},{9,1},{17,9},{25,17},{10,2},{18,10},{26,18},{... | collective-permute-start | bytes 786440 | tf_op jit(solution)/shard_map/ppermute | solution.py:373
  381.9 12.2 %collective-permute-start.32 = (bf16[64,2048]{1,0:T(8,128)(2,1)S(1)}, bf16[64,2048]{1,0:T(8,128)(2,1)}, u32[]{:S(2)}, u32[]{:S(2)}) collective-permute-start(bf16[64,2048]{1,0:T(8,128)(2,1)S(1)} %collective-permute-done.26.above_ref), channel_id=1, source_target_pairs={{0,8},{8,16},{16,24},{1,9},{9,17},{17,25},{2,10},{10,18},{18,26},{... | collective-permute-start | bytes 786440 | tf_op jit(solution)/shard_map/ppermute | solution.py:372
  386.4 9.1 %collective-permute-start.33 = (bf16[64,2048]{1,0:T(8,128)(2,1)}, bf16[64,2048]{1,0:T(8,128)(2,1)}, u32[]{:S(2)}, u32[]{:S(2)}) collective-permute-start(bf16[64,2048]{1,0:T(8,128)(2,1)} %collective-permute-done.27.below_ref), channel_id=1, source_target_pairs={{8,0},{16,8},{24,16},{9,1},{17,9},{25,17},{10,2},{18,10},{26,18},{... | collective-permute-start | bytes 786440 | tf_op jit(solution)/shard_map/ppermute | solution.py:373
  388.4 13.9 %collective-permute-start.36 = (bf16[64,2048]{1,0:T(8,128)(2,1)}, bf16[64,2048]{1,0:T(8,128)(2,1)}, u32[]{:S(2)}, u32[]{:S(2)}) collective-permute-start(bf16[64,2048]{1,0:T(8,128)(2,1)} %collective-permute-done.30.above_ref), channel_id=1, source_target_pairs={{0,8},{8,16},{16,24},{1,9},{9,17},{17,25},{2,10},{10,18},{18,26},{... | collective-permute-start | bytes 786440 | tf_op jit(solution)/shard_map/ppermute | solution.py:372
  394.1 9.4 %collective-permute-start.37 = (bf16[64,2048]{1,0:T(8,128)(2,1)}, bf16[64,2048]{1,0:T(8,128)(2,1)}, u32[]{:S(2)}, u32[]{:S(2)}) collective-permute-start(bf16[64,2048]{1,0:T(8,128)(2,1)} %collective-permute-done.31.below_ref), channel_id=1, source_target_pairs={{8,0},{16,8},{24,16},{9,1},{17,9},{25,17},{10,2},{18,10},{26,18},{... | collective-permute-start | bytes 786440 | tf_op jit(solution)/shard_map/ppermute | solution.py:373
  395.4 12.7 %collective-permute-start.38 = (bf16[64,2048]{1,0:T(8,128)(2,1)}, bf16[64,2048]{1,0:T(8,128)(2,1)}, u32[]{:S(2)}, u32[]{:S(2)}) collective-permute-start(bf16[64,2048]{1,0:T(8,128)(2,1)} %collective-permute-done.32.above_ref), channel_id=1, source_target_pairs={{0,8},{8,16},{16,24},{1,9},{9,17},{17,25},{2,10},{10,18},{18,26},{... | collective-permute-start | bytes 786440 | tf_op jit(solution)/shard_map/ppermute | solution.py:372
  402.3 22.5 %collective-permute-start.39 = (bf16[64,2048]{1,0:T(8,128)(2,1)}, bf16[64,2048]{1,0:T(8,128)(2,1)S(1)}, u32[]{:S(2)}, u32[]{:S(2)}) collective-permute-start(bf16[64,2048]{1,0:T(8,128)(2,1)} %collective-permute-done.33.below_ref), channel_id=1, source_target_pairs={{8,0},{16,8},{24,16},{9,1},{17,9},{25,17},{10,2},{18,10},{26,18},{... | collective-permute-start | bytes 786440 | tf_op jit(solution)/shard_map/ppermute | solution.py:373
  403.6 25.7 %collective-permute-start.42 = (bf16[64,2048]{1,0:T(8,128)(2,1)}, bf16[64,2048]{1,0:T(8,128)(2,1)S(1)}, u32[]{:S(2)}, u32[]{:S(2)}) collective-permute-start(bf16[64,2048]{1,0:T(8,128)(2,1)} %collective-permute-done.36.above_ref), channel_id=1, source_target_pairs={{0,8},{8,16},{16,24},{1,9},{9,17},{17,25},{2,10},{10,18},{18,26},{... | collective-permute-start | bytes 786440 | tf_op jit(solution)/shard_map/ppermute | solution.py:372
  408.1 21.2 %collective-permute-start.43 = (bf16[64,2048]{1,0:T(8,128)(2,1)}, bf16[64,2048]{1,0:T(8,128)(2,1)S(1)}, u32[]{:S(2)}, u32[]{:S(2)}) collective-permute-start(bf16[64,2048]{1,0:T(8,128)(2,1)} %collective-permute-done.37.below_ref), channel_id=1, source_target_pairs={{8,0},{16,8},{24,16},{9,1},{17,9},{25,17},{10,2},{18,10},{26,18},{... | collective-permute-start | bytes 786440 | tf_op jit(solution)/shard_map/ppermute | solution.py:373
  411.7 2.5 copy-start.8
  411.7 2.5 copy-start.10

commit v2 on v1

--- a/solution.py
+++ b/solution.py
@@ -12,7 +12,7 @@
 table_rate = 0.5
 table_decay = 0.2
 eps_norm = 1e-06
-weight_parts = (1, 6, 1)
+weight_parts = (2, 4, 2)
 lanes = 128
 mib = 1 << 20
 
@@ -61,9 +61,7 @@
             scratch_shapes=[pltpu.SemaphoreType.DMA((count,))],
         ),
         out_shape=[jax.ShapeDtypeStruct(shape, value.dtype)] * count,
-        compiler_params=pltpu.CompilerParams(
-            vmem_limit_bytes=4 * count * shape[0] * shape[1] + 2 * mib
-        ),
+        compiler_params=pltpu.CompilerParams(vmem_limit_bytes=56 * mib),
         cost_estimate=pl.CostEstimate(
             flops=0, bytes_accessed=4 * count * shape[0] * shape[1], transcendentals=0
         ),
@@ -71,21 +69,47 @@
     )(layer_owner, value)
 
 
-def accumulate(acc, inputs, near, far, last):
-    devices = lax.axis_size("dev")
-    half = devices // 2
-    count = len(inputs)
-    rows, tokens = inputs[0].shape
-    per_dev = tokens // devices
-    columns = near.shape[1]
+def pick_transposed(layer_owner, value, step):
+    groups = lax.axis_size("grp")
+    tokens, rows = value.shape[1:]
+    tile = min(tokens, 256)
+
+    def kernel(owner_ref, value_ref, out_ref):
+        out_ref[...] = value_ref[0].T
+
+    def source(i, owner_ref):
+        target = lax.rem(lax.axis_index("grp") + step, groups)
+        return layer_of(owner_ref, target), i, 0
+
+    return pl.pallas_call(
+        kernel,
+        grid_spec=pltpu.PrefetchScalarGridSpec(
+            num_scalar_prefetch=1,
+            grid=(tokens // tile,),
+            in_specs=[pl.BlockSpec((1, tile, rows), source)],
+            out_specs=pl.BlockSpec((rows, tile), lambda i, owner: (0, i)),
+        ),
+        out_shape=jax.ShapeDtypeStruct((rows, tokens), value.dtype),
+        compiler_params=pltpu.CompilerParams(vmem_limit_bytes=56 * mib),
+        cost_estimate=pl.CostEstimate(
+            flops=0, bytes_accessed=4 * rows * tokens, transcendentals=0
+        ),
+        name="pick_transposed",
+    )(layer_owner, value)
+
+
+def accumulate(acc, inputs, pieces, last):
+    rows, tokens = inputs.shape
+    per_dev, columns = pieces[0].shape
     tile = min(columns, 512)
     tiles = columns // tile
 
     def kernel(*refs):
         refs = list(refs)
         acc_ref = refs.pop(0) if acc is not None else None
-        x_refs = [refs.pop(0) for _ in range(count)]
-        near_ref, far_ref, out_ref = refs.pop(0), refs.pop(0), refs.pop(0)
+        x_ref = refs.pop(0)
+        piece_refs, refs = refs[: len(pieces)], refs[len(pieces) :]
+        out_ref = refs.pop(0)
         square_ref = refs.pop(0) if last else None
         x_all, g_all, x_sem, g_sem = refs
         column = pl.program_id(0)
@@ -93,28 +117,21 @@
 
         @pl.when(column == 0)
         def _():
-            for i in range(count):
-                pltpu.make_async_copy(x_refs[i], x_all.at[i], x_sem).start()
+            pltpu.make_async_copy(x_ref, x_all, x_sem).start()
             for t in range(tiles):
-                for side, ref in enumerate((near_ref, far_ref)):
-                    for place in range(half):
-                        owner = device ^ (2 * place + side)
-                        for i in range(count):
-                            pltpu.make_async_copy(
-                                ref.at[
-                                    pl.ds((place * count + i) * per_dev, per_dev),
-                                    pl.ds(t * tile, tile),
-                                ],
-                                g_all.at[t, i, pl.ds(pl.multiple_of(owner * per_dev, per_dev), per_dev)],
-                                g_sem.at[t],
-                            ).start()
+                for mask, ref in enumerate(piece_refs):
+                    first = pl.multiple_of((device ^ mask) * per_dev, per_dev)
+                    pltpu.make_async_copy(
+                        ref.at[:, pl.ds(t * tile, tile)],
+                        g_all.at[t, pl.ds(first, per_dev)],
+                        g_sem.at[t],
+                    ).start()
             pltpu.make_async_copy(x_all, x_all, x_sem).wait()
 
         pltpu.make_async_copy(g_all.at[column], g_all.at[column], g_sem.at[column]).wait()
-        total = acc_ref[...] if acc is not None else None
-        for i in range(count):
-            part = jnp.dot(x_all[i], g_all[column, i], preferred_element_type=jnp.float32)
-            total = part if total is None else total + part
+        total = jnp.dot(x_all[...], g_all[column], preferred_element_type=jnp.float32)
+        if acc is not None:
+            total = total + acc_ref[...]
         out_ref[...] = total
         if last:
             squares = jnp.sum(total * total, axis=0, keepdims=True)
@@ -129,7 +146,7 @@
                 square_ref[...] += folded
 
     block = pl.BlockSpec((rows, tile), lambda j: (0, j))
-    operands = ([acc] if acc is not None else []) + list(inputs) + [near, far]
+    operands = ([acc] if acc is not None else []) + [inputs, *pieces]
     out_shape = [jax.ShapeDtypeStruct((rows, columns), jnp.float32)]
     out_specs = [block]
     if last:
@@ -138,21 +155,21 @@
     result = pl.pallas_call(
         kernel,
         grid=(tiles,),
-        in_specs=([block] if acc is not None else []) + [anywhere] * (count + 2),
+        in_specs=([block] if acc is not None else []) + [anywhere] * (1 + len(pieces)),
         out_specs=out_specs,
         out_shape=out_shape,
         scratch_shapes=[
-            pltpu.VMEM((count, rows, tokens), jnp.bfloat16),
-            pltpu.VMEM((tiles, count, tokens, tile), jnp.bfloat16),
+            pltpu.VMEM((rows, tokens), jnp.bfloat16),
+            pltpu.VMEM((tiles, tokens, tile), jnp.bfloat16),
             pltpu.SemaphoreType.DMA,
             pltpu.SemaphoreType.DMA((tiles,)),
         ],
         compiler_params=pltpu.CompilerParams(
-            vmem_limit_bytes=2 * count * tokens * (rows + columns) + 16 * rows * tile + 2 * mib
+            vmem_limit_bytes=2 * tokens * (rows + columns) + 16 * rows * tile + 2 * mib
         ),
         cost_estimate=pl.CostEstimate(
-            flops=2 * count * rows * tokens * columns,
-            bytes_accessed=2 * count * tokens * (rows + columns) + 8 * rows * columns,
+            flops=2 * rows * tokens * columns,
+            bytes_accessed=2 * tokens * (rows + columns) + 8 * rows * columns,
             transcendentals=0,
         ),
         name="accumulate",
@@ -227,70 +244,101 @@
     )(*operands, *buffers)
 
 
-def place(layer_owner, weights, above, below, step, chunk):
-    groups = lax.axis_size("grp")
-    columns = above.shape[1]
+def exchanges(groups):
+    matchings = [
+        [(i, i + 1) for i in range(first, groups - 1, 2)] for first in (0, 1)
+    ]
+    held = [list(range(groups)) for _ in range(2)]
+    seen = [{group} for group in range(groups)]
+    swaps = []
+    for step in range(groups):
+        for chain in (step % 2, 1 - step % 2):
+            pairs = matchings[(step + chain) % 2]
+            pairs = pairs + [(j, i) for i, j in pairs]
+            got = [None] * groups
+            for i, j in pairs:
+                got[j] = held[chain][i]
+            held[chain] = got
+            new = [
+                source if source is not None and source not in seen[group] else None
+                for group, source in enumerate(got)
+            ]
+            if any(source is not None for source in new):
+                swaps.append((step, chain, pairs, new))
+            for group, source in enumerate(new):
+                seen[group].add(group if source is None else source)
+    if any(len(groups_seen) < groups for groups_seen in seen):
+        raise ValueError("incomplete exchange")
+    batches = []
+    for number, (*_, new) in enumerate(swaps):
+        for batch in batches:
+            if all(
+                source is None or all(swaps[other][3][group] is None for other in batch)
+                for group, source in enumerate(new)
+            ):
+                batch.append(number)
+                break
+        else:
+            batches.append([number])
+    return swaps, sorted(batches, key=lambda batch: batch[-1])
+
+
+def place(layer_owner, weights, pieces, sources, chunk):
+    columns = pieces[0].shape[1]
     start, height = chunk
-
-    def kernel(owner_ref, weights_ref, above_ref, below_ref, out_ref, held, in_sem, out_sem):
+    count = len(pieces)
+
+    def kernel(owner_ref, weights_ref, *refs):
+        piece_refs = refs[:count]
+        out_ref, held, in_sem, out_sem = refs[count:]
         group = lax.axis_index("grp")
-        sides = (
-            (above_ref, group - step, group >= step),
-            (below_ref, group + step, group + step < groups),
-        )
-        for side, (ref, source, valid) in enumerate(sides):
-
-            @pl.when(valid)
+
+        def select(values):
+            return sum(jnp.where(group == i, value, 0) for i, value in enumerate(values))
+
+        for ref, some in zip(piece_refs, sources):
+
+            @pl.when(select([int(source is not None) for source in some]) > 0)
             def _():
-                pltpu.make_async_copy(ref, held.at[side], in_sem.at[side]).start()
-
-        for side, (ref, source, valid) in enumerate(sides):
-
-            @pl.when(valid)
-            def _():
-                pltpu.make_async_copy(ref, held.at[side], in_sem.at[side]).wait()
+                source = select([0 if source is None else source for source in some])
+                inward = pltpu.make_async_copy(ref, held, in_sem)
+                inward.start()
+                inward.wait()
                 layer = layer_of(owner_ref, source)
-                copy = pltpu.make_async_copy(
-                    held.at[side], out_ref.at[layer, pl.ds(start, height)], out_sem.at[side]
+                outward = pltpu.make_async_copy(
+                    held, out_ref.at[layer, pl.ds(start, height)], out_sem
                 )
-                copy.start()
-
-        for side, (ref, source, valid) in enumerate(sides):
-
-            @pl.when(valid)
-            def _():
-                pltpu.make_async_copy(
-                    held.at[side], out_ref.at[0, pl.ds(start, height)], out_sem.at[side]
-                ).wait()
+                outward.start()
+                outward.wait()
 
     return pl.pallas_call(
         kernel,
         grid_spec=pltpu.PrefetchScalarGridSpec(
             num_scalar_prefetch=1,
             grid=(1,),
-            in_specs=[anywhere] * 3,
+            in_specs=[anywhere] * (1 + count),
             out_specs=anywhere,
             scratch_shapes=[
-                pltpu.VMEM((2, height, columns), jnp.bfloat16),
-                pltpu.SemaphoreType.DMA((2,)),
-                pltpu.SemaphoreType.DMA((2,)),
+                pltpu.VMEM((height, columns), jnp.bfloat16),
+                pltpu.SemaphoreType.DMA,
+                pltpu.SemaphoreType.DMA,
             ],
         ),
         out_shape=jax.ShapeDtypeStruct(weights.shape, weights.dtype),
         input_output_aliases={1: 0},
-        compiler_params=pltpu.CompilerParams(vmem_limit_bytes=4 * height * columns + 2 * mib),
+        compiler_params=pltpu.CompilerParams(vmem_limit_bytes=2 * height * columns + 2 * mib),
         cost_estimate=pl.CostEstimate(
-            flops=0, bytes_accessed=8 * height * columns, transcendentals=0
+            flops=0, bytes_accessed=4 * height * columns, transcendentals=0
         ),
         name="place",
-    )(layer_owner, weights, above, below)
-
-
-def rounds_of(groups):
-    rounds = [[0]]
+    )(layer_owner, weights, *pieces)
+
+
+def shifts_of(groups):
+    shifts = [0]
     for step in range(1, groups // 2 + 1):
-        rounds.append([step] if 2 * step == groups else [step, groups - step])
-    return rounds
+        shifts += [step] if 2 * step == groups else [step, groups - step]
+    return shifts
 
 
 def local(
@@ -306,7 +354,6 @@
 ):
     groups = lax.axis_size("grp")
     devices = lax.axis_size("dev")
-    group = lax.axis_index("grp")
     masks = range(2, devices, 2)
 
     def swap(value, mask):
@@ -325,53 +372,52 @@
     moment = momentum[0]
     rows, columns = master.shape
 
-    rounds = rounds_of(groups)
-    steps = [step for some in rounds for step in some]
-
-    layers = jnp.arange(groups, dtype=jnp.int32)
-
-    def owned(value, step):
-        target = (group + step) % groups
-        layer = jnp.sum(jnp.where(layer_owner == target, layers, 0)).astype(jnp.uint32)
-        return lax.dynamic_index_in_dim(value, layer, 0, keepdims=False)
-
-    g_own = dict(zip(steps, pick(layer_owner, output_grads, steps)))
+    shifts = shifts_of(groups)
+    g_own = dict(zip(shifts, pick(layer_owner, output_grads, shifts)))
+    x_own = {}
+    for step in shifts:
+        x_own[step] = pick_transposed(layer_owner, layer_inputs, step)
+    g_own = {step: shift(g_own[step], step) for step in shifts}
+    x_own = {step: shift(x_own[step], step) for step in shifts}
     new_table = update_table(table_blocks[0], block_grads[0, 0], block_ids[0, 0], block_counts[0, 0])
-    g_own = {step: shift(g_own[step], step) for step in steps}
-    x_own = {step: shift(owned(layer_inputs, step).T, step) for step in steps}
 
     squares = jnp.sum(master * master, axis=0, keepdims=True)
     squares = jnp.sum(squares.reshape(columns // lanes, lanes), axis=0, keepdims=True)
     weight_squares = dev_parts(squares)
 
     grad = None
-    for some in rounds:
-        pieces = [g_own[step] for step in some]
-        piece = jnp.concatenate(pieces, axis=0) if len(some) > 1 else pieces[0]
-        near = jnp.concatenate([piece] + [swap(piece, mask) for mask in masks], axis=0)
-        far = swap(near, 1)
-        inputs = [x_own[step] for step in some]
-        last = some is rounds[-1]
-        grad = accumulate(grad, inputs, near, far, last)
+    for step in shifts:
+        pieces = [None] * devices
+        for mask in range(0, devices, 2):
+            pieces[mask] = swap(g_own[step], mask) if mask else g_own[step]
+            pieces[mask + 1] = swap(pieces[mask], 1)
+        grad = accumulate(grad, x_own[step], pieces, step == shifts[-1])
     grad, squares = grad
     grad_squares = dev_parts(squares)
 
-    up = [(i, i + 1) for i in range(groups - 1)]
-    down = [(i + 1, i) for i in range(groups - 1)]
     chunks = chunks_of(rows)
-    buffers, above, below = [], [], []
+    swaps, batches = exchanges(groups)
+    buffers, held = [], []
     for chunk in chunks:
         piece, *buffers = update(
             layer_owner, weight_squares, grad_squares, grad, master, moment, chunk, buffers
         )
-        above.append(piece)
-        below.append(piece)
+        held.append([piece, piece])
     new_weights, new_master, new_moment = buffers
-    for step in range(1, groups):
+    pieces = {}
+    for number, (_, chain, pairs, _) in enumerate(swaps):
+        for chunk in range(len(chunks)):
+            piece = lax.ppermute(held[chunk][chain], "grp", pairs)
+            pieces[number, chunk] = held[chunk][chain] = piece
+    for batch in batches:
         for number, chunk in enumerate(chunks):
-            above[number] = lax.ppermute(above[number], "grp", up)
-            below[number] = lax.ppermute(below[number], "grp", down)
-            new_weights = place(layer_owner, new_weights, above[number], below[number], step, chunk)
+            new_weights = place(
+                layer_owner,
+                new_weights,
+                [pieces[step, number] for step in batch],
+                [swaps[step][3] for step in batch],
+                chunk,
+            )
     return (new_master[None], new_moment[None], new_weights, new_table[None])
 
 

time: 432 us -> 399 us (0.924)
  waiting for transfers between devices: 243 us -> 178 us
  starting transfers between devices: 84.6 us -> 123 us
  local copies, waits for them, and re-layouts: 32.5 us -> 10.4 us
  Pallas kernels: 50.5 us -> 71.3 us
    ppermute x6, waiting for transfers between devices: 113 us -> 26.6 us  [shift(): lax.ppermute(value, 'grp', [(i, (i + step) % groups) for i in range(group...]
    ppermute x6, starting transfers between devices: 10.1 us -> 41.3 us  [shift(): lax.ppermute(value, 'grp', [(i, (i + step) % groups) for i in range(group...]
    pallas_call x0 -> x4, Pallas kernels: none -> 17 us  [pick_transposed(): pl.pallas_call(kernel, grid_spec=pltpu.PrefetchScalarGridSpec(num_scalar_...]
    ppermute x18 -> x15, waiting for transfers between devices: 61.9 us -> 78.6 us  [local(): piece = lax.ppermute(held[chunk][chain], 'grp', pairs)]
    dynamic_slice x5 -> x0, local copies, waits for them, and re-layouts: 11.2 us -> none  [owned(): return lax.dynamic_index_in_dim(value, layer, 0, keepdims=False)]
    unnamed x43 -> x76, local copies, waits for them, and re-layouts: 18.3 us -> 10.2 us
    ppermute x20 -> x36, starting transfers between devices: 17.5 us -> 24.6 us  [swap(): return lax.ppermute(value, 'dev', [(i, i ^ mask) for i in range(devices)])]
    ppermute x20 -> x36, waiting for transfers between devices: 68.8 us -> 72.7 us  [swap(): return lax.ppermute(value, 'dev', [(i, i ^ mask) for i in range(devices)])]
  transfers between devices with their start and end apart: 45 -> 58, of which waited for: 19 -> 21; matrix products, arithmetic and copies ran while one was open for 7% -> 2% of each run, Pallas kernels for 9% -> 14%
where the time goes in v2:
time: 399 us; the launch traced here: 397 us
  waiting for transfers between devices  178 us (45%)
  starting transfers between devices  123 us (31%)
  Pallas kernels  71.3 us (18%)
  local copies, waits for them, and re-layouts  10.4 us (3%)
  blocking collectives  7.77 us (2%)
  other arithmetic  4.63 us (1%)
    ppermute x15, waiting for transfers between devices, local(): piece = lax.ppermute(held[chunk][chain], 'grp', pairs)  78.6 us
    ppermute x36, waiting for transfers between devices, swap(): return lax.ppermute(value, 'dev', [(i, i ^ mask) for i in range(devices)])  72.7 us
    ppermute x15, starting transfers between devices, local(): piece = lax.ppermute(held[chunk][chain], 'grp', pairs)  52.7 us
    ppermute x6, starting transfers between devices, shift(): lax.ppermute(value, 'grp', [(i, (i + step) % groups) for i in range(group...  41.3 us
    ppermute x6, waiting for transfers between devices, shift(): lax.ppermute(value, 'grp', [(i, (i + step) % groups) for i in range(group...  26.6 us
    ppermute x36, starting transfers between devices, swap(): return lax.ppermute(value, 'dev', [(i, i ^ mask) for i in range(devices)])  24.6 us
    pallas_call x9, Pallas kernels, place(): pl.pallas_call(kernel, grid_spec=pltpu.PrefetchScalarGridSpec(num_scalar_...  21.7 us
    pallas_call x4, Pallas kernels, accumulate(): pl.pallas_call(kernel, grid=(tiles,), in_specs=([block] if acc is not Non...  18.3 us
  transfers between devices with their start and end apart: 58, of which 21 were waited for; matrix products, arithmetic and copies ran while one was open for 2% of the time, Pallas kernels for 14%

profile of v2, /device:TPU:0, one launch (start us, length us, event | category | flops | bytes accessed | tf_op | source)
XLA Modules:
  0.0 397.5 jit_solution(16810563936114624130)
XLA Ops:
  0.6 3.5 pick.1
  4.2 4.0 %collective-permute-start.9 = (bf16[128,2048]{1,0:T(8,128)(2,1)}, bf16[128,2048]{1,0:T(8,128)(2,1)S(1)}, u32[]{:S(2)}, u32[]{:S(2)}) collective-permute-start(bf16[128,2048]{1,0:T(8,128)(2,1)} %get-tuple-element.22.refs_1_), channel_id=1, source_target_pairs={{0,6},{1,7},{2,4},{3,5},{4,2},{5,3},{6,0},{7,1},{8,14},{9,15},{10,... | collective-permute-start | bytes 1572872 | tf_op jit(solution)/shard_map/ppermute | solution.py:360
  8.8 2.0 collective-permute-start.12
  10.8 10.4 %collective-permute-done.9.refs_7_ = bf16[128,2048]{1,0:T(8,128)(2,1)S(1)} collective-permute-done((bf16[128,2048]{1,0:T(8,128)(2,1)}, bf16[128,2048]{1,0:T(8,128)(2,1)S(1)}, u32[]{:S(2)}, u32[]{:S(2)}) %collective-permute-start.9) | collective-permute-done | bytes 524320 | tf_op jit(solution)/shard_map/ppermute | solution.py:360
  21.2 4.1 %collective-permute-start.21 = (bf16[128,2048]{1,0:T(8,128)(2,1)}, bf16[128,2048]{1,0:T(8,128)(2,1)S(1)}, u32[]{:S(2)}, u32[]{:S(2)}) collective-permute-start(bf16[128,2048]{1,0:T(8,128)(2,1)} %get-tuple-element.24), channel_id=1, source_target_pairs={{0,24},{8,0},{16,8},{24,16},{1,25},{9,1},{17,9},{25,17},{2,26},{10... | collective-permute-start | bytes 1572872 | tf_op jit(solution)/shard_map/ppermute | solution.py:365
  25.3 6.6 %collective-permute-done.5.refs_3_ = bf16[128,2048]{1,0:T(8,128)(2,1)S(1)} collective-permute-done((bf16[128,2048]{1,0:T(8,128)(2,1)}, bf16[128,2048]{1,0:T(8,128)(2,1)S(1)}, u32[]{:S(2)}, u32[]{:S(2)}) %collective-permute-start.5) | collective-permute-done | bytes 524320 | tf_op jit(solution)/shard_map/ppermute | solution.py:360
  31.8 2.6 collective-permute-start.30
  35.0 4.3 %pick_transposed.5 = bf16[512,1024]{1,0:T(8,128)(2,1)} custom-call(s32[4]{0:T(128)} %owner_ref.33, bf16[4,1024,512]{2,1,0:T(8,128)(2,1)} %value_ref.9), custom_call_target="tpu_custom_call" | custom-call | bytes 2097152 | tf_op jit(solution)/shard_map/pick_transposed/pallas_call | solution.py:84
  39.3 32.7 %collective-permute-start.11 = (bf16[512,1024]{1,0:T(8,128)(2,1)}, bf16[512,1024]{1,0:T(8,128)(2,1)S(1)}, u32[]{:S(2)}, u32[]{:S(2)}) collective-permute-start(bf16[512,1024]{1,0:T(8,128)(2,1)} %pick_transposed.5), channel_id=1, source_target_pairs={{0,8},{8,16},{16,24},{24,0},{1,9},{9,17},{17,25},{25,1},{2,10},{10... | collective-permute-start | bytes 3145736 | tf_op jit(solution)/shard_map/ppermute | solution.py:365
  72.0 9.8 %collective-permute-done.30.refs_2_ = bf16[128,2048]{1,0:T(8,128)(2,1)S(1)} collective-permute-done((bf16[128,2048]{1,0:T(8,128)(2,1)}, bf16[128,2048]{1,0:T(8,128)(2,1)S(1)}, u32[]{:S(2)}, u32[]{:S(2)}) %collective-permute-start.30) | collective-permute-done | bytes 524320 | tf_op jit(solution)/shard_map/ppermute | solution.py:365
  81.8 1.5 collective-permute-start.14
  84.1 1.5 collective-permute-start.16
  87.7 4.3 %pick_transposed.6 = bf16[512,1024]{1,0:T(8,128)(2,1)} custom-call(s32[4]{0:T(128)} %owner_ref.33, bf16[4,1024,512]{2,1,0:T(8,128)(2,1)} %value_ref.9), custom_call_target="tpu_custom_call" | custom-call | bytes 2097152 | tf_op jit(solution)/shard_map/pick_transposed/pallas_call | solution.py:84
  92.0 4.7 %collective-permute-done.14.refs_4_ = bf16[128,2048]{1,0:T(8,128)(2,1)} collective-permute-done((bf16[128,2048]{1,0:T(8,128)(2,1)S(1)}, bf16[128,2048]{1,0:T(8,128)(2,1)}, u32[]{:S(2)}, u32[]{:S(2)}) %collective-permute-start.14) | collective-permute-done | bytes 524320 | tf_op jit(solution)/shard_map/ppermute | solution.py:360
  96.7 11.1 %collective-permute-done.16.refs_6_ = bf16[128,2048]{1,0:T(8,128)(2,1)} collective-permute-done((bf16[128,2048]{1,0:T(8,128)(2,1)S(1)}, bf16[128,2048]{1,0:T(8,128)(2,1)}, u32[]{:S(2)}, u32[]{:S(2)}) %collective-permute-start.16) | collective-permute-done | bytes 524320 | tf_op jit(solution)/shard_map/ppermute | solution.py:360
  108.9 1.5 collective-permute-start.25
  110.4 1.5 collective-permute-start.27
  112.8 10.0 %collective-permute-done.23.refs_4_ = bf16[128,2048]{1,0:T(8,128)(2,1)} collective-permute-done((bf16[128,2048]{1,0:T(8,128)(2,1)S(1)}, bf16[128,2048]{1,0:T(8,128)(2,1)}, u32[]{:S(2)}, u32[]{:S(2)}) %collective-permute-start.23) | collective-permute-done | bytes 524320 | tf_op jit(solution)/shard_map/ppermute | solution.py:360
  122.7 8.8 %collective-permute-done.25.refs_6_ = bf16[128,2048]{1,0:T(8,128)(2,1)} collective-permute-done((bf16[128,2048]{1,0:T(8,128)(2,1)S(1)}, bf16[128,2048]{1,0:T(8,128)(2,1)}, u32[]{:S(2)}, u32[]{:S(2)}) %collective-permute-start.25) | collective-permute-done | bytes 524320 | tf_op jit(solution)/shard_map/ppermute | solution.py:360
  131.5 3.1 collective-permute-start.34
  134.6 1.5 collective-permute-done.27.refs_8_
  137.4 7.7 %collective-permute-done.32.refs_4_ = bf16[128,2048]{1,0:T(8,128)(2,1)S(1)} collective-permute-done((bf16[128,2048]{1,0:T(8,128)(2,1)S(1)}, bf16[128,2048]{1,0:T(8,128)(2,1)S(1)}, u32[]{:S(2)}, u32[]{:S(2)}) %collective-permute-start.32) | collective-permute-done | bytes 524320 | tf_op jit(solution)/shard_map/ppermute | solution.py:360
  145.1 8.4 %collective-permute-done.34.refs_6_ = bf16[128,2048]{1,0:T(8,128)(2,1)S(1)} collective-permute-done((bf16[128,2048]{1,0:T(8,128)(2,1)S(1)}, bf16[128,2048]{1,0:T(8,128)(2,1)S(1)}, u32[]{:S(2)}, u32[]{:S(2)}) %collective-permute-start.34) | collective-permute-done | bytes 524320 | tf_op jit(solution)/shard_map/ppermute | solution.py:360
  155.6 4.3 %pick_transposed.7 = bf16[512,1024]{1,0:T(8,128)(2,1)} custom-call(s32[4]{0:T(128)} %owner_ref.33, bf16[4,1024,512]{2,1,0:T(8,128)(2,1)} %value_ref.9), custom_call_target="tpu_custom_call" | custom-call | bytes 2097152 | tf_op jit(solution)/shard_map/pick_transposed/pallas_call | solution.py:84
  160.7 4.3 %pick_transposed.4.refs_0_ = bf16[512,1024]{1,0:T(8,128)(2,1)} custom-call(s32[4]{0:T(128)} %owner_ref.33, bf16[4,1024,512]{2,1,0:T(8,128)(2,1)} %value_ref.9), custom_call_target="tpu_custom_call" | custom-call | bytes 2097152 | tf_op jit(solution)/shard_map/pick_transposed/pallas_call | solution.py:84
  169.2 3.9 accumulate.4.refs_0_
  173.2 4.9 %accumulate.5.refs_0_ = f32[512,2048]{1,0:T(8,128)S(1)} custom-call(f32[512,2048]{1,0:T(8,128)S(1)} %accumulate.4.refs_0_, bf16[512,1024]{1,0:T(8,128)(2,1)S(1)} %collective-permute-done.11.refs_1_, bf16[128,2048]{1,0:T(8,128)(2,1)S(1)} %copy-done.27, bf16[128,2048]{1,0:T(8,128)(2,1)} %collective-permute-done.13.refs_3_, ...), custom_call_target="tpu_custom_call" | custom-call | flops 2147483648 | bytes 13631488 | tf_op jit(solution)/shard_map/accumulate/pallas_call | solution.py:155
  178.2 5.1 %accumulate.6.refs_0_ = f32[512,2048]{1,0:T(8,128)S(1)} custom-call(f32[512,2048]{1,0:T(8,128)S(1)} %accumulate.5.refs_0_, bf16[512,1024]{1,0:T(8,128)(2,1)S(1)} %collective-permute-done.20.refs_1_, bf16[128,2048]{1,0:T(8,128)(2,1)S(1)} %copy-done.25, bf16[128,2048]{1,0:T(8,128)(2,1)S(1)} %copy-done.29, bf16[128,2048]{1,0:T(8,128)(2,1)} %collective-permute-done.23.refs_4_, ...), custom_call_target="tpu_custom_call" | custom-call | flops 2147483648 | bytes 13631488 | tf_op jit(solution)/shard_map/accumulate/pallas_call | solution.py:155
  183.5 16.8 %collective-permute-done.29.refs_1_ = bf16[512,1024]{1,0:T(8,128)(2,1)S(1)} collective-permute-done((bf16[512,1024]{1,0:T(8,128)(2,1)}, bf16[512,1024]{1,0:T(8,128)(2,1)S(1)}, u32[]{:S(2)}, u32[]{:S(2)}) %collective-permute-start.29) | collective-permute-done | bytes 1048608 | tf_op jit(solution)/shard_map/ppermute | solution.py:365
  200.3 4.4 %accumulate.7 = (f32[512,2048]{1,0:T(8,128)S(1)}, f32[1,128]{1,0:T(1,128)S(1)}) custom-call(f32[512,2048]{1,0:T(8,128)S(1)} %accumulate.6.refs_0_, bf16[512,1024]{1,0:T(8,128)(2,1)S(1)} %collective-permute-done.29.refs_1_, bf16[128,2048]{1,0:T(8,128)(2,1)S(1)} %collective-permute-done.30.refs_2_, bf16[128,2048]{1,0:T(8,128)(2,1)S(1)} %collective-permute-done.31.refs_3_, ...), custom_call_target="tpu_custom_call" | custom-call | flops 2147483648 | bytes 13631488 | tf_op jit(solution)/shard_map/accumulate/pallas_call | solution.py:155
  206.4 2.0 collective-permute-start.3
  209.9 2.0 collective-permute-start.41
  212.2 2.2 collective-permute-done.41.refs_7_
  214.3 2.9 update.3
  217.2 4.9 %update.4 = (bf16[256,2048]{1,0:T(8,128)(2,1)}, bf16[4,512,2048]{2,1,0:T(8,128)(2,1)}, f32[512,2048]{1,0:T(8,128)}, f32[512,2048]{1,0:T(8,128)}) custom-call(s32[4]{0:T(128)S(1)} %copy-done.34, f32[1,128]{1,0:T(1,128)S(1)} %bitcast_add_fusion.refs_0_, ...), custom_call_target="tpu_custom_call", output_to_operand_aliasing={{1}: (12, {}), {2}: (13, {}), {3}: (14, {})} | custom-call | flops 4194304 | bytes 12582912 | tf_op jit(solution)/shard_map/update/pallas_call | solution.py:216
  222.1 2.0 collective-permute-start.42
  224.9 23.5 %collective-permute-done.43.refs_0_ = bf16[256,2048]{1,0:T(8,128)(2,1)S(1)} collective-permute-done((bf16[256,2048]{1,0:T(8,128)(2,1)}, bf16[256,2048]{1,0:T(8,128)(2,1)S(1)}, u32[]{:S(2)}, u32[]{:S(2)}) %collective-permute-start.43) | collective-permute-done | bytes 1048608 | tf_op jit(solution)/shard_map/ppermute | solution.py:410
  249.1 1.5 collective-permute-start.45
  250.6 2.9 update.5
  253.5 3.7 collective-permute-start.44
  257.2 2.6 collective-permute-done.42.refs_0_
  259.7 1.5 collective-permute-start.49
  262.6 25.1 %collective-permute-start.46 = (bf16[128,2048]{1,0:T(8,128)(2,1)}, bf16[128,2048]{1,0:T(8,128)(2,1)}, u32[]{:S(2)}, u32[]{:S(2)}) collective-permute-start(bf16[128,2048]{1,0:T(8,128)(2,1)} %collective-permute-done.45.refs_0_), channel_id=1, source_target_pairs={{0,8},{16,24},{8,0},{24,16},{1,9},{17,25},{9,1},{25,17},{2,10},{18... | collective-permute-start | bytes 1572872 | tf_op jit(solution)/shard_map/ppermute | solution.py:410
  287.6 1.5 collective-permute-start.51
  289.1 1.5 collective-permute-start.55
  290.7 7.8 %all_to_all.11 = s32[8,2,1]{1,2,0:T(1,128)S(1)} all-to-all(s32[8,2,1]{1,2,0:T(1,128)S(1)} %bitcast.41), channel_id=1, replica_groups=mesh['grp'=4,'dev'=8] {'dev'}, dimensions={0} | all-to-all | bytes 128 | tf_op jit(solution)/shard_map/all_to_all | solution.py:430
  298.4 4.1 %all-to-all-start.1 = ((bf16[16,128,128]{2,1,0:T(8,128)(2,1)}), bf16[16,128,128]{2,1,0:T(8,128)(2,1)}, u32[]{:S(2)}, u32[]{:S(2)}) async-start(bf16[16,128,128]{2,1,0:T(8,128)(2,1)} %bitcast.40), calls=%async_computation.1 | async-start | bytes 1048576 | tf_op jit(solution)/shard_map/all_to_all | solution.py:431
  304.6 10.5 %collective-permute-start.48 = (bf16[256,2048]{1,0:T(8,128)(2,1)S(1)}, bf16[256,2048]{1,0:T(8,128)(2,1)}, u32[]{:S(2)}, u32[]{:S(2)}) collective-permute-start(bf16[256,2048]{1,0:T(8,128)(2,1)S(1)} %collective-permute-done.47.refs_0_), channel_id=1, source_target_pairs={{0,8},{16,24},{8,0},{24,16},{1,9},{17,25},{9,1},{25,17},{2,10},{18... | collective-permute-start | bytes 3145736 | tf_op jit(solution)/shard_map/ppermute | solution.py:410
  315.3 2.0 collective-permute-start.50
  317.4 1.9 collective-permute-start.56
  319.3 1.6 multiply_reduce_fusion.1
  323.2 2.4 place.9.weights_ref
  325.6 1.6 place.10.weights_ref
  327.2 2.4 place.11.weights_ref
  329.6 2.4 place.12.weights_ref
  332.1 7.1 %collective-permute-done.48.refs_1_ = bf16[256,2048]{1,0:T(8,128)(2,1)} collective-permute-done((bf16[256,2048]{1,0:T(8,128)(2,1)S(1)}, bf16[256,2048]{1,0:T(8,128)(2,1)}, u32[]{:S(2)}, u32[]{:S(2)}) %collective-permute-start.48) | collective-permute-done | bytes 1048608 | tf_op jit(solution)/shard_map/ppermute | solution.py:410
  339.2 2.8 place.13.weights_ref
  341.9 30.9 %collective-permute-done.50.refs_1_ = bf16[128,2048]{1,0:T(8,128)(2,1)} collective-permute-done((bf16[128,2048]{1,0:T(8,128)(2,1)}, bf16[128,2048]{1,0:T(8,128)(2,1)}, u32[]{:S(2)}, u32[]{:S(2)}) %collective-permute-start.50) | collective-permute-done | bytes 524320 | tf_op jit(solution)/shard_map/ppermute | solution.py:410
  372.9 2.4 place.14.weights_ref
  375.3 8.8 %collective-permute-done.52.refs_1_ = bf16[128,2048]{1,0:T(8,128)(2,1)} collective-permute-done((bf16[128,2048]{1,0:T(8,128)(2,1)}, bf16[128,2048]{1,0:T(8,128)(2,1)}, u32[]{:S(2)}, u32[]{:S(2)}) %collective-permute-start.52) | collective-permute-done | bytes 524320 | tf_op jit(solution)/shard_map/ppermute | solution.py:410
  384.1 2.4 place.15.weights_ref
  386.5 2.8 place.16.weights_ref
  389.3 5.7 %collective-permute-done.56.refs_1_ = bf16[128,2048]{1,0:T(8,128)(2,1)} collective-permute-done((bf16[128,2048]{1,0:T(8,128)(2,1)}, bf16[128,2048]{1,0:T(8,128)(2,1)}, u32[]{:S(2)}, u32[]{:S(2)}) %collective-permute-start.56) | collective-permute-done | bytes 524320 | tf_op jit(solution)/shard_map/ppermute | solution.py:410
  395.0 2.4 place.17
  (165 shorter events, 25.7 us)
Async XLA Ops:
  4.2 17.0 %collective-permute-start.9 = (bf16[128,2048]{1,0:T(8,128)(2,1)}, bf16[128,2048]{1,0:T(8,128)(2,1)S(1)}, u32[]{:S(2)}, u32[]{:S(2)}) collective-permute-start(bf16[128,2048]{1,0:T(8,128)(2,1)} %get-tuple-element.22.refs_1_), channel_id=1, source_target_pairs={{0,6},{1,7},{2,4},{3,5},{4,2},{5,3},{6,0},{7,1},{8,14},{9,15},{10,... | collective-permute-start | bytes 1572872 | tf_op jit(solution)/shard_map/ppermute | solution.py:360
  8.2 23.7 %collective-permute-start.5 = (bf16[128,2048]{1,0:T(8,128)(2,1)}, bf16[128,2048]{1,0:T(8,128)(2,1)S(1)}, u32[]{:S(2)}, u32[]{:S(2)}) collective-permute-start(bf16[128,2048]{1,0:T(8,128)(2,1)} %get-tuple-element.22.refs_1_), channel_id=1, source_target_pairs={{0,2},{1,3},{2,0},{3,1},{4,6},{5,7},{6,4},{7,5},{8,10},{9,11},{10,... | collective-permute-start | bytes 1572872 | tf_op jit(solution)/shard_map/ppermute | solution.py:360
  8.7 25.7 %collective-permute-start.7 = (bf16[128,2048]{1,0:T(8,128)(2,1)}, bf16[128,2048]{1,0:T(8,128)(2,1)S(1)}, u32[]{:S(2)}, u32[]{:S(2)}) collective-permute-start(bf16[128,2048]{1,0:T(8,128)(2,1)} %get-tuple-element.22.refs_1_), channel_id=1, source_target_pairs={{0,4},{1,5},{2,6},{3,7},{4,0},{5,1},{6,2},{7,3},{8,12},{9,13},{10,... | collective-permute-start | bytes 1572872 | tf_op jit(solution)/shard_map/ppermute | solution.py:360
  8.8 25.6 %collective-permute-start.4 = (bf16[128,2048]{1,0:T(8,128)(2,1)}, bf16[128,2048]{1,0:T(8,128)(2,1)S(1)}, u32[]{:S(2)}, u32[]{:S(2)}) collective-permute-start(bf16[128,2048]{1,0:T(8,128)(2,1)} %get-tuple-element.22.refs_1_), channel_id=1, source_target_pairs={{0,1},{1,0},{2,3},{3,2},{4,5},{5,4},{6,7},{7,6},{8,9},{9,8},{10,11... | collective-permute-start | bytes 1572872 | tf_op jit(solution)/shard_map/ppermute | solution.py:360
  8.8 26.1 %collective-permute-start.12 = (bf16[128,2048]{1,0:T(8,128)(2,1)}, bf16[128,2048]{1,0:T(8,128)(2,1)S(1)}, u32[]{:S(2)}, u32[]{:S(2)}) collective-permute-start(bf16[128,2048]{1,0:T(8,128)(2,1)} %get-tuple-element.23), channel_id=1, source_target_pairs={{0,8},{8,16},{16,24},{24,0},{1,9},{9,17},{17,25},{25,1},{2,10},{10... | collective-permute-start | bytes 1572872 | tf_op jit(solution)/shard_map/ppermute | solution.py:365
  21.2 70.8 %copy-start.4 = (bf16[128,2048]{1,0:T(8,128)(2,1)}, bf16[128,2048]{1,0:T(8,128)(2,1)S(1)}, u32[]{:S(2)}) copy-start(bf16[128,2048]{1,0:T(8,128)(2,1)S(1)} %collective-permute-done.9.refs_7_) | copy-start | bytes 1572868
  21.2 18.1 %collective-permute-start.21 = (bf16[128,2048]{1,0:T(8,128)(2,1)}, bf16[128,2048]{1,0:T(8,128)(2,1)S(1)}, u32[]{:S(2)}, u32[]{:S(2)}) collective-permute-start(bf16[128,2048]{1,0:T(8,128)(2,1)} %get-tuple-element.24), channel_id=1, source_target_pairs={{0,24},{8,0},{16,8},{24,16},{1,25},{9,1},{17,9},{25,17},{2,26},{10... | collective-permute-start | bytes 1572872 | tf_op jit(solution)/shard_map/ppermute | solution.py:365
  31.8 60.1 %copy-start.6 = (bf16[128,2048]{1,0:T(8,128)(2,1)}, bf16[128,2048]{1,0:T(8,128)(2,1)S(1)}, u32[]{:S(2)}) copy-start(bf16[128,2048]{1,0:T(8,128)(2,1)S(1)} %collective-permute-done.5.refs_3_) | copy-start | bytes 1572868
  31.8 50.0 %collective-permute-start.30 = (bf16[128,2048]{1,0:T(8,128)(2,1)}, bf16[128,2048]{1,0:T(8,128)(2,1)S(1)}, u32[]{:S(2)}, u32[]{:S(2)}) collective-permute-start(bf16[128,2048]{1,0:T(8,128)(2,1)} %get-tuple-element.25), channel_id=1, source_target_pairs={{0,16},{8,24},{16,0},{24,8},{1,17},{9,25},{17,1},{25,9},{2,18},{10... | collective-permute-start | bytes 1572872 | tf_op jit(solution)/shard_map/ppermute | solution.py:365
  34.4 53.3 %copy-start.8 = (bf16[128,2048]{1,0:T(8,128)(2,1)}, bf16[128,2048]{1,0:T(8,128)(2,1)S(1)}, u32[]{:S(2)}) copy-start(bf16[128,2048]{1,0:T(8,128)(2,1)S(1)} %collective-permute-done.7.refs_5_) | copy-start | bytes 1572868
  34.4 48.9 %collective-permute-start.10 = (bf16[128,2048]{1,0:T(8,128)(2,1)S(1)}, bf16[128,2048]{1,0:T(8,128)(2,1)S(1)}, u32[]{:S(2)}, u32[]{:S(2)}) collective-permute-start(bf16[128,2048]{1,0:T(8,128)(2,1)S(1)} %collective-permute-done.9.refs_7_), channel_id=1, source_target_pairs={{0,1},{1,0},{2,3},{3,2},{4,5},{5,4},{6,7},{7,6},{8,9},{9,8},{10,11... | collective-permute-start | bytes 1572872 | tf_op jit(solution)/shard_map/ppermute | solution.py:360
  34.4 53.2 %copy-start.10 = (bf16[128,2048]{1,0:T(8,128)(2,1)}, bf16[128,2048]{1,0:T(8,128)(2,1)S(1)}, u32[]{:S(2)}) copy-start(bf16[128,2048]{1,0:T(8,128)(2,1)S(1)} %collective-permute-done.4.refs_2_) | copy-start | bytes 1572868
  34.5 51.2 %collective-permute-start.6 = (bf16[128,2048]{1,0:T(8,128)(2,1)S(1)}, bf16[128,2048]{1,0:T(8,128)(2,1)S(1)}, u32[]{:S(2)}, u32[]{:S(2)}) collective-permute-start(bf16[128,2048]{1,0:T(8,128)(2,1)S(1)} %collective-permute-done.5.refs_3_), channel_id=1, source_target_pairs={{0,1},{1,0},{2,3},{3,2},{4,5},{5,4},{6,7},{7,6},{8,9},{9,8},{10,11... | collective-permute-start | bytes 1572872 | tf_op jit(solution)/shard_map/ppermute | solution.py:360
  34.9 57.0 %copy-start.26 = (bf16[128,2048]{1,0:T(8,128)(2,1)}, bf16[128,2048]{1,0:T(8,128)(2,1)S(1)}, u32[]{:S(2)}) copy-start(bf16[128,2048]{1,0:T(8,128)(2,1)S(1)} %collective-permute-done.12.refs_2_) | copy-start | bytes 1572868
  35.0 51.9 %collective-permute-start.8 = (bf16[128,2048]{1,0:T(8,128)(2,1)S(1)}, bf16[128,2048]{1,0:T(8,128)(2,1)S(1)}, u32[]{:S(2)}, u32[]{:S(2)}) collective-permute-start(bf16[128,2048]{1,0:T(8,128)(2,1)S(1)} %collective-permute-done.7.refs_5_), channel_id=1, source_target_pairs={{0,1},{1,0},{2,3},{3,2},{4,5},{5,4},{6,7},{7,6},{8,9},{9,8},{10,11... | collective-permute-start | bytes 1572872 | tf_op jit(solution)/shard_map/ppermute | solution.py:360
  39.3 72.6 %collective-permute-start.11 = (bf16[512,1024]{1,0:T(8,128)(2,1)}, bf16[512,1024]{1,0:T(8,128)(2,1)S(1)}, u32[]{:S(2)}, u32[]{:S(2)}) collective-permute-start(bf16[512,1024]{1,0:T(8,128)(2,1)} %pick_transposed.5), channel_id=1, source_target_pairs={{0,8},{8,16},{16,24},{24,0},{1,9},{9,17},{17,25},{25,1},{2,10},{10... | collective-permute-start | bytes 3145736 | tf_op jit(solution)/shard_map/ppermute | solution.py:365
  81.8 14.9 %collective-permute-start.14 = (bf16[128,2048]{1,0:T(8,128)(2,1)S(1)}, bf16[128,2048]{1,0:T(8,128)(2,1)}, u32[]{:S(2)}, u32[]{:S(2)}) collective-permute-start(bf16[128,2048]{1,0:T(8,128)(2,1)S(1)} %collective-permute-done.12.refs_2_), channel_id=1, source_target_pairs={{0,2},{1,3},{2,0},{3,1},{4,6},{5,7},{6,4},{7,5},{8,10},{9,11},{10,... | collective-permute-start | bytes 1572872 | tf_op jit(solution)/shard_map/ppermute | solution.py:360
  84.1 23.7 %collective-permute-start.16 = (bf16[128,2048]{1,0:T(8,128)(2,1)S(1)}, bf16[128,2048]{1,0:T(8,128)(2,1)}, u32[]{:S(2)}, u32[]{:S(2)}) collective-permute-start(bf16[128,2048]{1,0:T(8,128)(2,1)S(1)} %collective-permute-done.12.refs_2_), channel_id=1, source_target_pairs={{0,4},{1,5},{2,6},{3,7},{4,0},{5,1},{6,2},{7,3},{8,12},{9,13},{10,... | collective-permute-start | bytes 1572872 | tf_op jit(solution)/shard_map/ppermute | solution.py:360
  86.4 22.5 %collective-permute-start.18 = (bf16[128,2048]{1,0:T(8,128)(2,1)S(1)}, bf16[128,2048]{1,0:T(8,128)(2,1)}, u32[]{:S(2)}, u32[]{:S(2)}) collective-permute-start(bf16[128,2048]{1,0:T(8,128)(2,1)S(1)} %collective-permute-done.12.refs_2_), channel_id=1, source_target_pairs={{0,6},{1,7},{2,4},{3,5},{4,2},{5,3},{6,0},{7,1},{8,14},{9,15},{10,... | collective-permute-start | bytes 1572872 | tf_op jit(solution)/shard_map/ppermute | solution.py:360
  87.7 22.7 %collective-permute-start.13 = (bf16[128,2048]{1,0:T(8,128)(2,1)S(1)}, bf16[128,2048]{1,0:T(8,128)(2,1)}, u32[]{:S(2)}, u32[]{:S(2)}) collective-permute-start(bf16[128,2048]{1,0:T(8,128)(2,1)S(1)} %collective-permute-done.12.refs_2_), channel_id=1, source_target_pairs={{0,1},{1,0},{2,3},{3,2},{4,5},{5,4},{6,7},{7,6},{8,9},{9,8},{10,11... | collective-permute-start | bytes 1572872 | tf_op jit(solution)/shard_map/ppermute | solution.py:360
  92.0 73.0 %copy-start = (f32[1,512,2048]{2,1,0:T(8,128)S(1)}, f32[1,512,2048]{2,1,0:T(8,128)}, u32[]{:S(2)}) copy-start(f32[1,512,2048]{2,1,0:T(8,128)} %param.12) | copy-start | bytes 12582916
  96.7 40.2 %collective-permute-start.20 = (bf16[512,1024]{1,0:T(8,128)(2,1)}, bf16[512,1024]{1,0:T(8,128)(2,1)S(1)}, u32[]{:S(2)}, u32[]{:S(2)}) collective-permute-start(bf16[512,1024]{1,0:T(8,128)(2,1)} %pick_transposed.6), channel_id=1, source_target_pairs={{0,24},{8,0},{16,8},{24,16},{1,25},{9,1},{17,9},{25,17},{2,26},{10... | collective-permute-start | bytes 3145736 | tf_op jit(solution)/shard_map/ppermute | solution.py:365
  107.8 14.9 %collective-permute-start.23 = (bf16[128,2048]{1,0:T(8,128)(2,1)S(1)}, bf16[128,2048]{1,0:T(8,128)(2,1)}, u32[]{:S(2)}, u32[]{:S(2)}) collective-permute-start(bf16[128,2048]{1,0:T(8,128)(2,1)S(1)} %collective-permute-done.21.refs_2_), channel_id=1, source_target_pairs={{0,2},{1,3},{2,0},{3,1},{4,6},{5,7},{6,4},{7,5},{8,10},{9,11},{10,... | collective-permute-start | bytes 1572872 | tf_op jit(solution)/shard_map/ppermute | solution.py:360
  108.9 22.6 %collective-permute-start.25 = (bf16[128,2048]{1,0:T(8,128)(2,1)S(1)}, bf16[128,2048]{1,0:T(8,128)(2,1)}, u32[]{:S(2)}, u32[]{:S(2)}) collective-permute-start(bf16[128,2048]{1,0:T(8,128)(2,1)S(1)} %collective-permute-done.21.refs_2_), channel_id=1, source_target_pairs={{0,4},{1,5},{2,6},{3,7},{4,0},{5,1},{6,2},{7,3},{8,12},{9,13},{10,... | collective-permute-start | bytes 1572872 | tf_op jit(solution)/shard_map/ppermute | solution.py:360
  110.4 25.7 %collective-permute-start.27 = (bf16[128,2048]{1,0:T(8,128)(2,1)S(1)}, bf16[128,2048]{1,0:T(8,128)(2,1)}, u32[]{:S(2)}, u32[]{:S(2)}) collective-permute-start(bf16[128,2048]{1,0:T(8,128)(2,1)S(1)} %collective-permute-done.21.refs_2_), channel_id=1, source_target_pairs={{0,6},{1,7},{2,4},{3,5},{4,2},{5,3},{6,0},{7,1},{8,14},{9,15},{10,... | collective-permute-start | bytes 1572872 | tf_op jit(solution)/shard_map/ppermute | solution.py:360
  111.9 24.1 %collective-permute-start.22 = (bf16[128,2048]{1,0:T(8,128)(2,1)S(1)}, bf16[128,2048]{1,0:T(8,128)(2,1)S(1)}, u32[]{:S(2)}, u32[]{:S(2)}) collective-permute-start(bf16[128,2048]{1,0:T(8,128)(2,1)S(1)} %collective-permute-done.21.refs_2_), channel_id=1, source_target_pairs={{0,1},{1,0},{2,3},{3,2},{4,5},{5,4},{6,7},{7,6},{8,9},{9,8},{10,11... | collective-permute-start | bytes 1572872 | tf_op jit(solution)/shard_map/ppermute | solution.py:360
  122.7 22.4 %collective-permute-start.32 = (bf16[128,2048]{1,0:T(8,128)(2,1)S(1)}, bf16[128,2048]{1,0:T(8,128)(2,1)S(1)}, u32[]{:S(2)}, u32[]{:S(2)}) collective-permute-start(bf16[128,2048]{1,0:T(8,128)(2,1)S(1)} %collective-permute-done.30.refs_2_), channel_id=1, source_target_pairs={{0,2},{1,3},{2,0},{3,1},{4,6},{5,7},{6,4},{7,5},{8,10},{9,11},{10,... | collective-permute-start | bytes 1572872 | tf_op jit(solution)/shard_map/ppermute | solution.py:360
  131.5 22.0 %collective-permute-start.34 = (bf16[128,2048]{1,0:T(8,128)(2,1)S(1)}, bf16[128,2048]{1,0:T(8,128)(2,1)S(1)}, u32[]{:S(2)}, u32[]{:S(2)}) collective-permute-start(bf16[128,2048]{1,0:T(8,128)(2,1)S(1)} %collective-permute-done.30.refs_2_), channel_id=1, source_target_pairs={{0,4},{1,5},{2,6},{3,7},{4,0},{5,1},{6,2},{7,3},{8,12},{9,13},{10,... | collective-permute-start | bytes 1572872 | tf_op jit(solution)/shard_map/ppermute | solution.py:360
  136.1 17.4 %collective-permute-start.36 = (bf16[128,2048]{1,0:T(8,128)(2,1)S(1)}, bf16[128,2048]{1,0:T(8,128)(2,1)S(1)}, u32[]{:S(2)}, u32[]{:S(2)}) collective-permute-start(bf16[128,2048]{1,0:T(8,128)(2,1)S(1)} %collective-permute-done.30.refs_2_), channel_id=1, source_target_pairs={{0,6},{1,7},{2,4},{3,5},{4,2},{5,3},{6,0},{7,1},{8,14},{9,15},{10,... | collective-permute-start | bytes 1572872 | tf_op jit(solution)/shard_map/ppermute | solution.py:360
  136.9 17.4 %collective-permute-start.15 = (bf16[128,2048]{1,0:T(8,128)(2,1)}, bf16[128,2048]{1,0:T(8,128)(2,1)S(1)}, u32[]{:S(2)}, u32[]{:S(2)}) collective-permute-start(bf16[128,2048]{1,0:T(8,128)(2,1)} %collective-permute-done.14.refs_4_), channel_id=1, source_target_pairs={{0,1},{1,0},{2,3},{3,2},{4,5},{5,4},{6,7},{7,6},{8,9},{9,8},{10,11... | collective-permute-start | bytes 1572872 | tf_op jit(solution)/shard_map/ppermute | solution.py:360
  136.9 23.0 %collective-permute-start.17 = (bf16[128,2048]{1,0:T(8,128)(2,1)}, bf16[128,2048]{1,0:T(8,128)(2,1)S(1)}, u32[]{:S(2)}, u32[]{:S(2)}) collective-permute-start(bf16[128,2048]{1,0:T(8,128)(2,1)} %collective-permute-done.16.refs_6_), channel_id=1, source_target_pairs={{0,1},{1,0},{2,3},{3,2},{4,5},{5,4},{6,7},{7,6},{8,9},{9,8},{10,11... | collective-permute-start | bytes 1572872 | tf_op jit(solution)/shard_map/ppermute | solution.py:360
  145.1 20.3 %collective-permute-start.19 = (bf16[128,2048]{1,0:T(8,128)(2,1)}, bf16[128,2048]{1,0:T(8,128)(2,1)}, u32[]{:S(2)}, u32[]{:S(2)}) collective-permute-start(bf16[128,2048]{1,0:T(8,128)(2,1)} %collective-permute-done.18.refs_8_), channel_id=1, source_target_pairs={{0,1},{1,0},{2,3},{3,2},{4,5},{5,4},{6,7},{7,6},{8,9},{9,8},{10,11... | collective-permute-start | bytes 1572872 | tf_op jit(solution)/shard_map/ppermute | solution.py:360
  153.5 12.1 %collective-permute-start.24 = (bf16[128,2048]{1,0:T(8,128)(2,1)}, bf16[128,2048]{1,0:T(8,128)(2,1)}, u32[]{:S(2)}, u32[]{:S(2)}) collective-permute-start(bf16[128,2048]{1,0:T(8,128)(2,1)} %collective-permute-done.23.refs_4_), channel_id=1, source_target_pairs={{0,1},{1,0},{2,3},{3,2},{4,5},{5,4},{6,7},{7,6},{8,9},{9,8},{10,11... | collective-permute-start | bytes 1572872 | tf_op jit(solution)/shard_map/ppermute | solution.py:360
  153.5 12.5 %collective-permute-start.26 = (bf16[128,2048]{1,0:T(8,128)(2,1)}, bf16[128,2048]{1,0:T(8,128)(2,1)}, u32[]{:S(2)}, u32[]{:S(2)}) collective-permute-start(bf16[128,2048]{1,0:T(8,128)(2,1)} %collective-permute-done.25.refs_6_), channel_id=1, source_target_pairs={{0,1},{1,0},{2,3},{3,2},{4,5},{5,4},{6,7},{7,6},{8,9},{9,8},{10,11... | collective-permute-start | bytes 1572872 | tf_op jit(solution)/shard_map/ppermute | solution.py:360
  155.2 10.9 %collective-permute-start.28 = (bf16[128,2048]{1,0:T(8,128)(2,1)}, bf16[128,2048]{1,0:T(8,128)(2,1)}, u32[]{:S(2)}, u32[]{:S(2)}) collective-permute-start(bf16[128,2048]{1,0:T(8,128)(2,1)} %collective-permute-done.27.refs_8_), channel_id=1, source_target_pairs={{0,1},{1,0},{2,3},{3,2},{4,5},{5,4},{6,7},{7,6},{8,9},{9,8},{10,11... | collective-permute-start | bytes 1572872 | tf_op jit(solution)/shard_map/ppermute | solution.py:360
  160.7 39.6 %collective-permute-start.29 = (bf16[512,1024]{1,0:T(8,128)(2,1)}, bf16[512,1024]{1,0:T(8,128)(2,1)S(1)}, u32[]{:S(2)}, u32[]{:S(2)}) collective-permute-start(bf16[512,1024]{1,0:T(8,128)(2,1)} %pick_transposed.7), channel_id=1, source_target_pairs={{0,16},{8,24},{16,0},{24,8},{1,17},{9,25},{17,1},{25,9},{2,18},{10... | collective-permute-start | bytes 3145736 | tf_op jit(solution)/shard_map/ppermute | solution.py:365
  165.4 17.8 %collective-permute-start.31 = (bf16[128,2048]{1,0:T(8,128)(2,1)S(1)}, bf16[128,2048]{1,0:T(8,128)(2,1)S(1)}, u32[]{:S(2)}, u32[]{:S(2)}) collective-permute-start(bf16[128,2048]{1,0:T(8,128)(2,1)S(1)} %collective-permute-done.30.refs_2_), channel_id=1, source_target_pairs={{0,1},{1,0},{2,3},{3,2},{4,5},{5,4},{6,7},{7,6},{8,9},{9,8},{10,11... | collective-permute-start | bytes 1572872 | tf_op jit(solution)/shard_map/ppermute | solution.py:360
  165.6 34.7 %collective-permute-start.33 = (bf16[128,2048]{1,0:T(8,128)(2,1)}, bf16[128,2048]{1,0:T(8,128)(2,1)S(1)}, u32[]{:S(2)}, u32[]{:S(2)}) collective-permute-start(bf16[128,2048]{1,0:T(8,128)(2,1)} %copy-done.18), channel_id=1, source_target_pairs={{0,1},{1,0},{2,3},{3,2},{4,5},{5,4},{6,7},{7,6},{8,9},{9,8},{10,11... | collective-permute-start | bytes 1572872 | tf_op jit(solution)/shard_map/ppermute | solution.py:360
  166.0 34.3 %collective-permute-start.35 = (bf16[128,2048]{1,0:T(8,128)(2,1)}, bf16[128,2048]{1,0:T(8,128)(2,1)S(1)}, u32[]{:S(2)}, u32[]{:S(2)}) collective-permute-start(bf16[128,2048]{1,0:T(8,128)(2,1)} %copy-done.20), channel_id=1, source_target_pairs={{0,1},{1,0},{2,3},{3,2},{4,5},{5,4},{6,7},{7,6},{8,9},{9,8},{10,11... | collective-permute-start | bytes 1572872 | tf_op jit(solution)/shard_map/ppermute | solution.py:360
  166.1 34.1 %collective-permute-start.37 = (bf16[128,2048]{1,0:T(8,128)(2,1)}, bf16[128,2048]{1,0:T(8,128)(2,1)S(1)}, u32[]{:S(2)}, u32[]{:S(2)}) collective-permute-start(bf16[128,2048]{1,0:T(8,128)(2,1)} %copy-done.22), channel_id=1, source_target_pairs={{0,1},{1,0},{2,3},{3,2},{4,5},{5,4},{6,7},{7,6},{8,9},{9,8},{10,11... | collective-permute-start | bytes 1572872 | tf_op jit(solution)/shard_map/ppermute | solution.py:360
  183.3 21.6 %collective-permute-start = (f32[1,128]{1,0:T(1,128)S(1)}, f32[1,128]{1,0:T(1,128)S(1)}, u32[]{:S(2)}, u32[]{:S(2)}) collective-permute-start(f32[1,128]{1,0:T(1,128)S(1)} %bitcast.43), channel_id=1, source_target_pairs={{0,1},{1,0},{2,3},{3,2},{4,5},{5,4},{6,7},{7,6},{8,9},{9,8},{10,11... | collective-permute-start | bytes 1544 | tf_op jit(solution)/shard_map/ppermute | solution.py:360
  204.7 3.7 collective-permute-start.38
  204.8 5.0 %collective-permute-start.1 = (f32[1,128]{1,0:T(1,128)S(1)}, f32[1,128]{1,0:T(1,128)S(1)}, u32[]{:S(2)}, u32[]{:S(2)}) collective-permute-start(f32[1,128]{1,0:T(1,128)S(1)} %bitcast_add_fusion.refs_0_), channel_id=1, source_target_pairs={{0,2},{1,3},{2,0},{3,1},{4,6},{5,7},{6,4},{7,5},{8,10},{9,11},{10,... | collective-permute-start | bytes 1544 | tf_op jit(solution)/shard_map/ppermute | solution.py:360
  205.1 6.8 %collective-permute-start.2 = (f32[1,128]{1,0:T(1,128)S(1)}, f32[1,128]{1,0:T(1,128)S(1)}, u32[]{:S(2)}, u32[]{:S(2)}) collective-permute-start(f32[1,128]{1,0:T(1,128)S(1)} %bitcast_add_fusion.refs_0_), channel_id=1, source_target_pairs={{0,4},{1,5},{2,6},{3,7},{4,0},{5,1},{6,2},{7,3},{8,12},{9,13},{10,... | collective-permute-start | bytes 1544 | tf_op jit(solution)/shard_map/ppermute | solution.py:360
  206.4 5.5 %collective-permute-start.3 = (f32[1,128]{1,0:T(1,128)S(1)}, f32[1,128]{1,0:T(1,128)S(1)}, u32[]{:S(2)}, u32[]{:S(2)}) collective-permute-start(f32[1,128]{1,0:T(1,128)S(1)} %bitcast_add_fusion.refs_0_), channel_id=1, source_target_pairs={{0,6},{1,7},{2,4},{3,5},{4,2},{5,3},{6,0},{7,1},{8,14},{9,15},{10,... | collective-permute-start | bytes 1544 | tf_op jit(solution)/shard_map/ppermute | solution.py:360
  208.4 3.6 collective-permute-start.39
  208.6 3.6 collective-permute-start.40
  209.9 4.5 %collective-permute-start.41 = (f32[1,128]{1,0:T(1,128)S(1)}, f32[1,128]{1,0:T(1,128)S(1)}, u32[]{:S(2)}, u32[]{:S(2)}) collective-permute-start(f32[1,128]{1,0:T(1,128)S(1)} %add.51.refs_4_), channel_id=1, source_target_pairs={{0,6},{1,7},{2,4},{3,5},{4,2},{5,3},{6,0},{7,1},{8,14},{9,15},{10,... | collective-permute-start | bytes 1544 | tf_op jit(solution)/shard_map/ppermute | solution.py:360
  222.1 26.2 %collective-permute-start.43 = (bf16[256,2048]{1,0:T(8,128)(2,1)}, bf16[256,2048]{1,0:T(8,128)(2,1)S(1)}, u32[]{:S(2)}, u32[]{:S(2)}) collective-permute-start(bf16[256,2048]{1,0:T(8,128)(2,1)} %get-tuple-element.38), channel_id=1, source_target_pairs={{0,8},{16,24},{8,0},{24,16},{1,9},{17,25},{9,1},{25,17},{2,10},{18... | collective-permute-start | bytes 3145736 | tf_op jit(solution)/shard_map/ppermute | solution.py:410
  222.1 37.6 %collective-permute-start.42 = (bf16[128,2048]{1,0:T(8,128)(2,1)}, bf16[128,2048]{1,0:T(8,128)(2,1)}, u32[]{:S(2)}, u32[]{:S(2)}) collective-permute-start(bf16[128,2048]{1,0:T(8,128)(2,1)} %get-tuple-element.37), channel_id=1, source_target_pairs={{0,8},{16,24},{8,0},{24,16},{1,9},{17,25},{9,1},{25,17},{2,10},{18... | collective-permute-start | bytes 1572872 | tf_op jit(solution)/shard_map/ppermute | solution.py:410
  224.2 80.4 %collective-permute-start.47 = (bf16[256,2048]{1,0:T(8,128)(2,1)}, bf16[256,2048]{1,0:T(8,128)(2,1)S(1)}, u32[]{:S(2)}, u32[]{:S(2)}) collective-permute-start(bf16[256,2048]{1,0:T(8,128)(2,1)} %get-tuple-element.38), channel_id=1, source_target_pairs={{8,16},{16,8},{9,17},{17,9},{10,18},{18,10},{11,19},{19,11},{12,20... | collective-permute-start | bytes 3145736 | tf_op jit(solution)/shard_map/ppermute | solution.py:410
  248.4 66.7 %collective-permute-start.53 = (bf16[256,2048]{1,0:T(8,128)(2,1)S(1)}, bf16[256,2048]{1,0:T(8,128)(2,1)S(1)}, u32[]{:S(2)}, u32[]{:S(2)}) collective-permute-start(bf16[256,2048]{1,0:T(8,128)(2,1)S(1)} %collective-permute-done.43.refs_0_), channel_id=1, source_target_pairs={{8,16},{16,8},{9,17},{17,9},{10,18},{18,10},{11,19},{19,11},{12,20... | collective-permute-start | bytes 3145736 | tf_op jit(solution)/shard_map/ppermute | solution.py:410
  249.1 13.5 %collective-permute-start.45 = (bf16[128,2048]{1,0:T(8,128)(2,1)}, bf16[128,2048]{1,0:T(8,128)(2,1)}, u32[]{:S(2)}, u32[]{:S(2)}) collective-permute-start(bf16[128,2048]{1,0:T(8,128)(2,1)} %get-tuple-element.37), channel_id=1, source_target_pairs={{8,16},{16,8},{9,17},{17,9},{10,18},{18,10},{11,19},{19,11},{12,20... | collective-permute-start | bytes 1572872 | tf_op jit(solution)/shard_map/ppermute | solution.py:410
  253.5 34.2 %collective-permute-start.44 = (bf16[128,2048]{1,0:T(8,128)(2,1)}, bf16[128,2048]{1,0:T(8,128)(2,1)}, u32[]{:S(2)}, u32[]{:S(2)}) collective-permute-start(bf16[128,2048]{1,0:T(8,128)(2,1)} %get-tuple-element.39), channel_id=1, source_target_pairs={{0,8},{16,24},{8,0},{24,16},{1,9},{17,25},{9,1},{25,17},{2,10},{18... | collective-permute-start | bytes 1572872 | tf_op jit(solution)/shard_map/ppermute | solution.py:410
  259.7 29.4 %collective-permute-start.49 = (bf16[128,2048]{1,0:T(8,128)(2,1)}, bf16[128,2048]{1,0:T(8,128)(2,1)}, u32[]{:S(2)}, u32[]{:S(2)}) collective-permute-start(bf16[128,2048]{1,0:T(8,128)(2,1)} %get-tuple-element.39), channel_id=1, source_target_pairs={{8,16},{16,8},{9,17},{17,9},{10,18},{18,10},{11,19},{19,11},{12,20... | collective-permute-start | bytes 1572872 | tf_op jit(solution)/shard_map/ppermute | solution.py:410
  262.6 52.7 %collective-permute-start.46 = (bf16[128,2048]{1,0:T(8,128)(2,1)}, bf16[128,2048]{1,0:T(8,128)(2,1)}, u32[]{:S(2)}, u32[]{:S(2)}) collective-permute-start(bf16[128,2048]{1,0:T(8,128)(2,1)} %collective-permute-done.45.refs_0_), channel_id=1, source_target_pairs={{0,8},{16,24},{8,0},{24,16},{1,9},{17,25},{9,1},{25,17},{2,10},{18... | collective-permute-start | bytes 1572872 | tf_op jit(solution)/shard_map/ppermute | solution.py:410
  287.6 29.6 %collective-permute-start.51 = (bf16[128,2048]{1,0:T(8,128)(2,1)}, bf16[128,2048]{1,0:T(8,128)(2,1)}, u32[]{:S(2)}, u32[]{:S(2)}) collective-permute-start(bf16[128,2048]{1,0:T(8,128)(2,1)} %collective-permute-done.42.refs_0_), channel_id=1, source_target_pairs={{8,16},{16,8},{9,17},{17,9},{10,18},{18,10},{11,19},{19,11},{12,20... | collective-permute-start | bytes 1572872 | tf_op jit(solution)/shard_map/ppermute | solution.py:410
  289.1 28.2 %collective-permute-start.55 = (bf16[128,2048]{1,0:T(8,128)(2,1)}, bf16[128,2048]{1,0:T(8,128)(2,1)}, u32[]{:S(2)}, u32[]{:S(2)}) collective-permute-start(bf16[128,2048]{1,0:T(8,128)(2,1)} %collective-permute-done.44.refs_0_), channel_id=1, source_target_pairs={{8,16},{16,8},{9,17},{17,9},{10,18},{18,10},{11,19},{19,11},{12,20... | collective-permute-start | bytes 1572872 | tf_op jit(solution)/shard_map/ppermute | solution.py:410
  298.4 20.9 %all-to-all-start.1 = ((bf16[16,128,128]{2,1,0:T(8,128)(2,1)}), bf16[16,128,128]{2,1,0:T(8,128)(2,1)}, u32[]{:S(2)}, u32[]{:S(2)}) async-start(bf16[16,128,128]{2,1,0:T(8,128)(2,1)} %bitcast.40), calls=%async_computation.1 | async-start | bytes 1048576 | tf_op jit(solution)/shard_map/all_to_all | solution.py:431
  304.6 34.6 %collective-permute-start.48 = (bf16[256,2048]{1,0:T(8,128)(2,1)S(1)}, bf16[256,2048]{1,0:T(8,128)(2,1)}, u32[]{:S(2)}, u32[]{:S(2)}) collective-permute-start(bf16[256,2048]{1,0:T(8,128)(2,1)S(1)} %collective-permute-done.47.refs_0_), channel_id=1, source_target_pairs={{0,8},{16,24},{8,0},{24,16},{1,9},{17,25},{9,1},{25,17},{2,10},{18... | collective-permute-start | bytes 3145736 | tf_op jit(solution)/shard_map/ppermute | solution.py:410
  315.1 71.5 %collective-permute-start.54 = (bf16[256,2048]{1,0:T(8,128)(2,1)S(1)}, bf16[256,2048]{1,0:T(8,128)(2,1)}, u32[]{:S(2)}, u32[]{:S(2)}) collective-permute-start(bf16[256,2048]{1,0:T(8,128)(2,1)S(1)} %collective-permute-done.53.refs_0_), channel_id=1, source_target_pairs={{0,8},{16,24},{8,0},{24,16},{1,9},{17,25},{9,1},{25,17},{2,10},{18... | collective-permute-start | bytes 3145736 | tf_op jit(solution)/shard_map/ppermute | solution.py:410
  315.3 57.6 %collective-permute-start.50 = (bf16[128,2048]{1,0:T(8,128)(2,1)}, bf16[128,2048]{1,0:T(8,128)(2,1)}, u32[]{:S(2)}, u32[]{:S(2)}) collective-permute-start(bf16[128,2048]{1,0:T(8,128)(2,1)} %collective-permute-done.49.refs_0_), channel_id=1, source_target_pairs={{0,8},{16,24},{8,0},{24,16},{1,9},{17,25},{9,1},{25,17},{2,10},{18... | collective-permute-start | bytes 1572872 | tf_op jit(solution)/shard_map/ppermute | solution.py:410
  317.3 66.8 %collective-permute-start.52 = (bf16[128,2048]{1,0:T(8,128)(2,1)}, bf16[128,2048]{1,0:T(8,128)(2,1)}, u32[]{:S(2)}, u32[]{:S(2)}) collective-permute-start(bf16[128,2048]{1,0:T(8,128)(2,1)} %collective-permute-done.51.refs_0_), channel_id=1, source_target_pairs={{0,8},{16,24},{8,0},{24,16},{1,9},{17,25},{9,1},{25,17},{2,10},{18... | collective-permute-start | bytes 1572872 | tf_op jit(solution)/shard_map/ppermute | solution.py:410
  317.4 77.7 %collective-permute-start.56 = (bf16[128,2048]{1,0:T(8,128)(2,1)}, bf16[128,2048]{1,0:T(8,128)(2,1)}, u32[]{:S(2)}, u32[]{:S(2)}) collective-permute-start(bf16[128,2048]{1,0:T(8,128)(2,1)} %collective-permute-done.55.refs_0_), channel_id=1, source_target_pairs={{0,8},{16,24},{8,0},{24,16},{1,9},{17,25},{9,1},{25,17},{2,10},{18... | collective-permute-start | bytes 1572872 | tf_op jit(solution)/shard_map/ppermute | solution.py:410
  (31 other events, 231.7 us)

commit v3 on v2

--- a/solution.py
+++ b/solution.py
@@ -12,7 +12,7 @@
 table_rate = 0.5
 table_decay = 0.2
 eps_norm = 1e-06
-weight_parts = (2, 4, 2)
+weight_parts = (1, 2, 4, 1)
 lanes = 128
 mib = 1 << 20
 
@@ -69,36 +69,37 @@
     )(layer_owner, value)
 
 
-def pick_transposed(layer_owner, value, step):
+def pick_transposed(layer_owner, value, step, start, count):
     groups = lax.axis_size("grp")
-    tokens, rows = value.shape[1:]
-    tile = min(tokens, 256)
+    rows = value.shape[2]
+    tile = min(count, 256)
+    first = start // tile
 
     def kernel(owner_ref, value_ref, out_ref):
         out_ref[...] = value_ref[0].T
 
     def source(i, owner_ref):
         target = lax.rem(lax.axis_index("grp") + step, groups)
-        return layer_of(owner_ref, target), i, 0
+        return layer_of(owner_ref, target), first + i, 0
 
     return pl.pallas_call(
         kernel,
         grid_spec=pltpu.PrefetchScalarGridSpec(
             num_scalar_prefetch=1,
-            grid=(tokens // tile,),
+            grid=(count // tile,),
             in_specs=[pl.BlockSpec((1, tile, rows), source)],
             out_specs=pl.BlockSpec((rows, tile), lambda i, owner: (0, i)),
         ),
-        out_shape=jax.ShapeDtypeStruct((rows, tokens), value.dtype),
+        out_shape=jax.ShapeDtypeStruct((rows, count), value.dtype),
         compiler_params=pltpu.CompilerParams(vmem_limit_bytes=56 * mib),
         cost_estimate=pl.CostEstimate(
-            flops=0, bytes_accessed=4 * rows * tokens, transcendentals=0
+            flops=0, bytes_accessed=4 * rows * count, transcendentals=0
         ),
         name="pick_transposed",
     )(layer_owner, value)
 
 
-def accumulate(acc, inputs, pieces, last):
+def accumulate(acc, inputs, pieces):
     rows, tokens = inputs.shape
     per_dev, columns = pieces[0].shape
     tile = min(columns, 512)
@@ -110,7 +111,6 @@
         x_ref = refs.pop(0)
         piece_refs, refs = refs[: len(pieces)], refs[len(pieces) :]
         out_ref = refs.pop(0)
-        square_ref = refs.pop(0) if last else None
         x_all, g_all, x_sem, g_sem = refs
         column = pl.program_id(0)
         device = lax.axis_index("dev")
@@ -133,31 +133,15 @@
         if acc is not None:
             total = total + acc_ref[...]
         out_ref[...] = total
-        if last:
-            squares = jnp.sum(total * total, axis=0, keepdims=True)
-            folded = sum(squares[:, k * lanes : (k + 1) * lanes] for k in range(tile // lanes))
-
-            @pl.when(column == 0)
-            def _():
-                square_ref[...] = folded
-
-            @pl.when(column > 0)
-            def _():
-                square_ref[...] += folded
 
     block = pl.BlockSpec((rows, tile), lambda j: (0, j))
     operands = ([acc] if acc is not None else []) + [inputs, *pieces]
-    out_shape = [jax.ShapeDtypeStruct((rows, columns), jnp.float32)]
-    out_specs = [block]
-    if last:
-        out_shape.append(jax.ShapeDtypeStruct((1, lanes), jnp.float32))
-        out_specs.append(pl.BlockSpec((1, lanes), lambda j: (0, 0)))
-    result = pl.pallas_call(
+    return pl.pallas_call(
         kernel,
         grid=(tiles,),
         in_specs=([block] if acc is not None else []) + [anywhere] * (1 + len(pieces)),
-        out_specs=out_specs,
-        out_shape=out_shape,
+        out_specs=block,
+        out_shape=jax.ShapeDtypeStruct((rows, columns), jnp.float32),
         scratch_shapes=[
             pltpu.VMEM((rows, tokens), jnp.bfloat16),
             pltpu.VMEM((tiles, tokens, tile), jnp.bfloat16),
@@ -174,7 +158,34 @@
         ),
         name="accumulate",
     )(*operands)
-    return result if last else result[0]
+
+
+def arrange(pieces):
+    per_dev, columns = pieces[0].shape
+    devices = len(pieces)
+
+    def kernel(*refs):
+        piece_refs, (out_ref, sem) = refs[:devices], refs[devices:]
+        device = lax.axis_index("dev")
+        for mask, ref in enumerate(piece_refs):
+            first = pl.multiple_of((device ^ mask) * per_dev, per_dev)
+            pltpu.make_async_copy(ref, out_ref.at[pl.ds(first, per_dev)], sem).start()
+        pltpu.make_async_copy(out_ref, out_ref, sem).wait()
+
+    return pl.pallas_call(
+        kernel,
+        in_specs=[anywhere] * devices,
+        out_specs=pl.BlockSpec(memory_space=pltpu.VMEM),
+        out_shape=jax.ShapeDtypeStruct((devices * per_dev, columns), pieces[0].dtype),
+        scratch_shapes=[pltpu.SemaphoreType.DMA],
+        compiler_params=pltpu.CompilerParams(
+            vmem_limit_bytes=4 * devices * per_dev * columns + 2 * mib
+        ),
+        cost_estimate=pl.CostEstimate(
+            flops=0, bytes_accessed=4 * devices * per_dev * columns, transcendentals=0
+        ),
+        name="arrange",
+    )(*pieces)
 
 
 def update(layer_owner, weight_squares, grad_squares, grad, master, moment, chunk, buffers):
@@ -354,7 +365,7 @@
 ):
     groups = lax.axis_size("grp")
     devices = lax.axis_size("dev")
-    masks = range(2, devices, 2)
+    masks = range(devices - 2, 0, -2)
 
     def swap(value, mask):
         return lax.ppermute(value, "dev", [(i, i ^ mask) for i in range(devices)])
@@ -364,26 +375,36 @@
             return value
         return lax.ppermute(value, "grp", [(i, (i + step) % groups) for i in range(groups)])
 
+    def fold(value):
+        squares = jnp.sum(value * value, axis=0, keepdims=True)
+        return jnp.sum(squares.reshape(-1, lanes), axis=0, keepdims=True)
+
     def dev_parts(value):
         pair = value + swap(value, 1)
         return [pair] + [swap(pair, mask) for mask in masks]
 
     master = master_weights[0]
     moment = momentum[0]
-    rows, columns = master.shape
+    rows, _ = master.shape
 
     shifts = shifts_of(groups)
-    g_own = dict(zip(shifts, pick(layer_owner, output_grads, shifts)))
-    x_own = {}
-    for step in shifts:
-        x_own[step] = pick_transposed(layer_owner, layer_inputs, step)
+    g_own = dict(zip(shifts[1:2], pick(layer_owner, output_grads, shifts[1:2])))
+    rest = shifts[:1] + shifts[2:]
+    g_own.update(zip(rest, pick(layer_owner, output_grads, rest)))
     g_own = {step: shift(g_own[step], step) for step in shifts}
-    x_own = {step: shift(x_own[step], step) for step in shifts}
+    tokens = layer_inputs.shape[1]
+    early = tokens * 3 // 4
+
+    def inputs_of(step, start, count):
+        value = pick_transposed(layer_owner, layer_inputs, step, start, count)
+        return shift(value, step)
+
+    x_own = {step: inputs_of(step, 0, tokens) for step in shifts[:-1]}
+    x_early = inputs_of(shifts[-1], 0, early)
+    x_late = inputs_of(shifts[-1], early, tokens - early)
     new_table = update_table(table_blocks[0], block_grads[0, 0], block_ids[0, 0], block_counts[0, 0])
 
-    squares = jnp.sum(master * master, axis=0, keepdims=True)
-    squares = jnp.sum(squares.reshape(columns // lanes, lanes), axis=0, keepdims=True)
-    weight_squares = dev_parts(squares)
+    weight_squares = dev_parts(fold(master))
 
     grad = None
     for step in shifts:
@@ -391,8 +412,13 @@
         for mask in range(0, devices, 2):
             pieces[mask] = swap(g_own[step], mask) if mask else g_own[step]
             pieces[mask + 1] = swap(pieces[mask], 1)
-        grad = accumulate(grad, x_own[step], pieces, step == shifts[-1])
-    grad, squares = grad
+        if step != shifts[-1]:
+            grad = accumulate(grad, x_own[step], pieces)
+    cotangents = arrange(pieces)
+    grad = grad + jnp.dot(x_early, cotangents[:early], preferred_element_type=jnp.float32)
+    grad = lax.optimization_barrier(grad)
+    grad = grad + jnp.dot(x_late, cotangents[early:], preferred_element_type=jnp.float32)
+    squares = fold(grad)
     grad_squares = dev_parts(squares)
 
     chunks = chunks_of(rows)

time: 399 us -> 390 us (0.977)
  starting transfers between devices: 123 us -> 99.3 us
  Pallas kernels: 71.3 us -> 76.5 us
  waiting for transfers between devices: 178 us -> 183 us
    ppermute x6 -> x7, waiting for transfers between devices: 26.6 us -> 58 us  [shift(): lax.ppermute(value, 'grp', [(i, (i + step) % groups) for i in range(group...]
    ppermute x6 -> x7, starting transfers between devices: 41.3 us -> 12.6 us  [shift(): lax.ppermute(value, 'grp', [(i, (i + step) % groups) for i in range(group...]
    ppermute x15 -> x20, waiting for transfers between devices: 78.6 us -> 55.2 us  [local(): piece = lax.ppermute(held[chunk][chain], 'grp', pairs)]
    pallas_call x4 -> x3, Pallas kernels: 18.3 us -> 14 us  [accumulate(): pl.pallas_call(kernel, grid=(tiles,), in_specs=([block] if acc is not Non...]
    unnamed x76 -> x62, local copies, waits for them, and re-layouts: 10.2 us -> 7.46 us
    pallas_call x9 -> x12, Pallas kernels: 21.7 us -> 24.2 us  [place(): pl.pallas_call(kernel, grid_spec=pltpu.PrefetchScalarGridSpec(num_scalar_...]
    pallas_call x4 -> x5, Pallas kernels: 17 us -> 19.2 us  [pick_transposed(): pl.pallas_call(kernel, grid_spec=pltpu.PrefetchScalarGridSpec(num_scalar_...]
    ppermute x15 -> x20, starting transfers between devices: 52.7 us -> 53.9 us  [local(): piece = lax.ppermute(held[chunk][chain], 'grp', pairs)]
  transfers between devices with their start and end apart: 58 -> 64, of which waited for: 21 -> 19; matrix products, arithmetic and copies ran while one was open for 2% -> 3% of each run, Pallas kernels for 14% -> 16%
where the time goes in v3:
time: 390 us; the launch traced here: 388 us
  waiting for transfers between devices  183 us (47%)
  starting transfers between devices  99.3 us (25%)
  Pallas kernels  76.5 us (20%)
  blocking collectives  8.32 us (2%)
  local copies, waits for them, and re-layouts  7.62 us (2%)
  other arithmetic  6.74 us (2%)
  matrix products  5.23 us (1%)
    ppermute x36, waiting for transfers between devices, swap(): return lax.ppermute(value, 'dev', [(i, i ^ mask) for i in range(devices)])  69.7 us
    ppermute x7, waiting for transfers between devices, shift(): lax.ppermute(value, 'grp', [(i, (i + step) % groups) for i in range(group...  58 us
    ppermute x20, waiting for transfers between devices, local(): piece = lax.ppermute(held[chunk][chain], 'grp', pairs)  55.2 us
    ppermute x20, starting transfers between devices, local(): piece = lax.ppermute(held[chunk][chain], 'grp', pairs)  53.9 us
    ppermute x36, starting transfers between devices, swap(): return lax.ppermute(value, 'dev', [(i, i ^ mask) for i in range(devices)])  28.5 us
    pallas_call x12, Pallas kernels, place(): pl.pallas_call(kernel, grid_spec=pltpu.PrefetchScalarGridSpec(num_scalar_...  24.2 us
    pallas_call x5, Pallas kernels, pick_transposed(): pl.pallas_call(kernel, grid_spec=pltpu.PrefetchScalarGridSpec(num_scalar_...  19.2 us
    pallas_call x3, Pallas kernels, accumulate(): pl.pallas_call(kernel, grid=(tiles,), in_specs=([block] if acc is not Non...  14 us
  transfers between devices with their start and end apart: 64, of which 19 were waited for; matrix products, arithmetic and copies ran while one was open for 3% of the time, Pallas kernels for 16%

profile of v3, /device:TPU:0, one launch (start us, length us, event | category | flops | bytes accessed | tf_op | source)
XLA Modules:
  0.0 388.0 jit_solution(306840756592039403)
XLA Ops:
  0.6 3.2 pick.2
  3.8 4.0 %collective-permute-start.9 = (bf16[128,2048]{1,0:T(8,128)(2,1)}, bf16[128,2048]{1,0:T(8,128)(2,1)S(1)}, u32[]{:S(2)}, u32[]{:S(2)}) collective-permute-start(bf16[128,2048]{1,0:T(8,128)(2,1)} %get-tuple-element.23.refs_1_), channel_id=1, source_target_pairs={{0,6},{1,7},{2,4},{3,5},{4,2},{5,3},{6,0},{7,1},{8,14},{9,15},{10,... | collective-permute-start | bytes 1572872 | tf_op jit(solution)/shard_map/ppermute | solution.py:371
  8.5 2.5 pick.3
  11.0 2.0 collective-permute-start.12
  13.0 7.8 %collective-permute-done.9.refs_7_ = bf16[128,2048]{1,0:T(8,128)(2,1)S(1)} collective-permute-done((bf16[128,2048]{1,0:T(8,128)(2,1)}, bf16[128,2048]{1,0:T(8,128)(2,1)S(1)}, u32[]{:S(2)}, u32[]{:S(2)}) %collective-permute-start.9) | collective-permute-done | bytes 524320 | tf_op jit(solution)/shard_map/ppermute | solution.py:371
  20.9 4.1 %collective-permute-start.21 = (bf16[128,2048]{1,0:T(8,128)(2,1)}, bf16[128,2048]{1,0:T(8,128)(2,1)S(1)}, u32[]{:S(2)}, u32[]{:S(2)}) collective-permute-start(bf16[128,2048]{1,0:T(8,128)(2,1)} %get-tuple-element.24), channel_id=1, source_target_pairs={{0,24},{8,0},{16,8},{24,16},{1,25},{9,1},{17,9},{25,17},{2,26},{10... | collective-permute-start | bytes 1572872 | tf_op jit(solution)/shard_map/ppermute | solution.py:376
  24.9 3.7 pick_transposed.8
  28.6 2.9 collective-permute-done.5.refs_3_
  31.5 2.6 collective-permute-start.29
  34.9 4.2 %collective-permute-done.21.refs_2_ = bf16[128,2048]{1,0:T(8,128)(2,1)S(1)} collective-permute-done((bf16[128,2048]{1,0:T(8,128)(2,1)}, bf16[128,2048]{1,0:T(8,128)(2,1)S(1)}, u32[]{:S(2)}, u32[]{:S(2)}) %collective-permute-start.21) | collective-permute-done | bytes 524320 | tf_op jit(solution)/shard_map/ppermute | solution.py:376
  39.1 4.3 %pick_transposed.6 = bf16[512,1024]{1,0:T(8,128)(2,1)} custom-call(s32[4]{0:T(128)} %owner_ref.45, bf16[4,1024,512]{2,1,0:T(8,128)(2,1)} %value_ref.13), custom_call_target="tpu_custom_call" | custom-call | bytes 2097152 | tf_op jit(solution)/shard_map/pick_transposed/pallas_call | solution.py:85
  43.4 51.9 %collective-permute-done.30.refs_0_ = bf16[128,2048]{1,0:T(8,128)(2,1)S(1)} collective-permute-done((bf16[128,2048]{1,0:T(8,128)(2,1)}, bf16[128,2048]{1,0:T(8,128)(2,1)S(1)}, u32[]{:S(2)}, u32[]{:S(2)}) %collective-permute-start.30) | collective-permute-done | bytes 524320 | tf_op jit(solution)/shard_map/ppermute | solution.py:376
  95.3 1.6 collective-permute-start.14
  96.9 1.5 collective-permute-start.16
  98.9 11.6 %collective-permute-done.14.refs_4_ = bf16[128,2048]{1,0:T(8,128)(2,1)} collective-permute-done((bf16[128,2048]{1,0:T(8,128)(2,1)}, bf16[128,2048]{1,0:T(8,128)(2,1)}, u32[]{:S(2)}, u32[]{:S(2)}) %collective-permute-start.14) | collective-permute-done | bytes 524320 | tf_op jit(solution)/shard_map/ppermute | solution.py:371
  110.5 1.5 collective-permute-start.23
  112.0 10.2 %collective-permute-done.16.refs_6_ = bf16[128,2048]{1,0:T(8,128)(2,1)} collective-permute-done((bf16[128,2048]{1,0:T(8,128)(2,1)}, bf16[128,2048]{1,0:T(8,128)(2,1)}, u32[]{:S(2)}, u32[]{:S(2)}) %collective-permute-start.16) | collective-permute-done | bytes 524320 | tf_op jit(solution)/shard_map/ppermute | solution.py:371
  122.2 2.5 collective-permute-start.25
  125.5 3.5 collective-permute-start.36
  129.0 3.9 %collective-permute-done.23.refs_4_ = bf16[128,2048]{1,0:T(8,128)(2,1)S(1)} collective-permute-done((bf16[128,2048]{1,0:T(8,128)(2,1)}, bf16[128,2048]{1,0:T(8,128)(2,1)S(1)}, u32[]{:S(2)}, u32[]{:S(2)}) %collective-permute-start.23) | collective-permute-done | bytes 524320 | tf_op jit(solution)/shard_map/ppermute | solution.py:371
  132.9 2.4 collective-permute-start.27
  135.3 2.3 collective-permute-done.25.refs_6_
  137.7 6.5 %collective-permute-done.32.refs_2_ = bf16[128,2048]{1,0:T(8,128)(2,1)S(1)} collective-permute-done((bf16[128,2048]{1,0:T(8,128)(2,1)S(1)}, bf16[128,2048]{1,0:T(8,128)(2,1)S(1)}, u32[]{:S(2)}, u32[]{:S(2)}) %collective-permute-start.32) | collective-permute-done | bytes 524320 | tf_op jit(solution)/shard_map/ppermute | solution.py:371
  144.1 22.8 %collective-permute-done.34.refs_4_ = bf16[128,2048]{1,0:T(8,128)(2,1)} collective-permute-done((bf16[128,2048]{1,0:T(8,128)(2,1)S(1)}, bf16[128,2048]{1,0:T(8,128)(2,1)}, u32[]{:S(2)}, u32[]{:S(2)}) %collective-permute-start.34) | collective-permute-done | bytes 524320 | tf_op jit(solution)/shard_map/ppermute | solution.py:371
  167.5 4.3 %pick_transposed.7 = bf16[512,1024]{1,0:T(8,128)(2,1)} custom-call(s32[4]{0:T(128)} %owner_ref.45, bf16[4,1024,512]{2,1,0:T(8,128)(2,1)} %value_ref.13), custom_call_target="tpu_custom_call" | custom-call | bytes 2097152 | tf_op jit(solution)/shard_map/pick_transposed/pallas_call | solution.py:85
  171.8 3.5 collective-permute-start.20
  176.3 4.4 %pick_transposed.5.refs_0_ = bf16[512,1024]{1,0:T(8,128)(2,1)} custom-call(s32[4]{0:T(128)} %owner_ref.45, bf16[4,1024,512]{2,1,0:T(8,128)(2,1)} %value_ref.13), custom_call_target="tpu_custom_call" | custom-call | bytes 2097152 | tf_op jit(solution)/shard_map/pick_transposed/pallas_call | solution.py:85
  180.7 2.6 pick_transposed.9
  189.0 4.4 %accumulate.3.refs_0_ = f32[512,2048]{1,0:T(8,128)S(1)} custom-call(bf16[512,1024]{1,0:T(8,128)(2,1)S(1)} %copy-done.2, bf16[128,2048]{1,0:T(8,128)(2,1)S(1)} %copy-done.3, bf16[128,2048]{1,0:T(8,128)(2,1)S(1)} %copy-done.11, bf16[128,2048]{1,0:T(8,128)(2,1)S(1)} %copy-done.7, bf16[128,2048]{1,0:T(8,128)(2,1)} %collective-permute-done.6.refs_4_, ...), custom_call_target="tpu_custom_call" | custom-call | flops 2147483648 | bytes 13631488 | tf_op jit(solution)/shard_map/accumulate/pallas_call | solution.py:139
  193.5 2.0 arrange.1
  196.2 3.0 fusion
  199.3 4.9 %accumulate.4.refs_0_ = f32[512,2048]{1,0:T(8,128)S(1)} custom-call(f32[512,2048]{1,0:T(8,128)S(1)} %accumulate.3.refs_0_, bf16[512,1024]{1,0:T(8,128)(2,1)S(1)} %collective-permute-done.11.refs_1_, bf16[128,2048]{1,0:T(8,128)(2,1)} %collective-permute-done.12.refs_2_, bf16[128,2048]{1,0:T(8,128)(2,1)S(1)} %copy-done.25, ...), custom_call_target="tpu_custom_call" | custom-call | flops 2147483648 | bytes 13631488 | tf_op jit(solution)/shard_map/accumulate/pallas_call | solution.py:139
  204.7 4.7 %accumulate.5 = f32[512,2048]{1,0:T(8,128)S(1)} custom-call(f32[512,2048]{1,0:T(8,128)S(1)} %accumulate.4.refs_0_, bf16[512,1024]{1,0:T(8,128)(2,1)S(1)} %collective-permute-done.20.refs_1_, bf16[128,2048]{1,0:T(8,128)(2,1)S(1)} %copy-done.19, bf16[128,2048]{1,0:T(8,128)(2,1)} %collective-permute-done.22.refs_3_, bf16[128,2048]{1,0:T(8,128)(2,1)S(1)} %copy-done.21, ...), custom_call_target="tpu_custom_call" | custom-call | flops 2147483648 | bytes 13631488 | tf_op jit(solution)/shard_map/accumulate/pallas_call | solution.py:139
  210.4 1.9 collective-permute-done.38
  214.6 1.5 collective-permute-start.1
  216.2 1.9 collective-permute-start.3
  219.7 1.9 collective-permute-start.42
  223.3 1.8 update.4
  225.1 2.9 update.5
  228.0 4.9 %update.6 = (bf16[256,2048]{1,0:T(8,128)(2,1)}, bf16[4,512,2048]{2,1,0:T(8,128)(2,1)}, f32[512,2048]{1,0:T(8,128)}, f32[512,2048]{1,0:T(8,128)}) custom-call(s32[4]{0:T(128)S(1)} %copy-done.26, f32[1,128]{1,0:T(1,128)S(1)} %bitcast_add_fusion.1.refs_0_, ...), custom_call_target="tpu_custom_call", output_to_operand_aliasing={{1}: (12, {}), {2}: (13, {}), {3}: (14, {})} | custom-call | flops 4194304 | bytes 12582912 | tf_op jit(solution)/shard_map/update/pallas_call | solution.py:227
  233.6 22.7 %collective-permute-done.45.refs_0_ = bf16[256,2048]{1,0:T(8,128)(2,1)S(1)} collective-permute-done((bf16[256,2048]{1,0:T(8,128)(2,1)}, bf16[256,2048]{1,0:T(8,128)(2,1)S(1)}, u32[]{:S(2)}, u32[]{:S(2)}) %collective-permute-start.45) | collective-permute-done | bytes 1048608 | tf_op jit(solution)/shard_map/ppermute | solution.py:436
  257.2 2.7 collective-permute-start.43
  260.0 1.9 update.7
  261.9 2.0 collective-permute-start.44
  263.9 3.2 collective-permute-done.43.refs_0_
  268.5 4.4 %collective-permute-done.46.refs_0_ = bf16[64,2048]{1,0:T(8,128)(2,1)} collective-permute-done((bf16[64,2048]{1,0:T(8,128)(2,1)}, bf16[64,2048]{1,0:T(8,128)(2,1)}, u32[]{:S(2)}, u32[]{:S(2)}) %collective-permute-start.46) | collective-permute-done | bytes 262176 | tf_op jit(solution)/shard_map/ppermute | solution.py:436
  276.8 19.1 %collective-permute-start.48 = (bf16[64,2048]{1,0:T(8,128)(2,1)}, bf16[64,2048]{1,0:T(8,128)(2,1)}, u32[]{:S(2)}, u32[]{:S(2)}) collective-permute-start(bf16[64,2048]{1,0:T(8,128)(2,1)} %collective-permute-done.47.refs_0_), channel_id=1, source_target_pairs={{0,8},{16,24},{8,0},{24,16},{1,9},{17,25},{9,1},{25,17},{2,10},{18... | collective-permute-start | bytes 786440 | tf_op jit(solution)/shard_map/ppermute | solution.py:436
  297.4 1.7 collective-permute-start.52
  299.1 8.3 %all_to_all.11 = s32[8,2,1]{1,2,0:T(1,128)S(1)} all-to-all(s32[8,2,1]{1,2,0:T(1,128)S(1)} %bitcast.49), channel_id=1, replica_groups=mesh['grp'=4,'dev'=8] {'dev'}, dimensions={0} | all-to-all | bytes 128 | tf_op jit(solution)/shard_map/all_to_all | solution.py:456
  307.5 4.1 %all-to-all-start.1 = ((bf16[16,128,128]{2,1,0:T(8,128)(2,1)}), bf16[16,128,128]{2,1,0:T(8,128)(2,1)}, u32[]{:S(2)}, u32[]{:S(2)}) async-start(bf16[16,128,128]{2,1,0:T(8,128)(2,1)} %bitcast.48), calls=%async_computation.1 | async-start | bytes 1048576 | tf_op jit(solution)/shard_map/all_to_all | solution.py:457
  314.8 2.1 collective-permute-start.60
  318.6 9.0 %collective-permute-start.58 = (bf16[128,2048]{1,0:T(8,128)(2,1)}, bf16[128,2048]{1,0:T(8,128)(2,1)}, u32[]{:S(2)}, u32[]{:S(2)}) collective-permute-start(bf16[128,2048]{1,0:T(8,128)(2,1)} %collective-permute-done.57.refs_0_), channel_id=1, source_target_pairs={{0,8},{16,24},{8,0},{24,16},{1,9},{17,25},{9,1},{25,17},{2,10},{18... | collective-permute-start | bytes 1572872 | tf_op jit(solution)/shard_map/ppermute | solution.py:436
  327.5 1.6 multiply_reduce_fusion.2
  329.1 5.2 %collective-permute-start.54 = (bf16[64,2048]{1,0:T(8,128)(2,1)}, bf16[64,2048]{1,0:T(8,128)(2,1)S(1)}, u32[]{:S(2)}, u32[]{:S(2)}) collective-permute-start(bf16[64,2048]{1,0:T(8,128)(2,1)} %collective-permute-done.53.refs_0_), channel_id=1, source_target_pairs={{0,8},{16,24},{8,0},{24,16},{1,9},{17,25},{9,1},{25,17},{2,10},{18... | collective-permute-start | bytes 786440 | tf_op jit(solution)/shard_map/ppermute | solution.py:436
  334.3 23.4 %collective-permute-done.50.refs_1_ = bf16[128,2048]{1,0:T(8,128)(2,1)} collective-permute-done((bf16[128,2048]{1,0:T(8,128)(2,1)}, bf16[128,2048]{1,0:T(8,128)(2,1)}, u32[]{:S(2)}, u32[]{:S(2)}) %collective-permute-start.50) | collective-permute-done | bytes 524320 | tf_op jit(solution)/shard_map/ppermute | solution.py:436
  357.7 1.7 collective-permute-start.56
  363.4 2.4 place.13.weights_ref
  365.8 1.6 place.14.weights_ref
  367.4 2.2 place.15.weights_ref
  369.7 2.2 place.16.weights_ref
  371.9 2.4 place.17.weights_ref
  374.3 2.8 place.18.weights_ref
  381.2 2.4 place.21.weights_ref
  383.7 2.8 place.22.weights_ref
  (174 shorter events, 40.7 us)
Async XLA Ops:
  3.8 17.0 %collective-permute-start.9 = (bf16[128,2048]{1,0:T(8,128)(2,1)}, bf16[128,2048]{1,0:T(8,128)(2,1)S(1)}, u32[]{:S(2)}, u32[]{:S(2)}) collective-permute-start(bf16[128,2048]{1,0:T(8,128)(2,1)} %get-tuple-element.23.refs_1_), channel_id=1, source_target_pairs={{0,6},{1,7},{2,4},{3,5},{4,2},{5,3},{6,0},{7,1},{8,14},{9,15},{10,... | collective-permute-start | bytes 1572872 | tf_op jit(solution)/shard_map/ppermute | solution.py:371
  7.8 23.7 %collective-permute-start.5 = (bf16[128,2048]{1,0:T(8,128)(2,1)}, bf16[128,2048]{1,0:T(8,128)(2,1)S(1)}, u32[]{:S(2)}, u32[]{:S(2)}) collective-permute-start(bf16[128,2048]{1,0:T(8,128)(2,1)} %get-tuple-element.23.refs_1_), channel_id=1, source_target_pairs={{0,2},{1,3},{2,0},{3,1},{4,6},{5,7},{6,4},{7,5},{8,10},{9,11},{10,... | collective-permute-start | bytes 1572872 | tf_op jit(solution)/shard_map/ppermute | solution.py:371
  8.4 25.7 %collective-permute-start.7 = (bf16[128,2048]{1,0:T(8,128)(2,1)}, bf16[128,2048]{1,0:T(8,128)(2,1)S(1)}, u32[]{:S(2)}, u32[]{:S(2)}) collective-permute-start(bf16[128,2048]{1,0:T(8,128)(2,1)} %get-tuple-element.23.refs_1_), channel_id=1, source_target_pairs={{0,4},{1,5},{2,6},{3,7},{4,0},{5,1},{6,2},{7,3},{8,12},{9,13},{10,... | collective-permute-start | bytes 1572872 | tf_op jit(solution)/shard_map/ppermute | solution.py:371
  8.5 26.0 %collective-permute-start.4 = (bf16[128,2048]{1,0:T(8,128)(2,1)}, bf16[128,2048]{1,0:T(8,128)(2,1)S(1)}, u32[]{:S(2)}, u32[]{:S(2)}) collective-permute-start(bf16[128,2048]{1,0:T(8,128)(2,1)} %get-tuple-element.23.refs_1_), channel_id=1, source_target_pairs={{0,1},{1,0},{2,3},{3,2},{4,5},{5,4},{6,7},{7,6},{8,9},{9,8},{10,11... | collective-permute-start | bytes 1572872 | tf_op jit(solution)/shard_map/ppermute | solution.py:371
  11.0 23.4 %collective-permute-start.12 = (bf16[128,2048]{1,0:T(8,128)(2,1)}, bf16[128,2048]{1,0:T(8,128)(2,1)}, u32[]{:S(2)}, u32[]{:S(2)}) collective-permute-start(bf16[128,2048]{1,0:T(8,128)(2,1)} %pick.3), channel_id=1, source_target_pairs={{0,8},{8,16},{16,24},{24,0},{1,9},{9,17},{17,25},{25,1},{2,10},{10... | collective-permute-start | bytes 1572872 | tf_op jit(solution)/shard_map/ppermute | solution.py:376
  20.9 18.3 %collective-permute-start.21 = (bf16[128,2048]{1,0:T(8,128)(2,1)}, bf16[128,2048]{1,0:T(8,128)(2,1)S(1)}, u32[]{:S(2)}, u32[]{:S(2)}) collective-permute-start(bf16[128,2048]{1,0:T(8,128)(2,1)} %get-tuple-element.24), channel_id=1, source_target_pairs={{0,24},{8,0},{16,8},{24,16},{1,25},{9,1},{17,9},{25,17},{2,26},{10... | collective-permute-start | bytes 1572872 | tf_op jit(solution)/shard_map/ppermute | solution.py:376
  31.5 63.8 %collective-permute-start.29 = (bf16[512,768]{1,0:T(8,128)(2,1)}, bf16[512,768]{1,0:T(8,128)(2,1)}, u32[]{:S(2)}, u32[]{:S(2)}) collective-permute-start(bf16[512,768]{1,0:T(8,128)(2,1)} %pick_transposed.8), channel_id=1, source_target_pairs={{0,16},{8,24},{16,0},{24,8},{1,17},{9,25},{17,1},{25,9},{2,18},{10... | collective-permute-start | bytes 2359304 | tf_op jit(solution)/shard_map/ppermute | solution.py:376
  34.1 61.2 %collective-permute-start.30 = (bf16[128,2048]{1,0:T(8,128)(2,1)}, bf16[128,2048]{1,0:T(8,128)(2,1)S(1)}, u32[]{:S(2)}, u32[]{:S(2)}) collective-permute-start(bf16[128,2048]{1,0:T(8,128)(2,1)} %get-tuple-element.25), channel_id=1, source_target_pairs={{0,16},{8,24},{16,0},{24,8},{1,17},{9,25},{17,1},{25,9},{2,18},{10... | collective-permute-start | bytes 1572872 | tf_op jit(solution)/shard_map/ppermute | solution.py:376
  34.4 62.4 %collective-permute-start.10 = (bf16[128,2048]{1,0:T(8,128)(2,1)S(1)}, bf16[128,2048]{1,0:T(8,128)(2,1)S(1)}, u32[]{:S(2)}, u32[]{:S(2)}) collective-permute-start(bf16[128,2048]{1,0:T(8,128)(2,1)S(1)} %collective-permute-done.9.refs_7_), channel_id=1, source_target_pairs={{0,1},{1,0},{2,3},{3,2},{4,5},{5,4},{6,7},{7,6},{8,9},{9,8},{10,11... | collective-permute-start | bytes 1572872 | tf_op jit(solution)/shard_map/ppermute | solution.py:371
  34.4 63.9 %collective-permute-start.6 = (bf16[128,2048]{1,0:T(8,128)(2,1)S(1)}, bf16[128,2048]{1,0:T(8,128)(2,1)}, u32[]{:S(2)}, u32[]{:S(2)}) collective-permute-start(bf16[128,2048]{1,0:T(8,128)(2,1)S(1)} %collective-permute-done.5.refs_3_), channel_id=1, source_target_pairs={{0,1},{1,0},{2,3},{3,2},{4,5},{5,4},{6,7},{7,6},{8,9},{9,8},{10,11... | collective-permute-start | bytes 1572872 | tf_op jit(solution)/shard_map/ppermute | solution.py:371
  39.1 59.7 %collective-permute-start.8 = (bf16[128,2048]{1,0:T(8,128)(2,1)S(1)}, bf16[128,2048]{1,0:T(8,128)(2,1)}, u32[]{:S(2)}, u32[]{:S(2)}) collective-permute-start(bf16[128,2048]{1,0:T(8,128)(2,1)S(1)} %collective-permute-done.7.refs_5_), channel_id=1, source_target_pairs={{0,1},{1,0},{2,3},{3,2},{4,5},{5,4},{6,7},{7,6},{8,9},{9,8},{10,11... | collective-permute-start | bytes 1572872 | tf_op jit(solution)/shard_map/ppermute | solution.py:371
  95.3 30.2 %collective-permute-start.11 = (bf16[512,1024]{1,0:T(8,128)(2,1)}, bf16[512,1024]{1,0:T(8,128)(2,1)S(1)}, u32[]{:S(2)}, u32[]{:S(2)}) collective-permute-start(bf16[512,1024]{1,0:T(8,128)(2,1)} %pick_transposed.6), channel_id=1, source_target_pairs={{0,8},{8,16},{16,24},{24,0},{1,9},{9,17},{17,25},{25,1},{2,10},{10... | collective-permute-start | bytes 3145736 | tf_op jit(solution)/shard_map/ppermute | solution.py:376
  95.3 15.2 %collective-permute-start.14 = (bf16[128,2048]{1,0:T(8,128)(2,1)}, bf16[128,2048]{1,0:T(8,128)(2,1)}, u32[]{:S(2)}, u32[]{:S(2)}) collective-permute-start(bf16[128,2048]{1,0:T(8,128)(2,1)} %collective-permute-done.12.refs_2_), channel_id=1, source_target_pairs={{0,2},{1,3},{2,0},{3,1},{4,6},{5,7},{6,4},{7,5},{8,10},{9,11},{10,... | collective-permute-start | bytes 1572872 | tf_op jit(solution)/shard_map/ppermute | solution.py:371
  96.9 25.3 %collective-permute-start.16 = (bf16[128,2048]{1,0:T(8,128)(2,1)}, bf16[128,2048]{1,0:T(8,128)(2,1)}, u32[]{:S(2)}, u32[]{:S(2)}) collective-permute-start(bf16[128,2048]{1,0:T(8,128)(2,1)} %collective-permute-done.12.refs_2_), channel_id=1, source_target_pairs={{0,4},{1,5},{2,6},{3,7},{4,0},{5,1},{6,2},{7,3},{8,12},{9,13},{10,... | collective-permute-start | bytes 1572872 | tf_op jit(solution)/shard_map/ppermute | solution.py:371
  98.4 26.3 %collective-permute-start.18 = (bf16[128,2048]{1,0:T(8,128)(2,1)}, bf16[128,2048]{1,0:T(8,128)(2,1)}, u32[]{:S(2)}, u32[]{:S(2)}) collective-permute-start(bf16[128,2048]{1,0:T(8,128)(2,1)} %collective-permute-done.12.refs_2_), channel_id=1, source_target_pairs={{0,6},{1,7},{2,4},{3,5},{4,2},{5,3},{6,0},{7,1},{8,14},{9,15},{10,... | collective-permute-start | bytes 1572872 | tf_op jit(solution)/shard_map/ppermute | solution.py:371
  98.9 25.8 %collective-permute-start.13 = (bf16[128,2048]{1,0:T(8,128)(2,1)}, bf16[128,2048]{1,0:T(8,128)(2,1)S(1)}, u32[]{:S(2)}, u32[]{:S(2)}) collective-permute-start(bf16[128,2048]{1,0:T(8,128)(2,1)} %collective-permute-done.12.refs_2_), channel_id=1, source_target_pairs={{0,1},{1,0},{2,3},{3,2},{4,5},{5,4},{6,7},{7,6},{8,9},{9,8},{10,11... | collective-permute-start | bytes 1572872 | tf_op jit(solution)/shard_map/ppermute | solution.py:371
  110.5 22.4 %collective-permute-start.23 = (bf16[128,2048]{1,0:T(8,128)(2,1)}, bf16[128,2048]{1,0:T(8,128)(2,1)S(1)}, u32[]{:S(2)}, u32[]{:S(2)}) collective-permute-start(bf16[128,2048]{1,0:T(8,128)(2,1)} %copy-done.18), channel_id=1, source_target_pairs={{0,2},{1,3},{2,0},{3,1},{4,6},{5,7},{6,4},{7,5},{8,10},{9,11},{10,... | collective-permute-start | bytes 1572872 | tf_op jit(solution)/shard_map/ppermute | solution.py:371
  122.2 15.5 %collective-permute-start.25 = (bf16[128,2048]{1,0:T(8,128)(2,1)}, bf16[128,2048]{1,0:T(8,128)(2,1)S(1)}, u32[]{:S(2)}, u32[]{:S(2)}) collective-permute-start(bf16[128,2048]{1,0:T(8,128)(2,1)} %copy-done.18), channel_id=1, source_target_pairs={{0,4},{1,5},{2,6},{3,7},{4,0},{5,1},{6,2},{7,3},{8,12},{9,13},{10,... | collective-permute-start | bytes 1572872 | tf_op jit(solution)/shard_map/ppermute | solution.py:371
  124.7 19.4 %collective-permute-start.32 = (bf16[128,2048]{1,0:T(8,128)(2,1)S(1)}, bf16[128,2048]{1,0:T(8,128)(2,1)S(1)}, u32[]{:S(2)}, u32[]{:S(2)}) collective-permute-start(bf16[128,2048]{1,0:T(8,128)(2,1)S(1)} %collective-permute-done.30.refs_0_), channel_id=1, source_target_pairs={{0,2},{1,3},{2,0},{3,1},{4,6},{5,7},{6,4},{7,5},{8,10},{9,11},{10,... | collective-permute-start | bytes 1572872 | tf_op jit(solution)/shard_map/ppermute | solution.py:371
  125.5 41.4 %collective-permute-start.34 = (bf16[128,2048]{1,0:T(8,128)(2,1)S(1)}, bf16[128,2048]{1,0:T(8,128)(2,1)}, u32[]{:S(2)}, u32[]{:S(2)}) collective-permute-start(bf16[128,2048]{1,0:T(8,128)(2,1)S(1)} %collective-permute-done.30.refs_0_), channel_id=1, source_target_pairs={{0,4},{1,5},{2,6},{3,7},{4,0},{5,1},{6,2},{7,3},{8,12},{9,13},{10,... | collective-permute-start | bytes 1572872 | tf_op jit(solution)/shard_map/ppermute | solution.py:371
  125.5 41.4 %collective-permute-start.36 = (bf16[128,2048]{1,0:T(8,128)(2,1)S(1)}, bf16[128,2048]{1,0:T(8,128)(2,1)}, u32[]{:S(2)}, u32[]{:S(2)}) collective-permute-start(bf16[128,2048]{1,0:T(8,128)(2,1)S(1)} %collective-permute-done.30.refs_0_), channel_id=1, source_target_pairs={{0,6},{1,7},{2,4},{3,5},{4,2},{5,3},{6,0},{7,1},{8,14},{9,15},{10,... | collective-permute-start | bytes 1572872 | tf_op jit(solution)/shard_map/ppermute | solution.py:371
  132.9 38.9 %collective-permute-start.27 = (bf16[128,2048]{1,0:T(8,128)(2,1)}, bf16[128,2048]{1,0:T(8,128)(2,1)}, u32[]{:S(2)}, u32[]{:S(2)}) collective-permute-start(bf16[128,2048]{1,0:T(8,128)(2,1)} %copy-done.18), channel_id=1, source_target_pairs={{0,6},{1,7},{2,4},{3,5},{4,2},{5,3},{6,0},{7,1},{8,14},{9,15},{10,... | collective-permute-start | bytes 1572872 | tf_op jit(solution)/shard_map/ppermute | solution.py:371
  137.7 37.7 %collective-permute-start.31 = (bf16[128,2048]{1,0:T(8,128)(2,1)S(1)}, bf16[128,2048]{1,0:T(8,128)(2,1)}, u32[]{:S(2)}, u32[]{:S(2)}) collective-permute-start(bf16[128,2048]{1,0:T(8,128)(2,1)S(1)} %collective-permute-done.30.refs_0_), channel_id=1, source_target_pairs={{0,1},{1,0},{2,3},{3,2},{4,5},{5,4},{6,7},{7,6},{8,9},{9,8},{10,11... | collective-permute-start | bytes 1572872 | tf_op jit(solution)/shard_map/ppermute | solution.py:371
  144.1 31.2 %collective-permute-start.33 = (bf16[128,2048]{1,0:T(8,128)(2,1)S(1)}, bf16[128,2048]{1,0:T(8,128)(2,1)}, u32[]{:S(2)}, u32[]{:S(2)}) collective-permute-start(bf16[128,2048]{1,0:T(8,128)(2,1)S(1)} %collective-permute-done.32.refs_2_), channel_id=1, source_target_pairs={{0,1},{1,0},{2,3},{3,2},{4,5},{5,4},{6,7},{7,6},{8,9},{9,8},{10,11... | collective-permute-start | bytes 1572872 | tf_op jit(solution)/shard_map/ppermute | solution.py:371
  166.9 8.9 %collective-permute-start.35 = (bf16[128,2048]{1,0:T(8,128)(2,1)}, bf16[128,2048]{1,0:T(8,128)(2,1)}, u32[]{:S(2)}, u32[]{:S(2)}) collective-permute-start(bf16[128,2048]{1,0:T(8,128)(2,1)} %collective-permute-done.34.refs_4_), channel_id=1, source_target_pairs={{0,1},{1,0},{2,3},{3,2},{4,5},{5,4},{6,7},{7,6},{8,9},{9,8},{10,11... | collective-permute-start | bytes 1572872 | tf_op jit(solution)/shard_map/ppermute | solution.py:371
  166.9 16.3 %collective-permute-start.37 = (bf16[128,2048]{1,0:T(8,128)(2,1)}, bf16[128,2048]{1,0:T(8,128)(2,1)}, u32[]{:S(2)}, u32[]{:S(2)}) collective-permute-start(bf16[128,2048]{1,0:T(8,128)(2,1)} %collective-permute-done.36.refs_6_), channel_id=1, source_target_pairs={{0,1},{1,0},{2,3},{3,2},{4,5},{5,4},{6,7},{7,6},{8,9},{9,8},{10,11... | collective-permute-start | bytes 1572872 | tf_op jit(solution)/shard_map/ppermute | solution.py:371
  171.8 32.4 %collective-permute-start.20 = (bf16[512,1024]{1,0:T(8,128)(2,1)}, bf16[512,1024]{1,0:T(8,128)(2,1)S(1)}, u32[]{:S(2)}, u32[]{:S(2)}) collective-permute-start(bf16[512,1024]{1,0:T(8,128)(2,1)} %pick_transposed.7), channel_id=1, source_target_pairs={{0,24},{8,0},{16,8},{24,16},{1,25},{9,1},{17,9},{25,17},{2,26},{10... | collective-permute-start | bytes 3145736 | tf_op jit(solution)/shard_map/ppermute | solution.py:376
  175.3 20.2 %collective-permute-start.22 = (bf16[128,2048]{1,0:T(8,128)(2,1)}, bf16[128,2048]{1,0:T(8,128)(2,1)}, u32[]{:S(2)}, u32[]{:S(2)}) collective-permute-start(bf16[128,2048]{1,0:T(8,128)(2,1)} %copy-done.18), channel_id=1, source_target_pairs={{0,1},{1,0},{2,3},{3,2},{4,5},{5,4},{6,7},{7,6},{8,9},{9,8},{10,11... | collective-permute-start | bytes 1572872 | tf_op jit(solution)/shard_map/ppermute | solution.py:371
  175.3 20.3 %collective-permute-start.15 = (bf16[128,2048]{1,0:T(8,128)(2,1)}, bf16[128,2048]{1,0:T(8,128)(2,1)}, u32[]{:S(2)}, u32[]{:S(2)}) collective-permute-start(bf16[128,2048]{1,0:T(8,128)(2,1)} %collective-permute-done.14.refs_4_), channel_id=1, source_target_pairs={{0,1},{1,0},{2,3},{3,2},{4,5},{5,4},{6,7},{7,6},{8,9},{9,8},{10,11... | collective-permute-start | bytes 1572872 | tf_op jit(solution)/shard_map/ppermute | solution.py:371
  175.8 20.2 %collective-permute-start.17 = (bf16[128,2048]{1,0:T(8,128)(2,1)}, bf16[128,2048]{1,0:T(8,128)(2,1)}, u32[]{:S(2)}, u32[]{:S(2)}) collective-permute-start(bf16[128,2048]{1,0:T(8,128)(2,1)} %collective-permute-done.16.refs_6_), channel_id=1, source_target_pairs={{0,1},{1,0},{2,3},{3,2},{4,5},{5,4},{6,7},{7,6},{8,9},{9,8},{10,11... | collective-permute-start | bytes 1572872 | tf_op jit(solution)/shard_map/ppermute | solution.py:371
  183.3 15.9 %collective-permute-start.19 = (bf16[128,2048]{1,0:T(8,128)(2,1)}, bf16[128,2048]{1,0:T(8,128)(2,1)S(1)}, u32[]{:S(2)}, u32[]{:S(2)}) collective-permute-start(bf16[128,2048]{1,0:T(8,128)(2,1)} %collective-permute-done.18.refs_8_), channel_id=1, source_target_pairs={{0,1},{1,0},{2,3},{3,2},{4,5},{5,4},{6,7},{7,6},{8,9},{9,8},{10,11... | collective-permute-start | bytes 1572872 | tf_op jit(solution)/shard_map/ppermute | solution.py:371
  195.5 9.2 %collective-permute-start.24 = (bf16[128,2048]{1,0:T(8,128)(2,1)S(1)}, bf16[128,2048]{1,0:T(8,128)(2,1)S(1)}, u32[]{:S(2)}, u32[]{:S(2)}) collective-permute-start(bf16[128,2048]{1,0:T(8,128)(2,1)S(1)} %copy-done.21), channel_id=1, source_target_pairs={{0,1},{1,0},{2,3},{3,2},{4,5},{5,4},{6,7},{7,6},{8,9},{9,8},{10,11... | collective-permute-start | bytes 1572872 | tf_op jit(solution)/shard_map/ppermute | solution.py:371
  195.6 9.0 %collective-permute-start.26 = (bf16[128,2048]{1,0:T(8,128)(2,1)S(1)}, bf16[128,2048]{1,0:T(8,128)(2,1)S(1)}, u32[]{:S(2)}, u32[]{:S(2)}) collective-permute-start(bf16[128,2048]{1,0:T(8,128)(2,1)S(1)} %copy-done.23), channel_id=1, source_target_pairs={{0,1},{1,0},{2,3},{3,2},{4,5},{5,4},{6,7},{7,6},{8,9},{9,8},{10,11... | collective-permute-start | bytes 1572872 | tf_op jit(solution)/shard_map/ppermute | solution.py:371
  196.1 8.6 %collective-permute-start.28 = (bf16[128,2048]{1,0:T(8,128)(2,1)}, bf16[128,2048]{1,0:T(8,128)(2,1)S(1)}, u32[]{:S(2)}, u32[]{:S(2)}) collective-permute-start(bf16[128,2048]{1,0:T(8,128)(2,1)} %collective-permute-done.27.refs_8_), channel_id=1, source_target_pairs={{0,1},{1,0},{2,3},{3,2},{4,5},{5,4},{6,7},{7,6},{8,9},{9,8},{10,11... | collective-permute-start | bytes 1572872 | tf_op jit(solution)/shard_map/ppermute | solution.py:371
  199.2 13.2 %collective-permute-start.38 = (bf16[512,256]{1,0:T(8,128)(2,1)S(1)}, bf16[512,256]{1,0:T(8,128)(2,1)S(1)}, u32[]{:S(2)}, u32[]{:S(2)}) collective-permute-start(bf16[512,256]{1,0:T(8,128)(2,1)S(1)} %copy-done.27), channel_id=1, source_target_pairs={{0,16},{8,24},{16,0},{24,8},{1,17},{9,25},{17,1},{25,9},{2,18},{10... | collective-permute-start | bytes 786440 | tf_op jit(solution)/shard_map/ppermute | solution.py:376
  204.2 10.4 %collective-permute-start = (f32[1,128]{1,0:T(1,128)S(1)}, f32[1,128]{1,0:T(1,128)S(1)}, u32[]{:S(2)}, u32[]{:S(2)}) collective-permute-start(f32[1,128]{1,0:T(1,128)S(1)} %bitcast.51), channel_id=1, source_target_pairs={{0,1},{1,0},{2,3},{3,2},{4,5},{5,4},{6,7},{7,6},{8,9},{9,8},{10,11... | collective-permute-start | bytes 1544 | tf_op jit(solution)/shard_map/ppermute | solution.py:371
  214.5 3.7 collective-permute-start.39
  214.6 5.1 %collective-permute-start.1 = (f32[1,128]{1,0:T(1,128)S(1)}, f32[1,128]{1,0:T(1,128)S(1)}, u32[]{:S(2)}, u32[]{:S(2)}) collective-permute-start(f32[1,128]{1,0:T(1,128)S(1)} %bitcast_add_fusion.1.refs_0_), channel_id=1, source_target_pairs={{0,6},{1,7},{2,4},{3,5},{4,2},{5,3},{6,0},{7,1},{8,14},{9,15},{10,... | collective-permute-start | bytes 1544 | tf_op jit(solution)/shard_map/ppermute | solution.py:371
  216.1 5.5 %collective-permute-start.2 = (f32[1,128]{1,0:T(1,128)S(1)}, f32[1,128]{1,0:T(1,128)S(1)}, u32[]{:S(2)}, u32[]{:S(2)}) collective-permute-start(f32[1,128]{1,0:T(1,128)S(1)} %bitcast_add_fusion.1.refs_0_), channel_id=1, source_target_pairs={{0,4},{1,5},{2,6},{3,7},{4,0},{5,1},{6,2},{7,3},{8,12},{9,13},{10,... | collective-permute-start | bytes 1544 | tf_op jit(solution)/shard_map/ppermute | solution.py:371
  216.2 5.4 %collective-permute-start.3 = (f32[1,128]{1,0:T(1,128)S(1)}, f32[1,128]{1,0:T(1,128)S(1)}, u32[]{:S(2)}, u32[]{:S(2)}) collective-permute-start(f32[1,128]{1,0:T(1,128)S(1)} %bitcast_add_fusion.1.refs_0_), channel_id=1, source_target_pairs={{0,2},{1,3},{2,0},{3,1},{4,6},{5,7},{6,4},{7,5},{8,10},{9,11},{10,... | collective-permute-start | bytes 1544 | tf_op jit(solution)/shard_map/ppermute | solution.py:371
  218.1 4.5 %collective-permute-start.40 = (f32[1,128]{1,0:T(1,128)S(1)}, f32[1,128]{1,0:T(1,128)S(1)}, u32[]{:S(2)}, u32[]{:S(2)}) collective-permute-start(f32[1,128]{1,0:T(1,128)S(1)} %bitcast_add_fusion.refs_4_), channel_id=1, source_target_pairs={{0,6},{1,7},{2,4},{3,5},{4,2},{5,3},{6,0},{7,1},{8,14},{9,15},{10,... | collective-permute-start | bytes 1544 | tf_op jit(solution)/shard_map/ppermute | solution.py:371
  219.6 3.6 collective-permute-start.41
  219.7 3.6 collective-permute-start.42
  232.9 23.4 %collective-permute-start.45 = (bf16[256,2048]{1,0:T(8,128)(2,1)}, bf16[256,2048]{1,0:T(8,128)(2,1)S(1)}, u32[]{:S(2)}, u32[]{:S(2)}) collective-permute-start(bf16[256,2048]{1,0:T(8,128)(2,1)} %get-tuple-element.40), channel_id=1, source_target_pairs={{0,8},{16,24},{8,0},{24,16},{1,9},{17,25},{9,1},{25,17},{2,10},{18... | collective-permute-start | bytes 3145736 | tf_op jit(solution)/shard_map/ppermute | solution.py:436
  232.9 64.4 %collective-permute-start.51 = (bf16[256,2048]{1,0:T(8,128)(2,1)}, bf16[256,2048]{1,0:T(8,128)(2,1)S(1)}, u32[]{:S(2)}, u32[]{:S(2)}) collective-permute-start(bf16[256,2048]{1,0:T(8,128)(2,1)} %get-tuple-element.40), channel_id=1, source_target_pairs={{8,16},{16,8},{9,17},{17,9},{10,18},{18,10},{11,19},{19,11},{12,20... | collective-permute-start | bytes 3145736 | tf_op jit(solution)/shard_map/ppermute | solution.py:436
  256.3 58.5 %collective-permute-start.59 = (bf16[256,2048]{1,0:T(8,128)(2,1)S(1)}, bf16[256,2048]{1,0:T(8,128)(2,1)S(1)}, u32[]{:S(2)}, u32[]{:S(2)}) collective-permute-start(bf16[256,2048]{1,0:T(8,128)(2,1)S(1)} %collective-permute-done.45.refs_0_), channel_id=1, source_target_pairs={{8,16},{16,8},{9,17},{17,9},{10,18},{18,10},{11,19},{19,11},{12,20... | collective-permute-start | bytes 3145736 | tf_op jit(solution)/shard_map/ppermute | solution.py:436
  257.2 9.9 %collective-permute-start.43 = (bf16[64,2048]{1,0:T(8,128)(2,1)S(1)}, bf16[64,2048]{1,0:T(8,128)(2,1)S(1)}, u32[]{:S(2)}, u32[]{:S(2)}) collective-permute-start(bf16[64,2048]{1,0:T(8,128)(2,1)S(1)} %get-tuple-element.38), channel_id=1, source_target_pairs={{0,8},{16,24},{8,0},{24,16},{1,9},{17,25},{9,1},{25,17},{2,10},{18... | collective-permute-start | bytes 786440 | tf_op jit(solution)/shard_map/ppermute | solution.py:436
  261.8 11.0 %collective-permute-start.46 = (bf16[64,2048]{1,0:T(8,128)(2,1)}, bf16[64,2048]{1,0:T(8,128)(2,1)}, u32[]{:S(2)}, u32[]{:S(2)}) collective-permute-start(bf16[64,2048]{1,0:T(8,128)(2,1)} %get-tuple-element.41), channel_id=1, source_target_pairs={{0,8},{16,24},{8,0},{24,16},{1,9},{17,25},{9,1},{25,17},{2,10},{18... | collective-permute-start | bytes 786440 | tf_op jit(solution)/shard_map/ppermute | solution.py:436
  261.9 34.0 %collective-permute-start.44 = (bf16[128,2048]{1,0:T(8,128)(2,1)}, bf16[128,2048]{1,0:T(8,128)(2,1)}, u32[]{:S(2)}, u32[]{:S(2)}) collective-permute-start(bf16[128,2048]{1,0:T(8,128)(2,1)} %get-tuple-element.39), channel_id=1, source_target_pairs={{0,8},{16,24},{8,0},{24,16},{1,9},{17,25},{9,1},{25,17},{2,10},{18... | collective-permute-start | bytes 1572872 | tf_op jit(solution)/shard_map/ppermute | solution.py:436
  267.1 7.1 %collective-permute-start.47 = (bf16[64,2048]{1,0:T(8,128)(2,1)S(1)}, bf16[64,2048]{1,0:T(8,128)(2,1)}, u32[]{:S(2)}, u32[]{:S(2)}) collective-permute-start(bf16[64,2048]{1,0:T(8,128)(2,1)S(1)} %get-tuple-element.38), channel_id=1, source_target_pairs={{8,16},{16,8},{9,17},{17,9},{10,18},{18,10},{11,19},{19,11},{12,20... | collective-permute-start | bytes 786440 | tf_op jit(solution)/shard_map/ppermute | solution.py:436
  272.8 3.9 %collective-permute-start.53 = (bf16[64,2048]{1,0:T(8,128)(2,1)}, bf16[64,2048]{1,0:T(8,128)(2,1)}, u32[]{:S(2)}, u32[]{:S(2)}) collective-permute-start(bf16[64,2048]{1,0:T(8,128)(2,1)} %get-tuple-element.41), channel_id=1, source_target_pairs={{8,16},{16,8},{9,17},{17,9},{10,18},{18,10},{11,19},{19,11},{12,20... | collective-permute-start | bytes 786440 | tf_op jit(solution)/shard_map/ppermute | solution.py:436
  274.2 42.9 %collective-permute-start.49 = (bf16[128,2048]{1,0:T(8,128)(2,1)}, bf16[128,2048]{1,0:T(8,128)(2,1)}, u32[]{:S(2)}, u32[]{:S(2)}) collective-permute-start(bf16[128,2048]{1,0:T(8,128)(2,1)} %get-tuple-element.39), channel_id=1, source_target_pairs={{8,16},{16,8},{9,17},{17,9},{10,18},{18,10},{11,19},{19,11},{12,20... | collective-permute-start | bytes 1572872 | tf_op jit(solution)/shard_map/ppermute | solution.py:436
  276.8 36.7 %collective-permute-start.48 = (bf16[64,2048]{1,0:T(8,128)(2,1)}, bf16[64,2048]{1,0:T(8,128)(2,1)}, u32[]{:S(2)}, u32[]{:S(2)}) collective-permute-start(bf16[64,2048]{1,0:T(8,128)(2,1)} %collective-permute-done.47.refs_0_), channel_id=1, source_target_pairs={{0,8},{16,24},{8,0},{24,16},{1,9},{17,25},{9,1},{25,17},{2,10},{18... | collective-permute-start | bytes 786440 | tf_op jit(solution)/shard_map/ppermute | solution.py:436
  295.9 22.7 %collective-permute-start.57 = (bf16[128,2048]{1,0:T(8,128)(2,1)}, bf16[128,2048]{1,0:T(8,128)(2,1)}, u32[]{:S(2)}, u32[]{:S(2)}) collective-permute-start(bf16[128,2048]{1,0:T(8,128)(2,1)} %collective-permute-done.44.refs_0_), channel_id=1, source_target_pairs={{8,16},{16,8},{9,17},{17,9},{10,18},{18,10},{11,19},{19,11},{12,20... | collective-permute-start | bytes 1572872 | tf_op jit(solution)/shard_map/ppermute | solution.py:436
  297.4 62.1 %collective-permute-start.52 = (bf16[256,2048]{1,0:T(8,128)(2,1)S(1)}, bf16[256,2048]{1,0:T(8,128)(2,1)}, u32[]{:S(2)}, u32[]{:S(2)}) collective-permute-start(bf16[256,2048]{1,0:T(8,128)(2,1)S(1)} %collective-permute-done.51.refs_0_), channel_id=1, source_target_pairs={{0,8},{16,24},{8,0},{24,16},{1,9},{17,25},{9,1},{25,17},{2,10},{18... | collective-permute-start | bytes 3145736 | tf_op jit(solution)/shard_map/ppermute | solution.py:436
  307.5 20.1 %all-to-all-start.1 = ((bf16[16,128,128]{2,1,0:T(8,128)(2,1)}), bf16[16,128,128]{2,1,0:T(8,128)(2,1)}, u32[]{:S(2)}, u32[]{:S(2)}) async-start(bf16[16,128,128]{2,1,0:T(8,128)(2,1)} %bitcast.48), calls=%async_computation.1 | async-start | bytes 1048576 | tf_op jit(solution)/shard_map/all_to_all | solution.py:457
  313.5 3.7 collective-permute-start.55
  314.8 68.8 %collective-permute-start.60 = (bf16[256,2048]{1,0:T(8,128)(2,1)S(1)}, bf16[256,2048]{1,0:T(8,128)(2,1)}, u32[]{:S(2)}, u32[]{:S(2)}) collective-permute-start(bf16[256,2048]{1,0:T(8,128)(2,1)S(1)} %collective-permute-done.59.refs_0_), channel_id=1, source_target_pairs={{0,8},{16,24},{8,0},{24,16},{1,9},{17,25},{9,1},{25,17},{2,10},{18... | collective-permute-start | bytes 3145736 | tf_op jit(solution)/shard_map/ppermute | solution.py:436
  317.1 40.7 %collective-permute-start.50 = (bf16[128,2048]{1,0:T(8,128)(2,1)}, bf16[128,2048]{1,0:T(8,128)(2,1)}, u32[]{:S(2)}, u32[]{:S(2)}) collective-permute-start(bf16[128,2048]{1,0:T(8,128)(2,1)} %collective-permute-done.49.refs_0_), channel_id=1, source_target_pairs={{0,8},{16,24},{8,0},{24,16},{1,9},{17,25},{9,1},{25,17},{2,10},{18... | collective-permute-start | bytes 1572872 | tf_op jit(solution)/shard_map/ppermute | solution.py:436
  317.2 11.9 %collective-permute-start.61 = (bf16[64,2048]{1,0:T(8,128)(2,1)}, bf16[64,2048]{1,0:T(8,128)(2,1)}, u32[]{:S(2)}, u32[]{:S(2)}) collective-permute-start(bf16[64,2048]{1,0:T(8,128)(2,1)} %collective-permute-done.46.refs_0_), channel_id=1, source_target_pairs={{8,16},{16,8},{9,17},{17,9},{10,18},{18,10},{11,19},{19,11},{12,20... | collective-permute-start | bytes 786440 | tf_op jit(solution)/shard_map/ppermute | solution.py:436
  318.6 62.7 %collective-permute-start.58 = (bf16[128,2048]{1,0:T(8,128)(2,1)}, bf16[128,2048]{1,0:T(8,128)(2,1)}, u32[]{:S(2)}, u32[]{:S(2)}) collective-permute-start(bf16[128,2048]{1,0:T(8,128)(2,1)} %collective-permute-done.57.refs_0_), channel_id=1, source_target_pairs={{0,8},{16,24},{8,0},{24,16},{1,9},{17,25},{9,1},{25,17},{2,10},{18... | collective-permute-start | bytes 1572872 | tf_op jit(solution)/shard_map/ppermute | solution.py:436
  329.1 48.0 %collective-permute-start.54 = (bf16[64,2048]{1,0:T(8,128)(2,1)}, bf16[64,2048]{1,0:T(8,128)(2,1)S(1)}, u32[]{:S(2)}, u32[]{:S(2)}) collective-permute-start(bf16[64,2048]{1,0:T(8,128)(2,1)} %collective-permute-done.53.refs_0_), channel_id=1, source_target_pairs={{0,8},{16,24},{8,0},{24,16},{1,9},{17,25},{9,1},{25,17},{2,10},{18... | collective-permute-start | bytes 786440 | tf_op jit(solution)/shard_map/ppermute | solution.py:436
  357.7 22.2 %collective-permute-start.56 = (bf16[64,2048]{1,0:T(8,128)(2,1)}, bf16[64,2048]{1,0:T(8,128)(2,1)S(1)}, u32[]{:S(2)}, u32[]{:S(2)}) collective-permute-start(bf16[64,2048]{1,0:T(8,128)(2,1)} %collective-permute-done.55.refs_0_), channel_id=1, source_target_pairs={{0,8},{16,24},{8,0},{24,16},{1,9},{17,25},{9,1},{25,17},{2,10},{18... | collective-permute-start | bytes 786440 | tf_op jit(solution)/shard_map/ppermute | solution.py:436
  359.5 27.0 %collective-permute-start.62 = (bf16[64,2048]{1,0:T(8,128)(2,1)}, bf16[64,2048]{1,0:T(8,128)(2,1)S(1)}, u32[]{:S(2)}, u32[]{:S(2)}) collective-permute-start(bf16[64,2048]{1,0:T(8,128)(2,1)} %collective-permute-done.61.refs_0_), channel_id=1, source_target_pairs={{0,8},{16,24},{8,0},{24,16},{1,9},{17,25},{9,1},{25,17},{2,10},{18... | collective-permute-start | bytes 786440 | tf_op jit(solution)/shard_map/ppermute | solution.py:436
  (30 other events, 824.9 us)
